TPU v7x, 256 devices: a whole 4x4x8 slice. The times are simulated.
256 devices in a mesh: pb: 64 (over x, z, core), ka: 4 (over y).
Axes of the slice: x: 4, y: 4, z: 8, core: 2. Of those that a mesh axis runs over, the one named last changes fastest.
Arguments:
- valence: float32 [1664, 64, 1024], P('pb', 'ka'), may hold values from -6 to 6
- conduction: bfloat16 [1664, 196, 1024], P('pb', None, 'ka'), may hold values from -0.0024414062 to 0.0024414062
- screened: float32 [64, 1024, 1024], P('pb'), may hold values from -1 to 3, as said below
- momentum: int32 [1664, 1], P('pb'), may hold values from 0 to 63; in each aligned block of 26 rows (0 to 25, 26 to 51, ...) at most 2 rows name the same one
- kpairs: int32 [1664, 2], P('pb'), may hold values from 0 to 63
- kpoint_slot: int32 [64], replicated, may hold values from 0 to 63, each once
- trial_blocks: float32 [64, 14336], P('pb', 'ka'), may hold values from -6 to 6
Outputs:
- response: float32 [64, 14336], P('pb', 'ka')
Inputs may be any that keep to these rules, and one draw needn't show every extreme that they name: Among the k-pairs of one index of pb (rows i * 26 to (i + 1) * 26 - 1), at most 2 share a momentum transfer. `kpoint_slot`: each row number appears once. `screened`: each matrix is symmetric.
All inputs are finite; a program needn't handle non-finite values.
Results may differ from a plain program's by a relative error of at most 0.0003.
Values sent between devices are 32-bit elements; how exact they have to be, the bound alone decides.
No kernel may reach another device: no remote copies, remote signals or barrier semaphores. Data moves between devices by JAX's collectives and lax.ppermute only.
A program may use at most 128 MiB of HBM per device.

v0:
```python
import jax
import jax.numpy as jnp
from jax import lax
from jax.sharding import PartitionSpec as P

VB = 8
CB = 14


def local(valence, conduction, screened, momentum, kpairs, kpoint_slot, trial_blocks):
    highest = lax.Precision.HIGHEST
    pair_dev = valence.shape[0]
    owners = lax.axis_size("pb")
    capacity = max(2, 2 * pair_dev // owners)
    slot_count = owners * capacity
    target = momentum[:, 0]
    indices = jnp.arange(pair_dev, dtype=jnp.int32)
    earlier = (target[:, None] == target[None, :]) & (indices[None, :] < indices[:, None])
    position = target * capacity + jnp.sum(earlier.astype(jnp.int32), axis=1)
    matches = position[None, :] == jnp.arange(slot_count, dtype=jnp.int32)[:, None]
    source = jnp.sum(jnp.where(matches, indices[None, :], 0), axis=1)
    filled = jnp.any(matches, axis=1)
    outgoing = jnp.where(filled[:, None, None], jnp.take(valence, source, axis=0), 0.0)
    outgoing = outgoing.reshape(owners, capacity, valence.shape[1], valence.shape[2])
    matrix = screened[0]
    product = jnp.einsum(
        "scrg,gh->scrh",
        lax.all_to_all(outgoing, "pb", split_axis=0, concat_axis=0, tiled=True),
        matrix,
        precision=highest,
        preferred_element_type=jnp.float32,
    )
    returned = lax.all_to_all(
        lax.all_to_all(product, "pb", split_axis=0, concat_axis=0, tiled=True),
        "ka",
        split_axis=3,
        concat_axis=2,
        tiled=True,
    )
    by_slot = returned.reshape(slot_count, returned.shape[2], returned.shape[3])
    columns = jnp.take(by_slot, position, axis=0)
    conduct_wide = conduction.astype(jnp.float32)
    partial_kernel = jnp.einsum(
        "prg,pbg->prb", columns, conduct_wide, precision=highest, preferred_element_type=jnp.float32
    )
    kernel = lax.psum(partial_kernel, "ka")
    gathered = lax.all_gather(trial_blocks, "pb", axis=0, tiled=True)
    kpoint_count = gathered.shape[0]
    local_trials = gathered.shape[1] // (VB * CB)
    blocks = gathered.reshape(kpoint_count, local_trials, VB, CB)
    slot_near = jnp.take(kpoint_slot, kpairs[:, 0])
    slot_far = jnp.take(kpoint_slot, kpairs[:, 1])
    near_trials = jnp.take(blocks, slot_near, axis=0)
    far_trials = jnp.take(blocks, slot_far, axis=0)
    kernel_blocks = kernel.reshape(pair_dev, VB, VB, CB, CB)
    direct = jnp.einsum("pvwcd,pnwd->pnvc", kernel_blocks, far_trials, precision=highest)
    mirror = jnp.einsum("pvwcd,pnvc->pnwd", kernel_blocks, near_trials, precision=highest)
    kpoint_rows = jnp.arange(kpoint_count, dtype=jnp.int32)[:, None]
    onehot_near = (slot_near[None, :] == kpoint_rows).astype(jnp.float32)
    onehot_far = (slot_far[None, :] == kpoint_rows).astype(jnp.float32)
    summed = jnp.dot(
        onehot_near,
        direct.reshape(pair_dev, -1),
        precision=highest,
        preferred_element_type=jnp.float32,
    )
    summed = summed + jnp.dot(
        onehot_far,
        mirror.reshape(pair_dev, -1),
        precision=highest,
        preferred_element_type=jnp.float32,
    )
    return lax.psum_scatter(summed, "pb", scatter_dimension=0, tiled=True)


def solution(mesh):
    return jax.shard_map(
        local,
        mesh=mesh,
        in_specs=(
            P("pb", "ka", None),
            P("pb", None, "ka"),
            P("pb", None, None),
            P("pb", None),
            P("pb", None),
            P(),
            P("pb", "ka"),
        ),
        out_specs=P("pb", "ka"),
        check_vma=False,
    )
```

profile of v0, /device:TPU:1, one launch (start us, length us, event | category | flops | bytes accessed | tf_op | source)
XLA Modules:
  0.0 1161.9 jit_solution(17893508544063465319)
XLA Ops:
  6.5 0.0 copy-start
  6.5 1.0 convert_reduce_fusion
  7.5 0.7 multiply_add_fusion
  8.2 0.1 select_reduce_fusion
  8.3 0.1 fusion.16
  8.4 0.1 reduce_sum.27
  8.5 0.1 broadcast_in_dim.68
  8.7 5.8 gather_fusion
  14.5 4.0 select_select_fusion
  18.4 0.0 copy-start.5
  18.5 199.1 %all_to_all.25 = f32[64,2,16,1024]{3,2,1,0:T(8,128)S(1)} all-to-all(f32[64,2,16,1024]{3,2,1,0:T(8,128)S(1)} %select_select_fusion), channel_id=1, replica_groups=mesh['pb'=64,'ka'=4] {'pb'}, dimensions={0} | all-to-all | bytes 16777216 | tf_op jit(solution)/shard_map/all_to_all | solution.py:28
  217.5 0.0 copy-done.5
  217.5 27.7 %fusion = f32[64,2,16,1024]{3,2,1,0:T(8,128)S(1)} fusion(f32[64,2,16,1024]{3,2,1,0:T(8,128)S(1)} %all_to_all.25, f32[1,1024,1024]{2,1,0:T(8,128)S(1)} %copy-done.5), kind=kOutput, calls=%fused_computation.8 | convolution fusion | flops 25769803776 | bytes 20971520 | tf_op jit(solution)/shard_map/scrg,gh->scrh/dot_general | solution.py:26
  245.2 192.0 %all_to_all.26 = f32[64,2,16,1024]{3,2,1,0:T(8,128)} all-to-all(f32[64,2,16,1024]{3,2,1,0:T(8,128)S(1)} %fusion), channel_id=1, replica_groups=mesh['pb'=64,'ka'=4] {'pb'}, dimensions={0} | all-to-all | bytes 16777216 | tf_op jit(solution)/shard_map/all_to_all | solution.py:34
  437.2 16.3 %copy.61 = f32[64,2,16,1024]{0,2,1,3:T(8,128)} copy(f32[64,2,16,1024]{3,2,1,0:T(8,128)} %all_to_all.26) | data formatting | bytes 16777216 | tf_op jit(solution)/shard_map/all_to_all | solution.py:34
  453.5 14.3 %reshape.142 = f32[4,1,524288]{2,1,0:T(1,128)} reshape(f32[1024,2,16,64]{3,2,1,0:T(8,128)} %bitcast.68) | data formatting | bytes 16777216
  467.9 0.0 copy-start.4
  467.9 5.8 all-to-all-start.2
  473.6 0.0 all-reduce.4.cloned.1.call-start
  473.7 0.0 copy-done.4
  473.7 93.4 %all-to-all-done.2 = f32[4,1,524288]{2,1,0:T(1,128)} async-done(((f32[4,1,524288]{2,1,0:T(1,128)}), f32[4,1,524288]{2,1,0:T(1,128)}, u32[]{:S(2)}, u32[]{:S(2)}) %all-to-all-start.2) | async-done | bytes 8388640 | tf_op jit(solution)/shard_map/all_to_all | solution.py:33
  567.1 0.5 broadcast.181
  567.6 30.1 %reduce = f32[4,524288]{1,0:T(4,128)} reduce(f32[4,1,524288]{2,1,0:T(1,128)} %all-to-all-done.2, f32[]{:T(128)} %broadcast.181), dimensions={1}, to_apply=%all_to_all.19.reduce_sub_computation | reduce | bytes 16777220 | tf_op jit(solution)/shard_map/all_to_all | solution.py:33
  597.7 16.8 %reshape.143 = f32[1024,2,16,64]{3,2,1,0:T(8,128)} reshape(f32[4,524288]{1,0:T(4,128)} %reduce) | data formatting | bytes 16777216
  614.5 14.4 %copy.75 = f32[64,2,16,4,256]{4,3,2,1,0:T(4,128)} copy(f32[64,2,16,4,256]{0,2,1,4,3:T(8,128)} %bitcast.69) | data formatting | bytes 16777216 | tf_op jit(solution)/shard_map/all_to_all | solution.py:33
  628.9 8.6 copy.63
  637.5 5.3 gather_fusion.1
  642.8 0.0 copy-done
  642.8 5.3 fusion.2
  648.1 5.8 copy.64
  653.9 14.5 %copy.65 = f32[26,8,8,14,14]{3,2,4,1,0:T(8,128)} copy(f32[26,8,8,14,14]{0,2,1,4,3:T(8,128)} %bitcast.72) | data formatting | bytes 2609152 | tf_op jit(solution)/shard_map/reshape | solution.py:55
  668.4 0.0 copy-start.3
  668.4 0.0 copy-start.1
  668.4 0.0 copy-start.2
  668.4 0.0 all-reduce.4.cloned.1.call-update
  668.4 0.0 all-reduce.6.cloned.1.call-start
  668.5 0.6 copy-done.3
  669.1 0.0 copy-done.1
  669.1 0.7 gather_fusion.3
  669.8 0.7 gather_fusion.2
  670.5 0.0 copy-done.2
  670.5 53.8 %all-gather = f32[64,1,3584]{2,1,0:T(1,128)} all-gather(f32[1,1,3584]{2,1,0:T(1,128)S(1)} %bitcast.74), channel_id=1, replica_groups=mesh['pb'=64,'ka'=4] {'pb'}, dimensions={0}, use_global_device_ids=true | all-gather | bytes 931840 | tf_op jit(solution)/shard_map/all_gather | solution.py:47
  724.3 4.1 copy.59
  728.4 2.6 reshape.68
  731.1 5.5 copy.60
  736.5 3.9 gather_fusion.5
  740.4 3.8 gather_fusion.4
  744.2 141.9 %all-reduce.4.cloned.1.call-done = f32[26,8,8,14,14]{3,2,4,1,0:T(8,128)} async-done(((f32[26,8,8,14,14]{3,2,4,1,0:T(8,128)}), f32[26,8,8,14,14]{3,2,4,1,0:T(8,128)}) %all-reduce.4.cloned.1.call-update) | async-done | bytes 1304592 | tf_op jit(solution)/shard_map/psum | solution.py:46
  886.2 16.3 %copy.68 = f32[26,8,8,14,14]{4,1,3,2,0:T(8,128)} copy(f32[26,8,8,14,14]{3,2,4,1,0:T(8,128)} %all-reduce.4.cloned.1.call-done) | data formatting | bytes 2609152 | tf_op jit(solution)/shard_map/psum | solution.py:46
  902.5 22.8 %convolution_bitcast_fusion = f32[26,32,8,14]{1,3,2,0:T(8,128)} fusion(f32[26,8,8,14,14]{4,1,3,2,0:T(8,128)} %copy.68, f32[26,32,8,14]{1,2,3,0:T(8,128)} %gather_fusion.5, pred[26]{0:T(512)(128)(4,1)S(1)} %get-tuple-element.6), kind=kOutput, calls=%fused_computation.12 | convolution fusion | flops 125332480 | bytes 2050074 | tf_op jit(solution)/shard_map/pvwcd,pnvc->pnwd/dot_general | solution.py:57
  925.3 3.7 copy.69
  929.0 4.0 reshape.72
  933.0 23.0 %convolution_bitcast_fusion.1 = f32[26,32,8,14]{1,3,2,0:T(8,128)} fusion(f32[26,8,8,14,14]{3,2,4,1,0:T(8,128)} %all-reduce.4.cloned.1.call-done, f32[26,32,8,14]{1,2,3,0:T(8,128)} %gather_fusion.4, pred[26]{0:T(512)(128)(4,1)S(1)} %get-tuple-element.13), kind=kOutput, calls=%fused_computation.13 | convolution fusion | flops 125332480 | bytes 2050074 | tf_op jit(solution)/shard_map/pvwcd,pnwd->pnvc/dot_general | solution.py:56
  956.0 3.7 copy.66
  959.7 0.0 copy-start.6
  959.7 4.6 reshape.71
  964.3 1.5 fusion.14
  965.8 1.5 convolution_add_fusion
  967.3 0.0 all-reduce.6.cloned.1.call-update
  967.3 0.0 copy-done.6
  967.4 0.7 dynamic-slice
  968.0 184.6 %all-reduce.6.cloned.1.call-done = f32[64,3584]{1,0:T(8,128)} async-done(((f32[64,3584]{1,0:T(8,128)}), f32[64,3584]{1,0:T(8,128)}) %all-reduce.6.cloned.1.call-update) | async-done | bytes 917520
  1152.6 2.2 constant_dynamic-slice_fusion
  (12 shorter events, 0.1 us)
Async XLA Ops:
  6.5 636.2 %copy-start = (bf16[26,196,256]{2,1,0:T(8,128)(2,1)S(1)}, bf16[26,196,256]{2,1,0:T(8,128)(2,1)}, u32[]{:S(2)}) copy-start(bf16[26,196,256]{2,1,0:T(8,128)(2,1)} %param.12) | copy-start | bytes 7827460
  18.4 199.1 %copy-start.5 = (f32[1,1024,1024]{2,1,0:T(8,128)S(1)}, f32[1,1024,1024]{2,1,0:T(8,128)}, u32[]{:S(2)}) copy-start(f32[1,1024,1024]{2,1,0:T(8,128)} %param.13) | copy-start | bytes 12582916
  467.9 5.8 copy-start.4
  467.9 99.2 %all-to-all-start.2 = ((f32[4,1,524288]{2,1,0:T(1,128)}), f32[4,1,524288]{2,1,0:T(1,128)}, u32[]{:S(2)}, u32[]{:S(2)}) async-start(f32[4,1,524288]{2,1,0:T(1,128)} %reshape.142), calls=%async_computation.2 | async-start | bytes 16777216 | tf_op jit(solution)/shard_map/all_to_all | solution.py:33
  473.6 412.5 %all-reduce.4.cloned.1.call-start = ((), (), s32[]{:S(2)}) async-start(), calls=%async_computation.3 | async-start | bytes 23855104 | tf_op jit(solution)/shard_map/psum | solution.py:46
  668.4 0.7 copy-start.3
  668.4 0.7 copy-start.1
  668.4 2.1 copy-start.2
  668.4 484.2 %all-reduce.6.cloned.1.call-start = ((), (), s32[]{:S(2)}) async-start(), calls=%async_computation.4 | async-start | bytes 1835008
  959.7 7.6 copy-start.6
Sparse Core Ops, SparseCore 0:
  668.6 217.5 all-reduce.3
  967.5 185.1 all-reduce.5
where the time goes:
time: 1170 us; the launch traced here: 1160 us
  blocking collectives  445 us (38%)
  waiting for transfers between devices  420 us (36%)
  local copies, waits for them, and re-layouts  160 us (14%)
  matrix products  81.8 us (7%)
  other arithmetic  36 us (3%)
  between operations  13.8 us (1%)
    all_to_all x1, blocking collectives, local(): lax.all_to_all(outgoing, 'pb', split_axis=0, concat_axis=0, tiled=True)  199 us
    all_to_all x1, blocking collectives, local(): lax.all_to_all(product, 'pb', split_axis=0, concat_axis=0, tiled=True)  192 us
    unnamed x3, waiting for transfers between devices  185 us
    psum x1, waiting for transfers between devices, local(): kernel = lax.psum(partial_kernel, 'ka')  142 us
    all_to_all x1, waiting for transfers between devices, local(): lax.all_to_all(lax.all_to_all(product, 'pb', split_axis=0, concat_axis=0,...  93.4 us
    all_gather x1, blocking collectives, local(): gathered = lax.all_gather(trial_blocks, 'pb', axis=0, tiled=True)  53.8 us
    unnamed x18, local copies, waits for them, and re-layouts  34.6 us
    all_to_all x1, other arithmetic, local(): lax.all_to_all(lax.all_to_all(product, 'pb', split_axis=0, concat_axis=0,...  30.1 us
  transfers between devices with their start and end apart: 3, of which 3 were waited for; matrix products, arithmetic and copies ran while one was open for 2% of the time, Pallas kernels for 0%

commit v1 on v0

v1 whole, which is shorter than its diff:
```python
import functools
import jax
import jax.numpy as jnp
from jax import lax
from jax.experimental import pallas as pl
from jax.experimental.pallas import tpu as pltpu
from jax.sharding import PartitionSpec as P

VB = 8
CB = 14
CD = 16
VC = VB * CD
F32 = jnp.float32
BF16 = jnp.bfloat16


def split(x):
    high = x.astype(BF16)
    return high, (x - high.astype(F32)).astype(BF16)


def mul(a, b, dims):
    return lax.dot_general(a, b, (dims, ((), ())), preferred_element_type=F32)


def mul3(a, b, dims=((1,), (0,))):
    rows = a.shape[0]
    a_high, a_low = split(a)
    b_high, b_low = split(b)
    both = mul(jnp.concatenate([a_high, a_low], axis=0), b_high, dims)
    return both[:rows] + both[rows:] + mul(a_high, b_low, dims)


def kernel_body(momentum_ref, valence_ref, matrix_ref, conduct_ref, out_ref, low_ref, high_ref, turn_ref):
    rows = valence_ref.shape[0] * valence_ref.shape[2]
    valence = valence_ref[...].reshape(rows, valence_ref.shape[3])
    screened_rows = mul3(valence, matrix_ref[0])
    rows_high, rows_low = split(screened_rows)
    both = mul(jnp.concatenate([rows_high, rows_low], axis=0), conduct_ref[0], ((1,), (1,)))
    kernel = both[:rows] + both[rows:]
    low_ref[...] = kernel[:, :VC]
    high_ref[...] = jnp.concatenate([kernel[:, VC:], jnp.zeros((rows, 2 * VC - kernel.shape[1]), F32)], axis=1)
    group = lax.broadcasted_iota(jnp.int32, (VB, VC), 1) // CD
    for half, ref in enumerate((low_ref, high_ref)):
        tiles = [ref[pl.ds(w, VB, stride=VB), :] for w in range(VB)]
        for step in (4, 2, 1):
            upper = (group & step) != 0
            for i in range(VB):
                if i & step:
                    continue
                a, b = tiles[i], tiles[i + step]
                tiles[i] = jnp.where(upper, pltpu.roll(b, step * CD, axis=1), a)
                tiles[i + step] = jnp.where(upper, b, pltpu.roll(a, VC - step * CD, axis=1))
        for i in range(VB):
            turn_ref[pl.ds((half * VB + i) * VB, VB), :] = tiles[i]
    for v in range(VB):
        out_ref[0, pl.ds(v * CD, CD), :] = turn_ref[pl.ds(v, CD, stride=VB), :]


def pair_kernels(momentum, valence, matrices, conduction):
    parts, pairs, rows, waves = valence.shape
    own = matrices.shape[2]
    columns = conduction.shape[1]
    return pl.pallas_call(
        kernel_body,
        out_shape=jax.ShapeDtypeStruct((pairs, VC, VC), F32),
        grid_spec=pltpu.PrefetchScalarGridSpec(
            num_scalar_prefetch=1,
            grid=(pairs,),
            in_specs=[
                pl.BlockSpec((parts, 1, rows, waves), lambda p, q: (0, p, 0, 0)),
                pl.BlockSpec((1, waves, own), lambda p, q: (q[p], 0, 0)),
                pl.BlockSpec((1, columns, own), lambda p, q: (p, 0, 0)),
            ],
            out_specs=pl.BlockSpec((1, VC, VC), lambda p, q: (p, 0, 0)),
            scratch_shapes=[
                pltpu.VMEM((VB * VB, VC), F32),
                pltpu.VMEM((VB * VB, VC), F32),
                pltpu.VMEM((VC, VC), F32),
            ],
        ),
        cost_estimate=pl.CostEstimate(flops=6 * pairs * 64 * waves * own, bytes_accessed=pairs * waves * own * 4, transcendentals=0),
    )(momentum, valence, matrices, conduction)


def response_body(near_ref, far_ref, kernel_ref, trial_ref, out_ref):
    out_ref[...] = jnp.zeros_like(out_ref)

    @pl.loop(0, kernel_ref.shape[0])
    def _(p):
        near, far = near_ref[p], far_ref[p]
        kernel = kernel_ref[p]
        direct = mul3(trial_ref[far], kernel, ((1,), (1,)))
        mirror = mul3(trial_ref[near], kernel, ((1,), (0,)))
        out_ref[near] = out_ref[near] + direct
        out_ref[far] = out_ref[far] + mirror


def contributions(near, far, kernel, trials):
    whole = pl.BlockSpec(memory_space=pltpu.VMEM)
    scalar = pl.BlockSpec(memory_space=pltpu.SMEM)
    return pl.pallas_call(
        response_body,
        out_shape=jax.ShapeDtypeStruct(trials.shape, F32),
        in_specs=[scalar, scalar, whole, whole],
        out_specs=whole,
        cost_estimate=pl.CostEstimate(flops=12 * kernel.size * trials.shape[1], bytes_accessed=4 * (kernel.size + 2 * trials.size), transcendentals=0),
    )(near, far, kernel, trials)


def sum_over_ka(x, ka):
    swap = [(i, i ^ 1) for i in range(ka)]
    fold = [(i, ka - 1 - i) for i in range(ka)]
    half = x.shape[0] // 2
    a, b = x[:half], x[half:]
    a_in, b_in = lax.ppermute(a, "ka", swap), lax.ppermute(b, "ka", fold)
    a, b = a + a_in, b + b_in
    a_in, b_in = lax.ppermute(a, "ka", fold), lax.ppermute(b, "ka", swap)
    return jnp.concatenate([a + a_in, b + b_in], axis=0)


def local(valence, conduction, screened, momentum, kpairs, kpoint_slot, trial_blocks):
    owners, ka = lax.axis_size("pb"), lax.axis_size("ka")
    pair_dev = valence.shape[0]
    own = conduction.shape[2]
    column = lax.axis_index("ka") * own
    piece = lax.dynamic_slice(screened[0], (0, column), (screened.shape[1], own))
    matrices = lax.all_gather(piece, "pb")
    spread = jnp.broadcast_to(valence[None], (ka,) + valence.shape)
    rows = lax.all_to_all(spread, "ka", split_axis=0, concat_axis=0, tiled=True)
    own_trials = trial_blocks.reshape(-1, VB, CB)
    local_trials = own_trials.shape[0]
    own_trials = jnp.pad(own_trials, ((0, 0), (0, 0), (0, CD - CB))).reshape(1, local_trials, VC)
    spread = jnp.broadcast_to(own_trials, (owners, local_trials, VC))
    trials = lax.all_to_all(spread, "pb", split_axis=0, concat_axis=0, tiled=True)
    conduct = conduction.reshape(pair_dev, CB, CB, own)
    conduct = jnp.pad(conduct, ((0, 0), (0, 0), (0, CD - CB), (0, 0))).reshape(pair_dev, CB * CD, own)
    near = jnp.take(kpoint_slot, kpairs[:, 0])
    far = jnp.take(kpoint_slot, kpairs[:, 1])
    rows, conduct, trials, near, far = lax.optimization_barrier((rows, conduct, trials, near, far))
    kernel = sum_over_ka(pair_kernels(momentum[:, 0], rows, matrices, conduct), ka)
    summed = contributions(near, far, kernel, trials)
    parts = lax.all_to_all(summed, "pb", split_axis=0, concat_axis=0, tiled=True)
    response = jnp.sum(parts, axis=0).reshape(local_trials, VB, CD)[:, :, :CB]
    return response.reshape(1, -1)


def solution(mesh):
    return jax.shard_map(
        local,
        mesh=mesh,
        in_specs=(
            P("pb", "ka", None),
            P("pb", None, "ka"),
            P("pb", None, None),
            P("pb", None),
            P("pb", None),
            P(),
            P("pb", "ka"),
        ),
        out_specs=P("pb", "ka"),
        check_vma=False,
    )
```

time: 1170 us -> 397 us (0.34)
  blocking collectives: 445 us -> 86.1 us
  waiting for transfers between devices: 420 us -> 229 us
  local copies, waits for them, and re-layouts: 160 us -> 16.4 us
  matrix products: 81.8 us -> 0 us
  Pallas kernels: 0 us -> 37.8 us
  other arithmetic: 36 us -> 2.47 us
    all_to_all x2, blocking collectives: 391 us -> 86.1 us  [the longest x1 49.7 us: local(): lax.all_to_all(spread, 'pb', split_axis=0, concat_axis=0, tiled=True)]
    unnamed x3 -> x1, waiting for transfers between devices: 185 us -> 0.02 us
    psum x1 -> x0, waiting for transfers between devices: 142 us -> none  [local(): kernel = lax.psum(partial_kernel, 'ka')]
    all_gather x0 -> x1, waiting for transfers between devices: none -> 121 us  [local(): matrices = lax.all_gather(piece, 'pb')]
    dot_general x6 -> x0, matrix products: 81.8 us -> none  [the longest x1 27.7 us: local(): jnp.einsum('scrg,gh->scrh', lax.all_to_all(outgoing, 'pb', split_axis=0,...]
    all_gather x1 -> x0, blocking collectives: 53.8 us -> none  [local(): gathered = lax.all_gather(trial_blocks, 'pb', axis=0, tiled=True)]
    all_to_all x4 -> x0, local copies, waits for them, and re-layouts: 39.8 us -> none  [the longest x3 23.5 us: local(): lax.all_to_all(lax.all_to_all(product, 'pb', split_axis=0, concat_axis=0,...]
    ppermute x0 -> x4, waiting for transfers between devices: none -> 38.4 us  [the longest x2 19.5 us: sum_over_ka(): a_in, b_in = (lax.ppermute(a, 'ka', swap), lax.ppermute(b, 'ka', fold))]
  transfers between devices with their start and end apart: 3 -> 6, of which waited for: 3 -> 6; matrix products, arithmetic and copies ran while one was open for 2% -> 3% of each run, Pallas kernels for 0% -> 0%
where the time goes in v1:
time: 397 us; the launch traced here: 396 us
  waiting for transfers between devices  229 us (58%)
  blocking collectives  86.1 us (22%)
  Pallas kernels  37.8 us (10%)
  local copies, waits for them, and re-layouts  16.4 us (4%)
  between operations  13.5 us (3%)
  starting transfers between devices  10.5 us (3%)
    all_gather x1, waiting for transfers between devices, local(): matrices = lax.all_gather(piece, 'pb')  121 us
    all_to_all x1, waiting for transfers between devices, local(): rows = lax.all_to_all(spread, 'ka', split_axis=0, concat_axis=0, tiled=True)  69.1 us
    all_to_all x1, blocking collectives, local(): lax.all_to_all(spread, 'pb', split_axis=0, concat_axis=0, tiled=True)  49.7 us
    all_to_all x1, blocking collectives, local(): lax.all_to_all(summed, 'pb', split_axis=0, concat_axis=0, tiled=True)  36.4 us
    pallas_call x1, Pallas kernels, pair_kernels(): pl.pallas_call(kernel_body, out_shape=jax.ShapeDtypeStruct((pairs, VC, VC...  30.1 us
    ppermute x2, waiting for transfers between devices, sum_over_ka(): a_in, b_in = (lax.ppermute(a, 'ka', swap), lax.ppermute(b, 'ka', fold))  19.5 us
    ppermute x2, waiting for transfers between devices, sum_over_ka(): a_in, b_in = (lax.ppermute(a, 'ka', fold), lax.ppermute(b, 'ka', swap))  18.9 us
  transfers between devices with their start and end apart: 6, of which 6 were waited for; matrix products, arithmetic and copies ran while one was open for 3% of the time, Pallas kernels for 0%

profile of v1, /device:TPU:1, one launch (start us, length us, event | category | flops | bytes accessed | tf_op | source)
XLA Modules:
  0.0 395.7 jit_solution(14146960609934138147)
XLA Ops:
  6.5 0.0 copy-start
  6.5 0.0 copy-start.3
  6.5 0.0 all-gather.2.cloned.1.call-start
  6.5 2.3 constant_dynamic-slice_fusion
  8.9 0.0 copy-start.2
  8.9 0.0 all-gather.2.cloned.1.call-update
  8.9 0.0 copy-done.3
  8.9 0.1 reshape.27
  9.1 0.1 copy.15
  9.2 0.1 copy.12
  9.3 0.1 broadcast_in_dim.18
  9.4 49.7 %all_to_all.15.trial_ref = f32[64,32,128]{2,1,0:T(8,128)} all-to-all(f32[64,32,128]{2,1,0:T(8,128)S(1)} %broadcast_in_dim.18), channel_id=1, replica_groups=mesh['pb'=64,'ka'=4] {'pb'}, dimensions={0} | all-to-all | bytes 2097152 | tf_op jit(solution)/shard_map/all_to_all | solution.py:135
  59.1 0.0 copy-done.2
  59.1 3.8 broadcast_in_dim.16
  62.9 0.0 copy-start.4
  62.9 5.5 %all-to-all-start = ((f32[4,26,16,1024]{3,2,1,0:T(8,128)}), f32[4,26,16,1024]{3,2,1,0:T(8,128)}, u32[]{:S(2)}, u32[]{:S(2)}) async-start(f32[4,26,16,1024]{3,2,1,0:T(8,128)} %broadcast_in_dim.16), calls=%async_computation | async-start | bytes 13631488 | tf_op jit(solution)/shard_map/all_to_all | solution.py:130
  68.5 0.0 copy-done.4
  68.5 0.0 copy-done
  68.5 0.7 gather_fusion
  69.2 0.7 gather_fusion.1
  69.9 3.7 reshape.25
  73.6 2.1 pad.8
  75.7 0.6 and_select_fusion
  76.2 69.1 %all-to-all-done.valence_ref = f32[4,26,16,1024]{3,2,1,0:T(8,128)} async-done(((f32[4,26,16,1024]{3,2,1,0:T(8,128)}), f32[4,26,16,1024]{3,2,1,0:T(8,128)}, u32[]{:S(2)}, u32[]{:S(2)}) %all-to-all-start) | async-done | bytes 6815776 | tf_op jit(solution)/shard_map/all_to_all | solution.py:130
  145.3 121.4 %all-gather.2.cloned.1.call-done.matrix_ref = f32[64,1024,256]{2,1,0:T(8,128)} async-done(((f32[1,1024,256]{2,1,0:T(8,128)}), f32[64,1024,256]{2,1,0:T(8,128)}) %all-gather.2.cloned.1.call-update) | async-done | bytes 67108880 | tf_op jit(solution)/shard_map/all_gather | solution.py:128
  266.7 30.1 %shard_map.73 = f32[26,128,128]{2,1,0:T(8,128)} custom-call(s32[26]{0:T(128)} %bitcast.16, f32[4,26,16,1024]{3,2,1,0:T(8,128)} %all-to-all-done.valence_ref, f32[64,1024,256]{2,1,0:T(8,128)} %all-gather.2.cloned.1.call-done.matrix_ref, bf16[26,224,256]{2,1,0:T(8,128)(2,1)} %bitcast.13), custom_call_target="tpu_custom_call" | custom-call | flops 2617245696 | bytes 27262976 | tf_op jit(solution)/shard_map/pallas_call | solution.py:64
  296.8 0.0 copy-start.1
  296.8 1.7 fusion
  298.5 1.3 collective-permute-start
  299.8 1.8 collective-permute-start.2
  301.6 17.4 %collective-permute-done = f32[13,128,128]{2,1,0:T(8,128)S(1)} collective-permute-done((f32[13,128,128]{2,1,0:T(8,128)S(1)}, f32[13,128,128]{2,1,0:T(8,128)S(1)}, u32[]{:S(2)}, u32[]{:S(2)}) %collective-permute-start) | collective-permute-done | bytes 852000 | tf_op jit(solution)/shard_map/ppermute | solution.py:116
  319.0 2.1 collective-permute-done.2
  321.1 0.0 copy-done.1
  321.1 0.2 slice_add_fusion.1
  321.4 1.9 collective-permute-start.1
  323.3 0.0 collective-permute-start.3
  323.3 18.7 %collective-permute-done.1 = f32[13,128,128]{2,1,0:T(8,128)S(1)} collective-permute-done((f32[13,128,128]{2,1,0:T(8,128)S(1)}, f32[13,128,128]{2,1,0:T(8,128)S(1)}, u32[]{:S(2)}, u32[]{:S(2)}) %collective-permute-start.1) | collective-permute-done | bytes 852000 | tf_op jit(solution)/shard_map/ppermute | solution.py:118
  341.9 0.1 add.24
  342.0 0.2 collective-permute-done.3
  342.2 0.1 add.26
  342.3 1.3 pad_maximum_fusion.kernel_ref
  343.7 7.7 %shard_map.74 = f32[64,32,128]{2,1,0:T(8,128)} custom-call(s32[26]{0:T(128)} %get-tuple-element.11.near_ref, s32[26]{0:T(128)} %get-tuple-element.12.far_ref, f32[26,128,128]{2,1,0:T(8,128)} %pad_maximum_fusion.kernel_ref, f32[64,32,128]{2,1,0:T(8,128)} %all_to_all.15.trial_ref), custom_call_target="tpu_custom_call" | custom-call | flops 163577856 | bytes 3801088 | tf_op jit(solution)/shard_map/pallas_call | solution.py:102
  351.4 36.4 %all_to_all.16 = f32[64,32,128]{2,1,0:T(8,128)S(1)} all-to-all(f32[64,32,128]{2,1,0:T(8,128)} %shard_map.74), channel_id=1, replica_groups=mesh['pb'=64,'ka'=4] {'pb'}, dimensions={0} | all-to-all | bytes 2097152 | tf_op jit(solution)/shard_map/all_to_all | solution.py:143
  387.8 0.1 reduce_sum.9
  387.9 0.1 copy.13
  388.0 0.1 copy.14
  388.1 0.8 reshape.29
  (4 shorter events, 0.1 us)
Async XLA Ops:
  6.5 62.0 %copy-start = (s32[64]{0:T(128)S(1)}, s32[64]{0:T(128)}, u32[]{:S(2)}) copy-start(s32[64]{0:T(128)} %param.14) | copy-start | bytes 772
  6.5 2.3 copy-start.3
  6.5 260.2 %all-gather.2.cloned.1.call-start = ((), (), s32[]{:S(2)}) async-start(), calls=%async_computation.3 | async-start | bytes 68157440 | tf_op jit(solution)/shard_map/all_gather | solution.py:128
  8.9 50.3 %copy-start.2 = (f32[26,16,1024]{2,1,0:T(8,128)S(1)}, f32[26,16,1024]{2,1,0:T(8,128)}, u32[]{:S(2)}) copy-start(f32[26,16,1024]{2,1,0:T(8,128)} %param.9) | copy-start | bytes 5111812
  62.9 5.5 %copy-start.4 = (s32[26,2]{0,1:T(2,128)S(1)}, s32[26,2]{0,1:T(2,128)}, u32[]{:S(2)}) copy-start(s32[26,2]{0,1:T(2,128)} %param.13) | copy-start | bytes 628
  62.9 82.4 %all-to-all-start = ((f32[4,26,16,1024]{3,2,1,0:T(8,128)}), f32[4,26,16,1024]{3,2,1,0:T(8,128)}, u32[]{:S(2)}, u32[]{:S(2)}) async-start(f32[4,26,16,1024]{3,2,1,0:T(8,128)} %broadcast_in_dim.16), calls=%async_computation | async-start | bytes 13631488 | tf_op jit(solution)/shard_map/all_to_all | solution.py:130
  296.8 24.3 %copy-start.1 = (f32[26,128,128]{2,1,0:T(8,128)S(1)}, f32[26,128,128]{2,1,0:T(8,128)}, u32[]{:S(2)}) copy-start(f32[26,128,128]{2,1,0:T(8,128)} %shard_map.73) | copy-start | bytes 5111812
  298.5 20.5 %collective-permute-start = (f32[13,128,128]{2,1,0:T(8,128)S(1)}, f32[13,128,128]{2,1,0:T(8,128)S(1)}, u32[]{:S(2)}, u32[]{:S(2)}) collective-permute-start(f32[13,128,128]{2,1,0:T(8,128)S(1)} %get-tuple-element.18), channel_id=1, source_target_pairs={{0,1},{1,0},{2,3},{3,2},{4,5},{5,4},{6,7},{7,6},{8,9},{9,8},{10,11... | collective-permute-start | bytes 2555912 | tf_op jit(solution)/shard_map/ppermute | solution.py:116
  299.8 21.3 %collective-permute-start.2 = (f32[13,128,128]{2,1,0:T(8,128)S(1)}, f32[13,128,128]{2,1,0:T(8,128)S(1)}, u32[]{:S(2)}, u32[]{:S(2)}) collective-permute-start(f32[13,128,128]{2,1,0:T(8,128)S(1)} %get-tuple-element.19), channel_id=1, source_target_pairs={{0,3},{1,2},{2,1},{3,0},{4,7},{5,6},{6,5},{7,4},{8,11},{9,10},{10,... | collective-permute-start | bytes 2555912 | tf_op jit(solution)/shard_map/ppermute | solution.py:116
  321.4 20.6 %collective-permute-start.1 = (f32[13,128,128]{2,1,0:T(8,128)S(1)}, f32[13,128,128]{2,1,0:T(8,128)S(1)}, u32[]{:S(2)}, u32[]{:S(2)}) collective-permute-start(f32[13,128,128]{2,1,0:T(8,128)S(1)} %get-tuple-element.16), channel_id=1, source_target_pairs={{0,3},{1,2},{2,1},{3,0},{4,7},{5,6},{6,5},{7,4},{8,11},{9,10},{10,... | collective-permute-start | bytes 2555912 | tf_op jit(solution)/shard_map/ppermute | solution.py:118
  323.3 19.0 %collective-permute-start.3 = (f32[13,128,128]{2,1,0:T(8,128)S(1)}, f32[13,128,128]{2,1,0:T(8,128)S(1)}, u32[]{:S(2)}, u32[]{:S(2)}) collective-permute-start(f32[13,128,128]{2,1,0:T(8,128)S(1)} %get-tuple-element.17), channel_id=1, source_target_pairs={{0,1},{1,0},{2,3},{3,2},{4,5},{5,4},{6,7},{7,6},{8,9},{9,8},{10,11... | collective-permute-start | bytes 2555912 | tf_op jit(solution)/shard_map/ppermute | solution.py:118
Sparse Core Ops, SparseCore 0:
  10.1 256.5 all-gather.1

commit v2 on v1

v2 whole, which is shorter than its diff:
```python
import jax
import jax.numpy as jnp
from jax import lax
from jax.experimental import pallas as pl
from jax.experimental.pallas import tpu as pltpu
from jax.sharding import PartitionSpec as P

VB = 8
CB = 14
CD = 16
VC = VB * CD
F32 = jnp.float32
BF16 = jnp.bfloat16
PLAIN = ((1,), (0,))
TURNED = ((1,), (1,))


def split(x):
    high = x.astype(BF16)
    return high, (x - high.astype(F32)).astype(BF16)


def mul(a, b, dims):
    return lax.dot_general(a, b, (dims, ((), ())), preferred_element_type=F32)


def mul3(a, b, dims=PLAIN):
    rows = a.shape[0]
    a_high, a_low = split(a)
    b_high, b_low = split(b)
    both = mul(jnp.concatenate([a_high, a_low], axis=0), b_high, dims)
    return both[:rows] + both[rows:] + mul(a_high, b_low, dims)


def flat(ref):
    return ref[...].reshape(ref.shape[0] * ref.shape[2], ref.shape[3])


def opposite_body(momentum_ref, ka_ref, own_ref, other_ref, quads_ref, keep_ref, send_ref):
    half = own_ref.shape[3] // 2
    own, other = flat(own_ref), flat(other_ref)
    first = ka_ref[0] < 2
    quad_a, quad_b = quads_ref[0, :half, :], quads_ref[0, half:, :]
    other_a = jnp.where(first, other[:, :half], other[:, half:])
    other_b = jnp.where(first, other[:, half:], other[:, :half])
    keep_ref[0] = jnp.concatenate([mul3(other_a, quad_a, TURNED), mul3(other_b, quad_b, TURNED)], axis=1)
    send_a, send_b = mul3(own[:, :half], quad_a), mul3(own[:, half:], quad_b)
    send_ref[0, :, :half] = jnp.where(first, send_a, send_b)
    send_ref[0, :, half:] = jnp.where(first, send_b, send_a)


def next_body(momentum_ref, ka_ref, own_ref, other_ref, block_ref, keep_ref, send_ref):
    block = block_ref[0]
    keep_ref[0] = mul3(flat(other_ref), block, TURNED)
    send_ref[0] = mul3(flat(own_ref), block)


def off_diagonal(body, distance, momentum, ka, valence, blocks):
    parts, pairs, rows, waves = valence.shape
    own = waves // parts
    shape = jax.ShapeDtypeStruct((pairs, parts * rows, own), F32)
    result = pl.BlockSpec((1, parts * rows, own), lambda p, q, y: (p, 0, 0))
    return pl.pallas_call(
        body,
        out_shape=(shape, shape),
        grid_spec=pltpu.PrefetchScalarGridSpec(
            num_scalar_prefetch=2,
            grid=(pairs,),
            in_specs=[
                pl.BlockSpec((parts, 1, rows, own), lambda p, q, y: (0, p, 0, y[0])),
                pl.BlockSpec((parts, 1, rows, own), lambda p, q, y: (0, p, 0, (y[0] + distance) % parts)),
                pl.BlockSpec((1,) + blocks.shape[1:], lambda p, q, y: (q[p], 0, 0)),
            ],
            out_specs=(result, result),
        ),
        cost_estimate=pl.CostEstimate(
            flops=12 * pairs * parts * rows * blocks.shape[1] * blocks.shape[2],
            bytes_accessed=pairs * blocks.shape[1] * blocks.shape[2] * 4,
            transcendentals=0,
        ),
    )(momentum, ka, valence, valence, blocks)


def diagonal_body(momentum_ref, ka_ref, own_ref, quads_ref, add1_ref, add2_ref, add3_ref, add4_ref, conduct_ref, out_ref, low_ref, high_ref):
    half = own_ref.shape[3] // 2
    own = flat(own_ref)
    rows = own.shape[0]
    own_a, own_b = own[:, :half], own[:, half:]
    quads = quads_ref[0]
    turned = mul3(own_b, quads[:, half : 2 * half], TURNED)
    product = mul3(own_a, quads[:, : 2 * half]) + jnp.concatenate([turned, mul3(own_b, quads[:, 2 * half :])], axis=1)
    product = product + ((add1_ref[0] + add2_ref[0]) + (add3_ref[0] + add4_ref[0]))
    high, low = split(product)
    both = mul(jnp.concatenate([high, low], axis=0), conduct_ref[0], TURNED)
    kernel = both[:rows] + both[rows:]
    low_ref[...] = kernel[:, :VC]
    high_ref[...] = jnp.concatenate([kernel[:, VC:], jnp.zeros((rows, 2 * VC - kernel.shape[1]), F32)], axis=1)
    group = lax.broadcasted_iota(jnp.int32, (VB, VC), 1) // CD
    for number, ref in enumerate((low_ref, high_ref)):
        tiles = [ref[pl.ds(w, VB, stride=VB), :] for w in range(VB)]
        for step in (4, 2, 1):
            upper = (group & step) != 0
            for i in range(VB):
                if i & step:
                    continue
                a, b = tiles[i], tiles[i + step]
                tiles[i] = jnp.where(upper, pltpu.roll(b, step * CD, axis=1), a)
                tiles[i + step] = jnp.where(upper, b, pltpu.roll(a, VC - step * CD, axis=1))
        for i in range(VB):
            c = number * VB + i
            if c < CB:
                out_ref[0, c * VB : (c + 1) * VB, :] = tiles[i]


def diagonal(start, count, momentum, ka, valence, quads, adds, conduction):
    parts, pairs, rows, waves = valence.shape
    own = waves // parts
    columns = conduction.shape[1]
    add = pl.BlockSpec((1, parts * rows, own), lambda p, q, y: (start + p, 0, 0))
    return pl.pallas_call(
        diagonal_body,
        out_shape=jax.ShapeDtypeStruct((count, VB * CB, VC), F32),
        grid_spec=pltpu.PrefetchScalarGridSpec(
            num_scalar_prefetch=2,
            grid=(count,),
            in_specs=[
                pl.BlockSpec((parts, 1, rows, own), lambda p, q, y: (0, start + p, 0, y[0])),
                pl.BlockSpec((1,) + quads.shape[1:], lambda p, q, y: (q[start + p], 0, 0)),
                add,
                add,
                add,
                add,
                pl.BlockSpec((1, columns, own), lambda p, q, y: (start + p, 0, 0)),
            ],
            out_specs=pl.BlockSpec((1, VB * CB, VC), lambda p, q, y: (p, 0, 0)),
            scratch_shapes=[pltpu.VMEM((VB * VB, VC), F32), pltpu.VMEM((VB * VB, VC), F32)],
        ),
        cost_estimate=pl.CostEstimate(flops=6 * count * 64 * own * own, bytes_accessed=count * own * own * 12, transcendentals=0),
    )(momentum, ka, valence, quads, *adds, conduction)


def response_body(near_ref, far_ref, first_ref, second_ref, trial_ref, out_ref, turn_ref):
    out_ref[...] = jnp.zeros_like(out_ref)
    turn_ref[...] = jnp.zeros_like(turn_ref)
    for start, kernel_ref in ((0, first_ref), (first_ref.shape[0], second_ref)):

        @pl.loop(0, kernel_ref.shape[0])
        def _(p, start=start, kernel_ref=kernel_ref):
            near, far = near_ref[start + p], far_ref[start + p]
            for v in range(VB):
                turn_ref[v * CD : v * CD + CB, :] = kernel_ref[p, pl.ds(v, CB, stride=VB), :]
            kernel = turn_ref[...]
            direct = mul3(trial_ref[far], kernel, TURNED)
            mirror = mul3(trial_ref[near], kernel, PLAIN)
            out_ref[near] = out_ref[near] + direct
            out_ref[far] = out_ref[far] + mirror


def contributions(near, far, first, second, trials):
    whole = pl.BlockSpec(memory_space=pltpu.VMEM)
    scalar = pl.BlockSpec(memory_space=pltpu.SMEM)
    size = first.size + second.size
    return pl.pallas_call(
        response_body,
        out_shape=jax.ShapeDtypeStruct(trials.shape, F32),
        in_specs=[scalar, scalar, whole, whole, whole],
        out_specs=whole,
        scratch_shapes=[pltpu.VMEM((VC, VC), F32)],
        cost_estimate=pl.CostEstimate(flops=12 * size * trials.shape[1], bytes_accessed=4 * (size + 2 * trials.size), transcendentals=0),
    )(near, far, first, second, trials)


def local(valence, conduction, screened, momentum, kpairs, kpoint_slot, trial_blocks):
    ka = lax.axis_size("ka")
    pair_dev = valence.shape[0]
    own = conduction.shape[2]
    half = own // 2
    here = lax.axis_index("ka").astype(jnp.int32)
    target = momentum[:, 0]
    matrix = screened[0]

    def block(row, column, rows, columns):
        return lax.dynamic_slice(matrix, (row, column), (rows, columns))

    top = here * own
    across = lax.rem(here + 2, ka) * own
    side = jnp.where(here < 2, 0, half)
    opposite = jnp.concatenate([block(top, across + side, half, half), block(top + half, across + half - side, half, half)], axis=0)
    beside = block(top, lax.rem(here + 1, ka) * own, own, own)
    middle = jnp.concatenate([block(top, top, half, own), block(top + half, top + half, half, half)], axis=1)
    opposite = lax.all_gather(opposite, "pb")
    beside = lax.all_gather(beside, "pb")
    middle = lax.all_gather(middle, "pb")

    spread = jnp.broadcast_to(valence[None], (ka,) + valence.shape)
    rows = lax.all_to_all(spread, "ka", split_axis=0, concat_axis=0, tiled=True)
    own_trials = trial_blocks.reshape(-1, VB, CB)
    local_trials = own_trials.shape[0]
    own_trials = jnp.pad(own_trials, ((0, 0), (0, 0), (0, CD - CB))).reshape(local_trials, VC)
    trials = lax.all_gather(own_trials, "pb")
    conduct = conduction.reshape(pair_dev, CB, CB, own)
    conduct = jnp.pad(conduct, ((0, 0), (0, 0), (0, CD - CB), (0, 0))).reshape(pair_dev, CB * CD, own)
    near = jnp.take(kpoint_slot, kpairs[:, 0])
    far = jnp.take(kpoint_slot, kpairs[:, 1])
    rows, conduct, near, far = lax.optimization_barrier((rows, conduct, near, far))

    here = here.reshape(1)
    keep2, send2 = off_diagonal(opposite_body, 2, target, here, rows, opposite)
    came2 = lax.ppermute(send2, "ka", [(i, (i + 2) % ka) for i in range(ka)])
    keep1, send1 = off_diagonal(next_body, 1, target, here, rows, beside)
    came1 = lax.ppermute(send1, "ka", [(i, (i + 1) % ka) for i in range(ka)])

    swap = [(i, i ^ 1) for i in range(ka)]
    fold = [(i, ka - 1 - i) for i in range(ka)]
    adds = (keep1, keep2, came1, came2)
    cut = pair_dev // 2
    first = diagonal(0, cut, target, here, rows, middle, adds, conduct)
    second = diagonal(cut, pair_dev - cut, target, here, rows, middle, adds, conduct)
    first = first + lax.ppermute(first, "ka", swap)
    second = second + lax.ppermute(second, "ka", fold)
    first = first + lax.ppermute(first, "ka", fold)
    second = second + lax.ppermute(second, "ka", swap)

    summed = contributions(near, far, first, second, trials)
    parts = lax.all_to_all(summed, "pb", split_axis=0, concat_axis=0, tiled=True)
    response = jnp.sum(parts, axis=0).reshape(local_trials, VB, CD)[:, :, :CB]
    return response.reshape(1, -1)


def solution(mesh):
    return jax.shard_map(
        local,
        mesh=mesh,
        in_specs=(
            P("pb", "ka", None),
            P("pb", None, "ka"),
            P("pb", None, None),
            P("pb", None),
            P("pb", None),
            P(),
            P("pb", "ka"),
        ),
        out_specs=P("pb", "ka"),
        check_vma=False,
    )
```

time: 397 us -> 415 us (1.045)
  blocking collectives: 86.1 us -> 35.2 us
  Pallas kernels: 37.8 us -> 74.3 us
  waiting for transfers between devices: 229 us -> 251 us
    all_to_all x1 -> x0, blocking collectives: 49.7 us -> none  [local(): lax.all_to_all(spread, 'pb', split_axis=0, concat_axis=0, tiled=True)]
    pallas_call x1 -> x4, Pallas kernels: 30.1 us -> 66.3 us  [the longest x2 38.2 us: off_diagonal(): pl.pallas_call(body, out_shape=(shape, shape), grid_spec=pltpu.PrefetchSc...]
    all_gather x1 -> x4, waiting for transfers between devices: 121 us -> 151 us  [the longest x1 77.6 us: local(): beside = lax.all_gather(beside, 'pb')]
    ppermute x4 -> x6, waiting for transfers between devices: 38.4 us -> 33.1 us  [the longest x1 14.8 us: local(): first = first + lax.ppermute(first, 'ka', swap)]
  transfers between devices with their start and end apart: 6 -> 11, of which waited for: 6 -> 9; matrix products, arithmetic and copies ran while one was open for 3% -> 5% of each run, Pallas kernels for 0% -> 16%
where the time goes in v2:
time: 415 us; the launch traced here: 413 us
  waiting for transfers between devices  251 us (60%)
  Pallas kernels  74.3 us (18%)
  blocking collectives  35.2 us (8%)
  local copies, waits for them, and re-layouts  19.9 us (5%)
  between operations  13.3 us (3%)
  starting transfers between devices  12.8 us (3%)
  other arithmetic  6.03 us (1%)
    all_gather x1, waiting for transfers between devices, local(): beside = lax.all_gather(beside, 'pb')  77.6 us
    all_to_all x1, waiting for transfers between devices, local(): rows = lax.all_to_all(spread, 'ka', split_axis=0, concat_axis=0, tiled=True)  67.5 us
    all_gather x1, waiting for transfers between devices, local(): middle = lax.all_gather(middle, 'pb')  64.7 us
    pallas_call x2, Pallas kernels, off_diagonal(): pl.pallas_call(body, out_shape=(shape, shape), grid_spec=pltpu.PrefetchSc...  38.2 us
    all_to_all x1, blocking collectives, local(): lax.all_to_all(summed, 'pb', split_axis=0, concat_axis=0, tiled=True)  35.2 us
    pallas_call x2, Pallas kernels, diagonal(): pl.pallas_call(diagonal_body, out_shape=jax.ShapeDtypeStruct((count, VB *...  28.1 us
    ppermute x1, waiting for transfers between devices, local(): first = first + lax.ppermute(first, 'ka', swap)  14.8 us
    ppermute x1, waiting for transfers between devices, local(): second = second + lax.ppermute(second, 'ka', swap)  14.1 us
  transfers between devices with their start and end apart: 11, of which 9 were waited for; matrix products, arithmetic and copies ran while one was open for 5% of the time, Pallas kernels for 16%

profile of v2, /device:TPU:1, one launch (start us, length us, event | category | flops | bytes accessed | tf_op | source)
XLA Modules:
  0.0 412.8 jit_solution(5501983622876573741)
XLA Ops:
  6.5 0.0 copy-start
  6.5 0.0 all-gather.13.cloned.1.call-start
  6.5 1.0 dynamic-slice_bitcast_fusion.2
  7.6 0.7 pad_maximum_fusion.1
  8.3 0.0 all-gather.13.cloned.1.call-update
  8.3 0.0 all-gather.7.cloned.1.call-start
  8.3 1.7 constant_dynamic-slice_fusion
  10.0 0.0 all-gather.7.cloned.1.call-update
  10.0 0.0 all-gather.11.cloned.1.call-start
  10.1 0.9 dynamic-slice_bitcast_fusion
  11.0 0.7 pad_maximum_fusion
  11.7 0.0 all-gather.11.cloned.1.call-update
  11.7 0.0 copy-done.5
  11.7 3.7 broadcast_in_dim.4
  15.4 5.5 %all-to-all-start = ((f32[4,26,16,1024]{3,2,1,0:T(8,128)}), f32[4,26,16,1024]{3,2,1,0:T(8,128)}, u32[]{:S(2)}, u32[]{:S(2)}) async-start(f32[4,26,16,1024]{3,2,1,0:T(8,128)} %broadcast_in_dim.4), calls=%async_computation | async-start | bytes 13631488 | tf_op jit(solution)/shard_map/all_to_all | solution.py:196
  20.9 0.0 all-gather.9.cloned.1.call-start
  21.0 0.0 copy-done.7
  21.0 0.0 copy-done
  21.0 0.7 gather_fusion
  21.7 0.7 gather_fusion.1
  22.4 3.7 reshape.30
  26.1 2.1 pad.8
  28.2 0.5 and_select_fusion
  28.8 67.5 %all-to-all-done.own_ref.other_ref = f32[4,26,16,1024]{3,2,1,0:T(8,128)} async-done(((f32[4,26,16,1024]{3,2,1,0:T(8,128)}), f32[4,26,16,1024]{3,2,1,0:T(8,128)}, u32[]{:S(2)}, u32[]{:S(2)}) %all-to-all-start) | async-done | bytes 6815776 | tf_op jit(solution)/shard_map/all_to_all | solution.py:196
  96.3 1.0 all-gather.13.cloned.1.call-done
  97.3 18.5 %shard_map.74 = (f32[26,64,256]{2,1,0:T(8,128)}, f32[26,64,256]{2,1,0:T(8,128)}) custom-call(s32[26]{0:T(128)} %bitcast.31, s32[1]{0:T(128)} %bitcast.4.ka_ref, f32[4,26,16,1024]{3,2,1,0:T(8,128)} %all-to-all-done.own_ref.other_ref, f32[4,26,16,1024]{3,2,1,0:T(8,128)} %all-to-all-done.own_ref.other_ref, f32[64,256,128]{2,1,0:T(8,128)} %bitcast.28), custom_call_target="tpu_custom_call" | custom-call | flops 654311424 | bytes 3407872 | tf_op jit(solution)/shard_map/pallas_call | solution.py:63
  115.8 2.7 collective-permute-start.1
  118.5 77.6 %all-gather.7.cloned.1.call-done.block_ref = f32[64,256,256]{2,1,0:T(8,128)} async-done(((f32[1,256,256]{2,1,0:T(8,128)}), f32[64,256,256]{2,1,0:T(8,128)}) %all-gather.7.cloned.1.call-update) | async-done | bytes 16777232 | tf_op jit(solution)/shard_map/all_gather | solution.py:192
  196.1 19.7 %shard_map.73 = (f32[26,64,256]{2,1,0:T(8,128)}, f32[26,64,256]{2,1,0:T(8,128)}) custom-call(s32[26]{0:T(128)} %bitcast.32, s32[1]{0:T(128)} %bitcast.4.ka_ref, f32[4,26,16,1024]{3,2,1,0:T(8,128)} %all-to-all-done.own_ref.other_ref, f32[4,26,16,1024]{3,2,1,0:T(8,128)} %all-to-all-done.own_ref.other_ref, f32[64,256,256]{2,1,0:T(8,128)} %all-gather.7.cloned.1.call-done.block_ref), custom_call_target="tpu_custom_call" | custom-call | flops 1308622848 | bytes 6815744 | tf_op jit(solution)/shard_map/pallas_call | solution.py:63
  215.7 1.2 collective-permute-start
  216.9 0.0 copy-done.6
  216.9 0.6 reduce
  217.6 0.9 reshape.33
  218.4 0.8 copy.15
  219.2 0.8 pad.9.clone
  220.1 0.7 copy.12
  220.7 0.0 all-gather.9.cloned.1.call-update
  220.8 0.0 collective-permute-done.1.add4_ref
  220.8 0.0 copy-start.2
  220.8 64.7 %all-gather.11.cloned.1.call-done = f32[8192,384]{1,0:T(8,128)} async-done(((f32[128,384]{1,0:T(8,128)}), f32[8192,384]{1,0:T(8,128)}) %all-gather.11.cloned.1.call-update) | async-done | bytes 12582928 | tf_op jit(solution)/shard_map/all_gather | solution.py:193
  285.5 0.0 collective-permute-done.add3_ref
  285.5 1.2 copy-done.3
  286.7 14.1 %shard_map.76 = f32[13,112,128]{2,1,0:T(8,128)} custom-call(s32[26]{0:T(128)} %bitcast.33, s32[1]{0:T(128)} %bitcast.4.ka_ref, f32[4,26,16,1024]{3,2,1,0:T(8,128)} %all-to-all-done.own_ref.other_ref, f32[64,128,384]{2,1,0:T(8,128)} %bitcast.24, f32[26,64,256]{2,1,0:T(8,128)} %get-tuple-element.17.add1_ref, f32[26,64,256]{2,1,0:T(8,128)} %get-tuple-element.18.add2_ref, ...), custom_call_target="tpu_custom_call" | custom-call | flops 327155712 | bytes 10223616 | tf_op jit(solution)/shard_map/pallas_call | solution.py:120
  300.7 2.5 collective-permute-start.4
  303.2 14.1 %shard_map.75 = f32[13,112,128]{2,1,0:T(8,128)} custom-call(s32[26]{0:T(128)} %bitcast.34, s32[1]{0:T(128)} %bitcast.4.ka_ref, f32[4,26,16,1024]{3,2,1,0:T(8,128)} %all-to-all-done.own_ref.other_ref, f32[64,128,384]{2,1,0:T(8,128)} %bitcast.25, f32[26,64,256]{2,1,0:T(8,128)} %get-tuple-element.17.add1_ref, f32[26,64,256]{2,1,0:T(8,128)} %get-tuple-element.18.add2_ref, ...), custom_call_target="tpu_custom_call" | custom-call | flops 327155712 | bytes 10223616 | tf_op jit(solution)/shard_map/pallas_call | solution.py:120
  317.3 0.0 collective-permute-start.2
  317.3 2.8 collective-permute-done.4
  320.1 0.1 add.70
  320.2 0.2 collective-permute-start.5
  320.4 14.8 %collective-permute-done.2 = f32[13,112,128]{2,1,0:T(8,128)S(1)} collective-permute-done((f32[13,112,128]{2,1,0:T(8,128)}, f32[13,112,128]{2,1,0:T(8,128)S(1)}, u32[]{:S(2)}, u32[]{:S(2)}) %collective-permute-start.2) | collective-permute-done | bytes 745504 | tf_op jit(solution)/shard_map/ppermute | solution.py:219
  335.2 1.3 add.68
  336.4 0.6 collective-permute-start.3
  337.0 14.1 %collective-permute-done.5 = f32[13,112,128]{2,1,0:T(8,128)S(1)} collective-permute-done((f32[13,112,128]{2,1,0:T(8,128)S(1)}, f32[13,112,128]{2,1,0:T(8,128)S(1)}, u32[]{:S(2)}, u32[]{:S(2)}) %collective-permute-start.5) | collective-permute-done | bytes 745504 | tf_op jit(solution)/shard_map/ppermute | solution.py:222
  351.1 1.0 add.71.second_ref
  352.1 1.4 collective-permute-done.3
  353.6 1.0 add.69.first_ref
  354.6 7.4 %all-gather.9.cloned.1.call-done.trial_ref = f32[64,32,128]{2,1,0:T(8,128)} async-done(((f32[1,32,128]{2,1,0:T(8,128)}), f32[64,32,128]{2,1,0:T(8,128)}) %all-gather.9.cloned.1.call-update) | async-done | bytes 1048592 | tf_op jit(solution)/shard_map/all_gather | solution.py:200
  362.0 8.0 %shard_map.77 = f32[64,32,128]{2,1,0:T(8,128)} custom-call(s32[26]{0:T(128)} %get-tuple-element.14.near_ref, s32[26]{0:T(128)} %get-tuple-element.15.far_ref, f32[13,112,128]{2,1,0:T(8,128)} %add.69.first_ref, f32[13,112,128]{2,1,0:T(8,128)} %add.71.second_ref, f32[64,32,128]{2,1,0:T(8,128)} %all-gather.9.cloned.1.call-done.trial_ref), custom_call_target="tpu_custom_call" | custom-call | flops 143130624 | bytes 3588096 | tf_op jit(solution)/shard_map/pallas_call | solution.py:163
  370.0 35.2 %all_to_all.10 = f32[64,32,128]{2,1,0:T(8,128)S(1)} all-to-all(f32[64,32,128]{2,1,0:T(8,128)} %shard_map.77), channel_id=1, replica_groups=mesh['pb'=64,'ka'=4] {'pb'}, dimensions={0} | all-to-all | bytes 2097152 | tf_op jit(solution)/shard_map/all_to_all | solution.py:225
  405.2 0.1 reduce_sum.9
  405.3 0.1 copy.13
  405.4 0.1 copy.14
  405.5 0.8 reshape.35
  406.3 0.0 copy-done.1
  (10 shorter events, 0.0 us)
Async XLA Ops:
  6.5 14.5 %copy-start = (s32[64]{0:T(128)S(1)}, s32[64]{0:T(128)}, u32[]{:S(2)}) copy-start(s32[64]{0:T(128)} %param.14) | copy-start | bytes 772
  6.5 5.2 %copy-start.5 = (f32[26,16,1024]{2,1,0:T(8,128)S(1)}, f32[26,16,1024]{2,1,0:T(8,128)}, u32[]{:S(2)}) copy-start(f32[26,16,1024]{2,1,0:T(8,128)} %param.9) | copy-start | bytes 5111812
  6.5 90.7 %all-gather.13.cloned.1.call-start = ((), (), s32[]{:S(2)}) async-start(), calls=%async_computation.5 | async-start | bytes 8519680 | tf_op jit(solution)/shard_map/all_gather | solution.py:191
  8.3 187.8 %all-gather.7.cloned.1.call-start = ((), (), s32[]{:S(2)}) async-start(), calls=%async_computation.2 | async-start | bytes 17039360 | tf_op jit(solution)/shard_map/all_gather | solution.py:192
  10.0 275.4 %all-gather.11.cloned.1.call-start = ((), (), s32[]{:S(2)}) async-start(), calls=%async_computation.4 | async-start | bytes 12779520 | tf_op jit(solution)/shard_map/all_gather | solution.py:193
  15.4 5.5 %copy-start.7 = (s32[26,2]{0,1:T(2,128)S(1)}, s32[26,2]{0,1:T(2,128)}, u32[]{:S(2)}) copy-start(s32[26,2]{0,1:T(2,128)} %param.13) | copy-start | bytes 628
  15.4 80.9 %all-to-all-start = ((f32[4,26,16,1024]{3,2,1,0:T(8,128)}), f32[4,26,16,1024]{3,2,1,0:T(8,128)}, u32[]{:S(2)}, u32[]{:S(2)}) async-start(f32[4,26,16,1024]{3,2,1,0:T(8,128)} %broadcast_in_dim.4), calls=%async_computation | async-start | bytes 13631488 | tf_op jit(solution)/shard_map/all_to_all | solution.py:196
  20.9 341.1 %all-gather.9.cloned.1.call-start = ((), (), s32[]{:S(2)}) async-start(), calls=%async_computation.3 | async-start | bytes 1064960 | tf_op jit(solution)/shard_map/all_gather | solution.py:200
  115.8 101.2 %copy-start.6 = (f32[1,3584]{1,0:T(1,128)S(1)}, f32[1,3584]{1,0:T(1,128)}, u32[]{:S(2)}) copy-start(f32[1,3584]{1,0:T(1,128)} %param.15) | copy-start | bytes 43012
  115.8 105.0 %collective-permute-start.1 = (f32[26,64,256]{2,1,0:T(8,128)}, f32[26,64,256]{2,1,0:T(8,128)S(1)}, u32[]{:S(2)}, u32[]{:S(2)}) collective-permute-start(f32[26,64,256]{2,1,0:T(8,128)} %get-tuple-element.20), channel_id=1, source_target_pairs={{0,2},{1,3},{2,0},{3,1},{4,6},{5,7},{6,4},{7,5},{8,10},{9,11},{10,... | collective-permute-start | bytes 5111816 | tf_op jit(solution)/shard_map/ppermute | solution.py:209
  215.7 69.7 %collective-permute-start = (f32[26,64,256]{2,1,0:T(8,128)}, f32[26,64,256]{2,1,0:T(8,128)S(1)}, u32[]{:S(2)}, u32[]{:S(2)}) collective-permute-start(f32[26,64,256]{2,1,0:T(8,128)} %get-tuple-element.19), channel_id=1, source_target_pairs={{0,1},{1,2},{2,3},{3,0},{4,5},{5,6},{6,7},{7,4},{8,9},{9,10},{10,1... | collective-permute-start | bytes 5111816 | tf_op jit(solution)/shard_map/ppermute | solution.py:211
  220.8 64.7 %copy-start.2 = (f32[26,64,256]{2,1,0:T(8,128)}, f32[26,64,256]{2,1,0:T(8,128)S(1)}, u32[]{:S(2)}) copy-start(f32[26,64,256]{2,1,0:T(8,128)S(1)} %collective-permute-done.1.add4_ref) | copy-start | bytes 5111812
  285.5 1.2 copy-start.3
  300.7 19.4 %copy-start.4 = (f32[13,112,128]{2,1,0:T(8,128)S(1)}, f32[13,112,128]{2,1,0:T(8,128)}, u32[]{:S(2)}) copy-start(f32[13,112,128]{2,1,0:T(8,128)} %shard_map.76) | copy-start | bytes 2236420
  300.7 19.4 %collective-permute-start.4 = (f32[13,112,128]{2,1,0:T(8,128)}, f32[13,112,128]{2,1,0:T(8,128)S(1)}, u32[]{:S(2)}, u32[]{:S(2)}) collective-permute-start(f32[13,112,128]{2,1,0:T(8,128)} %shard_map.76), channel_id=1, source_target_pairs={{0,3},{1,2},{2,1},{3,0},{4,7},{5,6},{6,5},{7,4},{8,11},{9,10},{10,... | collective-permute-start | bytes 2236424 | tf_op jit(solution)/shard_map/ppermute | solution.py:220
  317.3 17.9 %collective-permute-start.2 = (f32[13,112,128]{2,1,0:T(8,128)}, f32[13,112,128]{2,1,0:T(8,128)S(1)}, u32[]{:S(2)}, u32[]{:S(2)}) collective-permute-start(f32[13,112,128]{2,1,0:T(8,128)} %shard_map.75), channel_id=1, source_target_pairs={{0,1},{1,0},{2,3},{3,2},{4,5},{5,4},{6,7},{7,6},{8,9},{9,8},{10,11... | collective-permute-start | bytes 2236424 | tf_op jit(solution)/shard_map/ppermute | solution.py:219
  320.2 30.9 %collective-permute-start.5 = (f32[13,112,128]{2,1,0:T(8,128)S(1)}, f32[13,112,128]{2,1,0:T(8,128)S(1)}, u32[]{:S(2)}, u32[]{:S(2)}) collective-permute-start(f32[13,112,128]{2,1,0:T(8,128)S(1)} %add.70), channel_id=1, source_target_pairs={{0,1},{1,0},{2,3},{3,2},{4,5},{5,4},{6,7},{7,6},{8,9},{9,8},{10,11... | collective-permute-start | bytes 2236424 | tf_op jit(solution)/shard_map/ppermute | solution.py:222
  336.4 17.1 %collective-permute-start.3 = (f32[13,112,128]{2,1,0:T(8,128)S(1)}, f32[13,112,128]{2,1,0:T(8,128)S(1)}, u32[]{:S(2)}, u32[]{:S(2)}) collective-permute-start(f32[13,112,128]{2,1,0:T(8,128)S(1)} %add.68), channel_id=1, source_target_pairs={{0,3},{1,2},{2,1},{3,0},{4,7},{5,6},{6,5},{7,4},{8,11},{9,10},{10,... | collective-permute-start | bytes 2236424 | tf_op jit(solution)/shard_map/ppermute | solution.py:221
  353.6 52.7 %copy-start.1 = (s32[64]{0:T(128)S(1)}, s32[64]{0:T(128)}, u32[]{:S(2)}) copy-start(s32[64]{0:T(128)} %param.14) | copy-start | bytes 772
Sparse Core Ops, SparseCore 0:
  10.1 87.1 all-gather.12
  100.1 95.9 all-gather.6
  198.8 86.5 all-gather.10
  288.1 73.8 all-gather.8

commit v3 on v2

v3 whole, which is shorter than its diff:
```python
import jax
import jax.numpy as jnp
from jax import lax
from jax.experimental import pallas as pl
from jax.experimental.pallas import tpu as pltpu
from jax.sharding import PartitionSpec as P

VB = 8
CB = 14
CD = 16
VC = VB * CD
F32 = jnp.float32
BF16 = jnp.bfloat16
PLAIN = ((1,), (0,))
TURNED = ((1,), (1,))


def split(x):
    high = x.astype(BF16)
    return high, (x - high.astype(F32)).astype(BF16)


def mul(a, b, dims):
    return lax.dot_general(a, b, (dims, ((), ())), preferred_element_type=F32)


def mul3(a, b, dims=PLAIN):
    rows = a.shape[0]
    a_high, a_low = split(a)
    b_high, b_low = split(b)
    both = mul(jnp.concatenate([a_high, a_low], axis=0), b_high, dims)
    return both[:rows] + both[rows:] + mul(a_high, b_low, dims)


def pair_body(momentum_ref, ka_ref, *refs):
    parts = len(refs) // 3 - 2
    valence_refs = refs[: 3 * parts]
    blocks_ref, conduct_ref, conduct_next_ref, out_ref, low_ref, high_ref = refs[3 * parts :]
    own, beside, across = (
        jnp.concatenate([ref[0] for ref in valence_refs[i * parts : (i + 1) * parts]], axis=0) for i in range(3)
    )
    rows, width = own.shape
    half = width // 2
    blocks = blocks_ref[0]
    corner = blocks[:, half : 2 * half]
    start = 3 * half
    next_block = jnp.concatenate([blocks[:, start : start + width], blocks[:, start + width : start + 2 * width]], axis=0)
    start += 2 * width
    far_block = jnp.concatenate([blocks[:, start : start + width], blocks[:, start + width : start + 2 * width]], axis=0)
    below = jnp.concatenate([mul3(own[:, half:], corner, TURNED), mul3(own[:, half:], blocks[:, 2 * half : 3 * half])], axis=1)
    here = mul3(own[:, :half], blocks[:, : 2 * half]) + below + mul3(beside, next_block) + mul3(across, far_block)
    there = mul3(own, next_block, TURNED)
    product = jnp.concatenate([here, there], axis=1)
    high, low = split(product)
    conduct = jnp.concatenate([conduct_ref[0], conduct_next_ref[0].astype(BF16)], axis=1)
    both = mul(jnp.concatenate([high, low], axis=0), conduct, TURNED)
    kernel = both[:rows] + both[rows:]
    each = rows // parts
    rest = jnp.zeros((each, 2 * VC - kernel.shape[1]), F32)
    for k in range(parts):
        place = pl.ds(pl.multiple_of(lax.rem(ka_ref[0] + parts - k, parts) * each, each), each)
        part = kernel[k * each : (k + 1) * each]
        low_ref[place, :] = part[:, :VC]
        high_ref[place, :] = jnp.concatenate([part[:, VC:], rest], axis=1)
    group = lax.broadcasted_iota(jnp.int32, (VB, VC), 1) // CD
    for number, ref in enumerate((low_ref, high_ref)):
        tiles = [ref[pl.ds(w, VB, stride=VB), :] for w in range(VB)]
        for step in (4, 2, 1):
            upper = (group & step) != 0
            for i in range(VB):
                if i & step:
                    continue
                a, b = tiles[i], tiles[i + step]
                tiles[i] = jnp.where(upper, pltpu.roll(b, step * CD, axis=1), a)
                tiles[i + step] = jnp.where(upper, b, pltpu.roll(a, VC - step * CD, axis=1))
        for i in range(VB):
            c = number * VB + i
            if c < CB:
                out_ref[0, c * VB : (c + 1) * VB, :] = tiles[i]


def pair_kernels(start, count, momentum, ka, valence, blocks, conduction, conduction_next):
    pairs, rows, waves = valence[0].shape
    parts = len(valence)
    own = waves // parts
    columns = conduction.shape[1]

    def column(i):
        return pl.BlockSpec((1, rows, own), lambda p, q, y: (start + p, 0, (y[0] + i) % parts))

    conduct = pl.BlockSpec((1, columns, own), lambda p, q, y: (start + p, 0, 0))
    return pl.pallas_call(
        pair_body,
        out_shape=jax.ShapeDtypeStruct((count, VB * CB, VC), F32),
        grid_spec=pltpu.PrefetchScalarGridSpec(
            num_scalar_prefetch=2,
            grid=(count,),
            in_specs=[column(i) for i in range(3) for _ in range(parts)]
            + [pl.BlockSpec((1,) + blocks.shape[1:], lambda p, q, y: (q[start + p], 0, 0)), conduct, conduct],
            out_specs=pl.BlockSpec((1, VB * CB, VC), lambda p, q, y: (p, 0, 0)),
            scratch_shapes=[pltpu.VMEM((VB * VB, VC), F32), pltpu.VMEM((VB * VB, VC), F32)],
        ),
        cost_estimate=pl.CostEstimate(flops=24 * count * 64 * own * own, bytes_accessed=count * own * own * 12, transcendentals=0),
    )(momentum, ka, *(valence * 3), blocks, conduction, conduction_next)


def response_body(near_ref, far_ref, first_ref, second_ref, trial_ref, out_ref, turn_ref):
    out_ref[...] = jnp.zeros_like(out_ref)
    turn_ref[...] = jnp.zeros_like(turn_ref)
    for start, kernel_ref in ((0, first_ref), (first_ref.shape[0], second_ref)):

        @pl.loop(0, kernel_ref.shape[0])
        def _(p, start=start, kernel_ref=kernel_ref):
            near, far = near_ref[start + p], far_ref[start + p]
            for v in range(VB):
                turn_ref[v * CD : v * CD + CB, :] = kernel_ref[p, pl.ds(v, CB, stride=VB), :]
            kernel = turn_ref[...]
            direct = mul3(trial_ref[far], kernel, TURNED)
            mirror = mul3(trial_ref[near], kernel, PLAIN)
            out_ref[near] = out_ref[near] + direct
            out_ref[far] = out_ref[far] + mirror


def contributions(near, far, first, second, trials):
    whole = pl.BlockSpec(memory_space=pltpu.VMEM)
    scalar = pl.BlockSpec(memory_space=pltpu.SMEM)
    size = first.size + second.size
    return pl.pallas_call(
        response_body,
        out_shape=jax.ShapeDtypeStruct(trials.shape, F32),
        in_specs=[scalar, scalar, whole, whole, whole],
        out_specs=whole,
        scratch_shapes=[pltpu.VMEM((VC, VC), F32)],
        cost_estimate=pl.CostEstimate(flops=12 * size * trials.shape[1], bytes_accessed=4 * (size + 2 * trials.size), transcendentals=0),
    )(near, far, first, second, trials)


def local(valence, conduction, screened, momentum, kpairs, kpoint_slot, trial_blocks):
    ka = lax.axis_size("ka")
    pair_dev = valence.shape[0]
    own = conduction.shape[2]
    half = own // 2
    here = lax.axis_index("ka").astype(jnp.int32)
    target = momentum[:, 0]
    matrix = screened[0]

    def block(row, column, rows, columns):
        return lax.dynamic_slice(matrix, (row, column), (rows, columns))

    top = here * own
    beside, across = lax.rem(here + 1, ka) * own, lax.rem(here + 2, ka) * own
    pieces = [block(top, top, half, own), block(top + half, top + half, half, half)]
    pieces += [block(row + side, top, half, own) for row in (beside, across) for side in (0, half)]
    blocks = lax.all_gather(jnp.concatenate(pieces, axis=1), "pb")

    own_trials = trial_blocks.reshape(-1, VB, CB)
    local_trials = own_trials.shape[0]
    own_trials = jnp.pad(own_trials, ((0, 0), (0, 0), (0, CD - CB))).reshape(local_trials, VC)
    trials = lax.all_gather(own_trials, "pb")
    ahead = [(i, (i + 1) % ka) for i in range(ka)]
    back = [((i + 1) % ka, i) for i in range(ka)]
    conduct = conduction.reshape(pair_dev, CB, CB, own)
    conduct = jnp.pad(conduct, ((0, 0), (0, 0), (0, CD - CB), (0, 0))).reshape(pair_dev, CB * CD, own)
    conduct_next = lax.ppermute(conduct.astype(F32), "ka", back)
    rows = [valence]
    for _ in range(ka - 1):
        rows.append(lax.ppermute(rows[-1], "ka", ahead))
    near = jnp.take(kpoint_slot, kpairs[:, 0])
    far = jnp.take(kpoint_slot, kpairs[:, 1])
    rows, conduct, conduct_next, near, far = lax.optimization_barrier((rows, conduct, conduct_next, near, far))

    here = here.reshape(1)
    swap = [(i, i ^ 1) for i in range(ka)]
    fold = [(i, ka - 1 - i) for i in range(ka)]
    cut = pair_dev // 2
    first = pair_kernels(0, cut, target, here, rows, blocks, conduct, conduct_next)
    second = pair_kernels(cut, pair_dev - cut, target, here, rows, blocks, conduct, conduct_next)
    first = first + lax.ppermute(first, "ka", swap)
    second = second + lax.ppermute(second, "ka", fold)
    first = first + lax.ppermute(first, "ka", fold)
    second = second + lax.ppermute(second, "ka", swap)

    summed = contributions(near, far, first, second, trials)
    parts = lax.all_to_all(summed, "pb", split_axis=0, concat_axis=0, tiled=True)
    response = jnp.sum(parts, axis=0).reshape(local_trials, VB, CD)[:, :, :CB]
    return response.reshape(1, -1)


def solution(mesh):
    return jax.shard_map(
        local,
        mesh=mesh,
        in_specs=(
            P("pb", "ka", None),
            P("pb", None, "ka"),
            P("pb", None, None),
            P("pb", None),
            P("pb", None),
            P(),
            P("pb", "ka"),
        ),
        out_specs=P("pb", "ka"),
        check_vma=False,
    )
```

time: 415 us -> 320 us (0.77)
  waiting for transfers between devices: 251 us -> 195 us
  Pallas kernels: 74.3 us -> 43.3 us
  starting transfers between devices: 12.8 us -> 7.83 us
    ppermute x2 -> x4, waiting for transfers between devices: 0.01 us -> 122 us  [the longest x3 109 us: local(): rows.append(lax.ppermute(rows[-1], 'ka', ahead))]
    all_gather x3 -> x1, waiting for transfers between devices: 143 us -> 39.5 us  [local(): blocks = lax.all_gather(jnp.concatenate(pieces, axis=1), 'pb')]
    all_to_all x1 -> x0, waiting for transfers between devices: 67.5 us -> none  [local(): rows = lax.all_to_all(spread, 'ka', split_axis=0, concat_axis=0, tiled=True)]
    pallas_call x4 -> x2, Pallas kernels: 66.3 us -> 35.4 us  [pair_kernels(): pl.pallas_call(pair_body, out_shape=jax.ShapeDtypeStruct((count, VB * CB,...]
    ppermute x1, waiting for transfers between devices: 14.8 us -> 0.01 us  [local(): first = first + lax.ppermute(first, 'ka', swap)]
    ppermute x1, waiting for transfers between devices: 14.1 us -> 0.52 us  [local(): second = second + lax.ppermute(second, 'ka', swap)]
    ppermute x1, waiting for transfers between devices: 2.83 us -> 16.4 us  [local(): second = second + lax.ppermute(second, 'ka', fold)]
    ppermute x1, waiting for transfers between devices: 1.43 us -> 14.6 us  [local(): first = first + lax.ppermute(first, 'ka', fold)]
  transfers between devices with their start and end apart: 11 -> 10, of which waited for: 9 -> 9; matrix products, arithmetic and copies ran while one was open for 5% -> 5% of each run, Pallas kernels for 16% -> 11%
where the time goes in v3:
time: 320 us; the launch traced here: 319 us
  waiting for transfers between devices  195 us (61%)
  Pallas kernels  43.3 us (14%)
  blocking collectives  35.3 us (11%)
  local copies, waits for them, and re-layouts  16.2 us (5%)
  between operations  13.6 us (4%)
  other arithmetic  8.18 us (3%)
  starting transfers between devices  7.83 us (2%)
    ppermute x3, waiting for transfers between devices, local(): rows.append(lax.ppermute(rows[-1], 'ka', ahead))  109 us
    all_gather x1, waiting for transfers between devices, local(): blocks = lax.all_gather(jnp.concatenate(pieces, axis=1), 'pb')  39.5 us
    pallas_call x2, Pallas kernels, pair_kernels(): pl.pallas_call(pair_body, out_shape=jax.ShapeDtypeStruct((count, VB * CB,...  35.4 us
    all_to_all x1, blocking collectives, local(): lax.all_to_all(summed, 'pb', split_axis=0, concat_axis=0, tiled=True)  35.3 us
    ppermute x1, waiting for transfers between devices, local(): second = second + lax.ppermute(second, 'ka', fold)  16.4 us
    ppermute x1, waiting for transfers between devices, local(): first = first + lax.ppermute(first, 'ka', fold)  14.6 us
    ppermute x1, waiting for transfers between devices, local(): conduct_next = lax.ppermute(conduct.astype(F32), 'ka', back)  12.7 us
    pallas_call x1, Pallas kernels, contributions(): pl.pallas_call(response_body, out_shape=jax.ShapeDtypeStruct(trials.shape...  7.94 us
  transfers between devices with their start and end apart: 10, of which 9 were waited for; matrix products, arithmetic and copies ran while one was open for 5% of the time, Pallas kernels for 11%

profile of v3, /device:TPU:1, one launch (start us, length us, event | category | flops | bytes accessed | tf_op | source)
XLA Modules:
  0.0 319.0 jit_solution(7459049246851701998)
XLA Ops:
  6.5 0.0 copy-start
  6.5 0.0 all-gather.6.cloned.1.call-start
  6.5 0.9 bitcast_dynamic-update-slice_fusion.4
  7.5 0.9 bitcast_dynamic-update-slice_fusion.5
  8.3 0.9 bitcast_dynamic-update-slice_fusion.3
  9.2 0.9 bitcast_dynamic-update-slice_fusion.2
  10.2 0.9 bitcast_dynamic-update-slice_fusion.1
  11.1 0.9 bitcast_dynamic-update-slice_fusion
  12.0 0.0 copy-start.7
  12.0 0.8 copy-done.7
  12.9 0.0 all-gather.6.cloned.1.call-update
  12.9 0.0 all-gather.4.cloned.1.call-start
  13.0 3.7 %reshape.29 = bf16[26,14,14,256]{3,2,1,0:T(8,128)(2,1)S(1)} reshape(bf16[26,196,256]{2,1,0:T(8,128)(2,1)} %param.10) | data formatting | bytes 5218304 | tf_op jit(solution)/shard_map/reshape | solution.py:162
  16.6 0.5 pad.8
  17.1 0.0 copy-start.5
  17.1 0.0 copy-start.2
  17.1 0.0 copy-start.8
  17.1 0.0 copy-start.9
  17.2 3.4 %bitcast_convert_fusion = f32[26,224,256]{2,1,0:T(8,128)} fusion(bf16[26,14,16,256]{3,2,1,0:T(8,128)(2,1)S(1)} %pad.8), kind=kLoop, calls=%fused_computation.14 | loop fusion | flops 1490944 | bytes 8945664 | tf_op jit(solution)/shard_map/convert_element_type | solution.py:164
  20.5 0.2 copy-done.5
  20.7 3.6 %collective-permute-start.3 = (f32[26,224,256]{2,1,0:T(8,128)}, f32[26,224,256]{2,1,0:T(8,128)}, u32[]{:S(2)}, u32[]{:S(2)}) collective-permute-start(f32[26,224,256]{2,1,0:T(8,128)} %bitcast_convert_fusion), channel_id=1, source_target_pairs={{1,0},{2,1},{3,2},{0,3},{5,4},{6,5},{7,6},{4,7},{9,8},{10,9},{11,1... | collective-permute-start | bytes 17891336 | tf_op jit(solution)/shard_map/ppermute | solution.py:164
  24.3 0.0 copy-done.2
  24.3 0.0 collective-permute-start
  24.3 39.0 %collective-permute-done.refs_1_.refs_5_.refs_9_ = f32[26,16,1024]{2,1,0:T(8,128)S(1)} collective-permute-done((f32[26,16,1024]{2,1,0:T(8,128)S(1)}, f32[26,16,1024]{2,1,0:T(8,128)S(1)}, u32[]{:S(2)}, u32[]{:S(2)}) %collective-permute-start) | collective-permute-done | bytes 1703968 | tf_op jit(solution)/shard_map/ppermute | solution.py:167
  63.3 0.0 collective-permute-start.1
  63.3 38.3 %collective-permute-done.1.refs_2_.refs_6_.refs_10_ = f32[26,16,1024]{2,1,0:T(8,128)S(1)} collective-permute-done((f32[26,16,1024]{2,1,0:T(8,128)S(1)}, f32[26,16,1024]{2,1,0:T(8,128)S(1)}, u32[]{:S(2)}, u32[]{:S(2)}) %collective-permute-start.1) | collective-permute-done | bytes 1703968 | tf_op jit(solution)/shard_map/ppermute | solution.py:167
  101.6 0.0 collective-permute-start.2
  101.6 0.0 copy-done.8
  101.6 0.7 reduce
  102.3 0.9 reshape.32
  103.2 0.7 copy.15
  103.9 0.8 pad.9.clone
  104.8 0.7 copy.12
  105.4 0.0 all-gather.4.cloned.1.call-update
  105.5 0.0 copy-done.9
  105.5 0.7 gather_fusion.1
  106.2 0.7 gather_fusion
  106.9 0.6 and_select_fusion
  107.5 31.6 %collective-permute-done.2.refs_3_.refs_7_.refs_11_ = f32[26,16,1024]{2,1,0:T(8,128)} collective-permute-done((f32[26,16,1024]{2,1,0:T(8,128)S(1)}, f32[26,16,1024]{2,1,0:T(8,128)}, u32[]{:S(2)}, u32[]{:S(2)}) %collective-permute-start.2) | collective-permute-done | bytes 1703968 | tf_op jit(solution)/shard_map/ppermute | solution.py:167
  139.1 12.7 %collective-permute-done.3.refs_14_ = f32[26,224,256]{2,1,0:T(8,128)} collective-permute-done((f32[26,224,256]{2,1,0:T(8,128)}, f32[26,224,256]{2,1,0:T(8,128)}, u32[]{:S(2)}, u32[]{:S(2)}) %collective-permute-start.3) | collective-permute-done | bytes 5963808 | tf_op jit(solution)/shard_map/ppermute | solution.py:164
  151.8 39.5 %all-gather.6.cloned.1.call-done = f32[8192,1408]{1,0:T(8,128)} async-done(((f32[128,1408]{1,0:T(8,128)}), f32[8192,1408]{1,0:T(8,128)}) %all-gather.6.cloned.1.call-update) | async-done | bytes 46137360 | tf_op jit(solution)/shard_map/all_gather | solution.py:154
  191.3 0.0 copy-done.4
  191.3 17.6 %shard_map.73 = f32[13,112,128]{2,1,0:T(8,128)} custom-call(s32[26]{0:T(128)} %bitcast.34, s32[1]{0:T(128)} %bitcast.4.ka_ref, f32[26,16,1024]{2,1,0:T(8,128)} %refs_8_.1, f32[26,16,1024]{2,1,0:T(8,128)} %copy-done.3, f32[26,16,1024]{2,1,0:T(8,128)} %copy-done.4, f32[26,16,1024]{2,1,0:T(8,128)} %collective-permute-done.2.refs_3_.refs_7_.refs_11_, ...), custom_call_target="tpu_custom_call" | custom-call | flops 1308622848 | bytes 10223616 | tf_op jit(solution)/shard_map/pallas_call | solution.py:92
  208.9 1.3 collective-permute-start.4
  210.2 17.8 %shard_map.74 = f32[13,112,128]{2,1,0:T(8,128)} custom-call(s32[26]{0:T(128)} %bitcast.35, s32[1]{0:T(128)} %bitcast.4.ka_ref, f32[26,16,1024]{2,1,0:T(8,128)} %refs_8_.1, f32[26,16,1024]{2,1,0:T(8,128)} %copy-done.3, f32[26,16,1024]{2,1,0:T(8,128)} %copy-done.4, f32[26,16,1024]{2,1,0:T(8,128)} %collective-permute-done.2.refs_3_.refs_7_.refs_11_, ...), custom_call_target="tpu_custom_call" | custom-call | flops 1308622848 | bytes 10223616 | tf_op jit(solution)/shard_map/pallas_call | solution.py:92
  228.0 1.9 collective-permute-start.6
  229.9 0.0 collective-permute-done.4
  229.9 0.0 copy-done.6
  229.9 0.1 add.76
  230.0 1.0 collective-permute-start.5
  231.0 16.4 %collective-permute-done.6 = f32[13,112,128]{2,1,0:T(8,128)S(1)} collective-permute-done((f32[13,112,128]{2,1,0:T(8,128)}, f32[13,112,128]{2,1,0:T(8,128)S(1)}, u32[]{:S(2)}, u32[]{:S(2)}) %collective-permute-start.6) | collective-permute-done | bytes 745504 | tf_op jit(solution)/shard_map/ppermute | solution.py:179
  247.4 1.3 add.78
  248.6 0.1 collective-permute-start.7
  248.7 14.6 %collective-permute-done.5 = f32[13,112,128]{2,1,0:T(8,128)S(1)} collective-permute-done((f32[13,112,128]{2,1,0:T(8,128)S(1)}, f32[13,112,128]{2,1,0:T(8,128)S(1)}, u32[]{:S(2)}, u32[]{:S(2)}) %collective-permute-start.5) | collective-permute-done | bytes 745504 | tf_op jit(solution)/shard_map/ppermute | solution.py:180
  263.3 1.0 add.77.first_ref
  264.3 0.5 collective-permute-done.7
  264.8 1.0 add.79.second_ref
  265.9 2.0 all-gather.4.cloned.1.call-done.trial_ref
  267.9 7.9 %shard_map.75 = f32[64,32,128]{2,1,0:T(8,128)} custom-call(s32[26]{0:T(128)} %get-tuple-element.14.near_ref, s32[26]{0:T(128)} %get-tuple-element.15.far_ref, f32[13,112,128]{2,1,0:T(8,128)} %add.77.first_ref, f32[13,112,128]{2,1,0:T(8,128)} %add.79.second_ref, f32[64,32,128]{2,1,0:T(8,128)} %all-gather.4.cloned.1.call-done.trial_ref), custom_call_target="tpu_custom_call" | custom-call | flops 143130624 | bytes 3588096 | tf_op jit(solution)/shard_map/pallas_call | solution.py:128
  275.8 35.3 %all_to_all.5 = f32[64,32,128]{2,1,0:T(8,128)S(1)} all-to-all(f32[64,32,128]{2,1,0:T(8,128)} %shard_map.75), channel_id=1, replica_groups=mesh['pb'=64,'ka'=4] {'pb'}, dimensions={0} | all-to-all | bytes 2097152 | tf_op jit(solution)/shard_map/all_to_all | solution.py:184
  311.1 0.1 reduce_sum.9
  311.2 0.1 copy.13
  311.3 0.1 copy.14
  311.4 0.8 reshape.34
  (9 shorter events, 0.0 us)
Async XLA Ops:
  6.5 99.0 %copy-start = (s32[64]{0:T(128)S(1)}, s32[64]{0:T(128)}, u32[]{:S(2)}) copy-start(s32[64]{0:T(128)} %param.14) | copy-start | bytes 772
  6.5 184.7 %all-gather.6.cloned.1.call-start = ((), (), s32[]{:S(2)}) async-start(), calls=%async_computation.2 | async-start | bytes 46858240 | tf_op jit(solution)/shard_map/all_gather | solution.py:154
  12.0 0.9 copy-start.7
  12.9 255.0 %all-gather.4.cloned.1.call-start = ((), (), s32[]{:S(2)}) async-start(), calls=%async_computation.1 | async-start | bytes 1064960 | tf_op jit(solution)/shard_map/all_gather | solution.py:159
  17.1 3.6 %copy-start.5 = (bf16[26,14,16,256]{3,2,1,0:T(8,128)(2,1)}, bf16[26,14,16,256]{3,2,1,0:T(8,128)(2,1)S(1)}, u32[]{:S(2)}) copy-start(bf16[26,14,16,256]{3,2,1,0:T(8,128)(2,1)S(1)} %pad.8) | copy-start | bytes 8945668
  17.1 7.2 %copy-start.2 = (f32[26,16,1024]{2,1,0:T(8,128)S(1)}, f32[26,16,1024]{2,1,0:T(8,128)}, u32[]{:S(2)}) copy-start(f32[26,16,1024]{2,1,0:T(8,128)} %refs_8_.1) | copy-start | bytes 5111812
  17.1 84.5 %copy-start.8 = (f32[1,3584]{1,0:T(1,128)S(1)}, f32[1,3584]{1,0:T(1,128)}, u32[]{:S(2)}) copy-start(f32[1,3584]{1,0:T(1,128)} %param.15) | copy-start | bytes 43012
  17.1 88.3 %copy-start.9 = (s32[26,2]{0,1:T(2,128)S(1)}, s32[26,2]{0,1:T(2,128)}, u32[]{:S(2)}) copy-start(s32[26,2]{0,1:T(2,128)} %param.13) | copy-start | bytes 628
  20.7 131.0 %collective-permute-start.3 = (f32[26,224,256]{2,1,0:T(8,128)}, f32[26,224,256]{2,1,0:T(8,128)}, u32[]{:S(2)}, u32[]{:S(2)}) collective-permute-start(f32[26,224,256]{2,1,0:T(8,128)} %bitcast_convert_fusion), channel_id=1, source_target_pairs={{1,0},{2,1},{3,2},{0,3},{5,4},{6,5},{7,6},{4,7},{9,8},{10,9},{11,1... | collective-permute-start | bytes 17891336 | tf_op jit(solution)/shard_map/ppermute | solution.py:164
  24.3 39.0 %collective-permute-start = (f32[26,16,1024]{2,1,0:T(8,128)S(1)}, f32[26,16,1024]{2,1,0:T(8,128)S(1)}, u32[]{:S(2)}, u32[]{:S(2)}) collective-permute-start(f32[26,16,1024]{2,1,0:T(8,128)S(1)} %copy-done.2), channel_id=1, source_target_pairs={{0,1},{1,2},{2,3},{3,0},{4,5},{5,6},{6,7},{7,4},{8,9},{9,10},{10,1... | collective-permute-start | bytes 5111816 | tf_op jit(solution)/shard_map/ppermute | solution.py:167
  63.3 128.0 %copy-start.3 = (f32[26,16,1024]{2,1,0:T(8,128)}, f32[26,16,1024]{2,1,0:T(8,128)S(1)}, u32[]{:S(2)}) copy-start(f32[26,16,1024]{2,1,0:T(8,128)S(1)} %collective-permute-done.refs_1_.refs_5_.refs_9_) | copy-start | bytes 5111812
  63.3 38.3 %collective-permute-start.1 = (f32[26,16,1024]{2,1,0:T(8,128)S(1)}, f32[26,16,1024]{2,1,0:T(8,128)S(1)}, u32[]{:S(2)}, u32[]{:S(2)}) collective-permute-start(f32[26,16,1024]{2,1,0:T(8,128)S(1)} %collective-permute-done.refs_1_.refs_5_.refs_9_), channel_id=1, source_target_pairs={{0,1},{1,2},{2,3},{3,0},{4,5},{5,6},{6,7},{7,4},{8,9},{9,10},{10,1... | collective-permute-start | bytes 5111816 | tf_op jit(solution)/shard_map/ppermute | solution.py:167
  101.6 89.7 %copy-start.4 = (f32[26,16,1024]{2,1,0:T(8,128)}, f32[26,16,1024]{2,1,0:T(8,128)S(1)}, u32[]{:S(2)}) copy-start(f32[26,16,1024]{2,1,0:T(8,128)S(1)} %collective-permute-done.1.refs_2_.refs_6_.refs_10_) | copy-start | bytes 5111812
  101.6 37.5 %collective-permute-start.2 = (f32[26,16,1024]{2,1,0:T(8,128)S(1)}, f32[26,16,1024]{2,1,0:T(8,128)}, u32[]{:S(2)}, u32[]{:S(2)}) collective-permute-start(f32[26,16,1024]{2,1,0:T(8,128)S(1)} %collective-permute-done.1.refs_2_.refs_6_.refs_10_), channel_id=1, source_target_pairs={{0,1},{1,2},{2,3},{3,0},{4,5},{5,6},{6,7},{7,4},{8,9},{9,10},{10,1... | collective-permute-start | bytes 5111816 | tf_op jit(solution)/shard_map/ppermute | solution.py:167
  208.9 21.0 %copy-start.6 = (f32[13,112,128]{2,1,0:T(8,128)S(1)}, f32[13,112,128]{2,1,0:T(8,128)}, u32[]{:S(2)}) copy-start(f32[13,112,128]{2,1,0:T(8,128)} %shard_map.73) | copy-start | bytes 2236420
  208.9 21.0 %collective-permute-start.4 = (f32[13,112,128]{2,1,0:T(8,128)}, f32[13,112,128]{2,1,0:T(8,128)S(1)}, u32[]{:S(2)}, u32[]{:S(2)}) collective-permute-start(f32[13,112,128]{2,1,0:T(8,128)} %shard_map.73), channel_id=1, source_target_pairs={{0,1},{1,0},{2,3},{3,2},{4,5},{5,4},{6,7},{7,6},{8,9},{9,8},{10,11... | collective-permute-start | bytes 2236424 | tf_op jit(solution)/shard_map/ppermute | solution.py:178
  228.0 19.4 %collective-permute-start.6 = (f32[13,112,128]{2,1,0:T(8,128)}, f32[13,112,128]{2,1,0:T(8,128)S(1)}, u32[]{:S(2)}, u32[]{:S(2)}) collective-permute-start(f32[13,112,128]{2,1,0:T(8,128)} %shard_map.74), channel_id=1, source_target_pairs={{0,3},{1,2},{2,1},{3,0},{4,7},{5,6},{6,5},{7,4},{8,11},{9,10},{10,... | collective-permute-start | bytes 2236424 | tf_op jit(solution)/shard_map/ppermute | solution.py:179
  230.0 33.3 %collective-permute-start.5 = (f32[13,112,128]{2,1,0:T(8,128)S(1)}, f32[13,112,128]{2,1,0:T(8,128)S(1)}, u32[]{:S(2)}, u32[]{:S(2)}) collective-permute-start(f32[13,112,128]{2,1,0:T(8,128)S(1)} %add.76), channel_id=1, source_target_pairs={{0,3},{1,2},{2,1},{3,0},{4,7},{5,6},{6,5},{7,4},{8,11},{9,10},{10,... | collective-permute-start | bytes 2236424 | tf_op jit(solution)/shard_map/ppermute | solution.py:180
  248.6 16.2 %collective-permute-start.7 = (f32[13,112,128]{2,1,0:T(8,128)S(1)}, f32[13,112,128]{2,1,0:T(8,128)S(1)}, u32[]{:S(2)}, u32[]{:S(2)}) collective-permute-start(f32[13,112,128]{2,1,0:T(8,128)S(1)} %add.78), channel_id=1, source_target_pairs={{0,1},{1,0},{2,3},{3,2},{4,5},{5,4},{6,7},{7,6},{8,9},{9,8},{10,11... | collective-permute-start | bytes 2236424 | tf_op jit(solution)/shard_map/ppermute | solution.py:181
  263.3 48.9 %copy-start.1 = (s32[64]{0:T(128)S(1)}, s32[64]{0:T(128)}, u32[]{:S(2)}) copy-start(s32[64]{0:T(128)} %param.14) | copy-start | bytes 772
Sparse Core Ops, SparseCore 0:
  13.0 178.2 all-gather.5
  194.1 73.7 all-gather.3

commit v4 on v3

v4 whole, which is shorter than its diff:
```python
import jax
import jax.numpy as jnp
import numpy as np
from jax import lax
from jax.experimental import pallas as pl
from jax.experimental.pallas import tpu as pltpu
from jax.sharding import PartitionSpec as P

VB = 8
CB = 14
CD = 16
VC = VB * CD
PAIR = 2
F32 = jnp.float32
BF16 = jnp.bfloat16
PLAIN = ((1,), (0,))
TURNED = ((1,), (1,))


def split(x):
    high = x.astype(BF16)
    return high, (x - high.astype(F32)).astype(BF16)


def mul(a, b, dims):
    return lax.dot_general(a, b, (dims, ((), ())), preferred_element_type=F32)


def mul3(a, b, dims=PLAIN):
    rows = a.shape[0]
    a_high, a_low = split(a)
    b_high, b_low = split(b)
    both = mul(jnp.concatenate([a_high, a_low], axis=0), b_high, dims)
    return both[:rows] + both[rows:] + mul(a_high, b_low, dims)


def quads(x, half):
    return [x[i : i + half, j : j + half] for i in (0, half) for j in (0, half)]


def pack_body(ka_ref, trial_ref, spread_ref, own_ref, beside_ref, across_ref, out_ref):
    trials = trial_ref.shape[0]
    half = own_ref.shape[1] // 2
    out_ref[:trials, :] = jnp.dot(trial_ref[...], spread_ref[...], precision=lax.Precision.HIGHEST, preferred_element_type=F32)
    row = lax.broadcasted_iota(jnp.int32, (half, half), 0)
    column = lax.broadcasted_iota(jnp.int32, (half, half), 1)
    a, b, _, d = quads(own_ref[0], half)
    squares = [jnp.where(row <= column, a, d), b] + quads(beside_ref[0], half) + quads(across_ref[0], half)
    for i, square in enumerate(squares):
        start = trials + i * half
        out_ref[start : start + half, :] = square
    line = jnp.sum(jnp.where(row == column, d, 0.0), axis=0, keepdims=True)
    start = trials + len(squares) * half
    out_ref[start:, :] = jnp.broadcast_to(line, (out_ref.shape[0] - start, half))


def pack(ka, trials, spread, screened, parts):
    own = screened.shape[1] // parts
    half = own // 2

    def block(i):
        return pl.BlockSpec((1, own, own), lambda g, y: (0, (y[0] + i) % parts, y[0]))

    rows = trials.shape[0] + 10 * half + 8
    return pl.pallas_call(
        pack_body,
        out_shape=jax.ShapeDtypeStruct((rows, half), F32),
        grid_spec=pltpu.PrefetchScalarGridSpec(
            num_scalar_prefetch=1,
            grid=(1,),
            in_specs=[
                pl.BlockSpec(trials.shape, lambda g, y: (0, 0)),
                pl.BlockSpec(spread.shape, lambda g, y: (0, 0)),
                block(0),
                block(1),
                block(2),
            ],
            out_specs=pl.BlockSpec((rows, half), lambda g, y: (0, 0)),
        ),
    )(ka, trials, spread, screened, screened, screened)


def prepare_body(ka_ref, *refs):
    parts = len(refs) // 3 - 1
    conduct_ref, conduct_next_ref, rows_ref, joined_ref = refs[3 * parts :]
    each, width = refs[0].shape[1:]
    for i in range(3):
        for k in range(parts):
            place = pl.multiple_of(lax.rem(ka_ref[0] + parts - k, parts) * each, each)
            high, low = split(refs[i * parts + k][0])
            rows_ref[0, pl.ds(place, each), i * width : (i + 1) * width] = high
            rows_ref[0, pl.ds(parts * each + place, each), i * width : (i + 1) * width] = low
    joined_ref[0, :, :width] = conduct_ref[0]
    joined_ref[0, :, width:] = conduct_next_ref[0].astype(BF16)


def prepare(ka, valence, conduction, conduction_next):
    pairs, rows, waves = valence[0].shape
    parts = len(valence)
    own = waves // parts
    columns = conduction.shape[1]

    def column(i):
        return pl.BlockSpec((1, rows, own), lambda p, y: (p, 0, (y[0] + i) % parts))

    conduct = pl.BlockSpec((1, columns, own), lambda p, y: (p, 0, 0))
    shapes = (pairs, 2 * parts * rows, 3 * own), (pairs, columns, 2 * own)
    return pl.pallas_call(
        prepare_body,
        out_shape=tuple(jax.ShapeDtypeStruct(shape, BF16) for shape in shapes),
        grid_spec=pltpu.PrefetchScalarGridSpec(
            num_scalar_prefetch=1,
            grid=(pairs,),
            in_specs=[column(i) for i in range(3) for _ in range(parts)] + [conduct, conduct],
            out_specs=tuple(pl.BlockSpec((1,) + shape[1:], lambda p, y: (p, 0, 0)) for shape in shapes),
        ),
        cost_estimate=pl.CostEstimate(flops=0, bytes_accessed=pairs * rows * waves * 40, transcendentals=0),
    )(ka, *(valence * 3), conduction, conduction_next)


def one_pair(rows, blocks, conduct, out_ref, number, low_ref, high_ref, skip):
    half = blocks.shape[1]
    width = 2 * half
    count = rows.shape[0] // 2
    squares = [blocks[skip + i * half : skip + (i + 1) * half] for i in range(10)]
    line = blocks[skip + 10 * half : skip + 10 * half + 1]
    row = lax.broadcasted_iota(jnp.int32, (half, half), 0)
    column = lax.broadcasted_iota(jnp.int32, (half, half), 1)
    shared, corner = squares[:2]
    turned = shared.T
    a = jnp.where(row <= column, shared, turned)
    d = jnp.where(row > column, shared, jnp.where(row == column, line, turned))
    left = jnp.concatenate([a, corner.T, squares[2], squares[4], squares[6], squares[8]], axis=0)
    right = jnp.concatenate([corner, d, squares[3], squares[5], squares[7], squares[9]], axis=0)
    high, low = split(jnp.concatenate([left, right], axis=1))
    both = mul(rows, high, PLAIN)
    here = both[:count] + both[count:] + mul(rows[:count], low, PLAIN)
    both = mul(rows[:, :width], high[width : 2 * width], TURNED)
    there = both[:count] + both[count:] + mul(rows[:count, :width], low[width : 2 * width], TURNED)
    high, low = split(jnp.concatenate([here, there], axis=1))
    both = mul(jnp.concatenate([high, low], axis=0), conduct, TURNED)
    kernel = both[:count] + both[count:]
    low_ref[...] = kernel[:, :VC]
    high_ref[...] = jnp.concatenate([kernel[:, VC:], jnp.zeros((count, 2 * VC - kernel.shape[1]), F32)], axis=1)
    group = lax.broadcasted_iota(jnp.int32, (VB, VC), 1) // CD
    for part, ref in enumerate((low_ref, high_ref)):
        tiles = [ref[pl.ds(w, VB, stride=VB), :] for w in range(VB)]
        for step in (4, 2, 1):
            upper = (group & step) != 0
            for i in range(VB):
                if i & step:
                    continue
                a, b = tiles[i], tiles[i + step]
                tiles[i] = jnp.where(upper, pltpu.roll(b, step * CD, axis=1), a)
                tiles[i + step] = jnp.where(upper, b, pltpu.roll(a, VC - step * CD, axis=1))
        for i in range(VB):
            c = part * VB + i
            if c < CB:
                out_ref[number, c * VB : (c + 1) * VB, :] = tiles[i]


def pair_body(skip, momentum_ref, rows_ref, *refs):
    blocks, (conduct_ref, out_ref), scratch = refs[:PAIR], refs[PAIR : PAIR + 2], refs[PAIR + 2 :]
    for i in range(PAIR):
        one_pair(rows_ref[i], blocks[i][0], conduct_ref[i], out_ref, i, scratch[2 * i], scratch[2 * i + 1], skip)


def pair_kernels(start, count, momentum, rows, blocks, conduct, skip):
    first = start // PAIR

    def block(i):
        return pl.BlockSpec((1,) + blocks.shape[1:], lambda p, q: (q[start + PAIR * p + i], 0, 0))

    return pl.pallas_call(
        lambda *refs: pair_body(skip, *refs),
        out_shape=jax.ShapeDtypeStruct((count, VB * CB, VC), F32),
        grid_spec=pltpu.PrefetchScalarGridSpec(
            num_scalar_prefetch=1,
            grid=(count // PAIR,),
            in_specs=[pl.BlockSpec((PAIR,) + rows.shape[1:], lambda p, q: (first + p, 0, 0))]
            + [block(i) for i in range(PAIR)]
            + [pl.BlockSpec((PAIR,) + conduct.shape[1:], lambda p, q: (first + p, 0, 0))],
            out_specs=pl.BlockSpec((PAIR, VB * CB, VC), lambda p, q: (p, 0, 0)),
            scratch_shapes=[pltpu.VMEM((VB * VB, VC), F32)] * (2 * PAIR),
        ),
        cost_estimate=pl.CostEstimate(flops=count * 10**8, bytes_accessed=count * 11 * 10**5, transcendentals=0),
    )(momentum, rows, *([blocks] * PAIR), conduct)


def response_body(start, counts, near_ref, far_ref, trial_ref, *refs):
    kernels, (out_ref, turn_ref) = refs[: len(counts)], refs[-2:]
    if len(refs) > len(counts) + 2:
        out_ref[...] = refs[len(counts)][...]
    else:
        out_ref[...] = jnp.zeros_like(out_ref)
    turn_ref[...] = jnp.zeros_like(turn_ref)
    for count, kernel_ref in zip(counts, kernels):

        @pl.loop(0, count)
        def _(p, start=start, kernel_ref=kernel_ref):
            near, far = near_ref[start + p], far_ref[start + p]
            for v in range(VB):
                turn_ref[v * CD : v * CD + CB, :] = kernel_ref[p, pl.ds(v, CB, stride=VB), :]
            kernel = turn_ref[...]
            direct = mul3(trial_ref[far], kernel, TURNED)
            mirror = mul3(trial_ref[near], kernel, PLAIN)
            out_ref[near] = out_ref[near] + direct
            out_ref[far] = out_ref[far] + mirror

        start += count


def contributions(start, near, far, blocks, trials, kernels, before=()):
    counts = [kernel.shape[0] for kernel in kernels]
    shape = (blocks.shape[0], trials, VC)
    whole = [pl.BlockSpec(x.shape, lambda g: (0, 0, 0)) for x in kernels]
    result = pl.BlockSpec(shape, lambda g: (0, 0, 0))
    scalar = pl.BlockSpec(memory_space=pltpu.SMEM)
    return pl.pallas_call(
        lambda *refs: response_body(start, counts, *refs),
        out_shape=jax.ShapeDtypeStruct(shape, F32),
        grid=(1,),
        in_specs=[scalar, scalar, result, *whole] + [result] * len(before),
        out_specs=result,
        scratch_shapes=[pltpu.VMEM((VC, VC), F32)],
        cost_estimate=pl.CostEstimate(flops=sum(counts) * 10**7, bytes_accessed=4 * 10**6, transcendentals=0),
    )(near, far, blocks, *kernels, *before)


def local(valence, conduction, screened, momentum, kpairs, kpoint_slot, trial_blocks):
    ka = lax.axis_size("ka")
    pair_dev = valence.shape[0]
    own = conduction.shape[2]
    here = lax.axis_index("ka").astype(jnp.int32).reshape(1)
    own_trials = trial_blocks.reshape(-1, VB * CB)
    local_trials = own_trials.shape[0]
    entry = np.arange(VB * CB)
    spread = np.zeros((VB * CB, VC), np.float32)
    spread[entry, entry // CB * CD + entry % CB] = 1.0
    blocks = lax.all_gather(pack(here, own_trials, jnp.asarray(spread), screened, ka), "pb")

    ahead = [(i, (i + 1) % ka) for i in range(ka)]
    back = [((i + 1) % ka, i) for i in range(ka)]
    conduct = conduction.reshape(pair_dev, CB, CB, own)
    conduct = jnp.pad(conduct, ((0, 0), (0, 0), (0, CD - CB), (0, 0))).reshape(pair_dev, CB * CD, own)
    conduct_next = lax.ppermute(conduct.astype(F32), "ka", back)
    rows = [valence]
    for _ in range(ka - 1):
        rows.append(lax.ppermute(rows[-1], "ka", ahead))
    near = jnp.take(kpoint_slot, kpairs[:, 0])
    far = jnp.take(kpoint_slot, kpairs[:, 1])
    rows, conduct = prepare(here, rows, conduct, conduct_next)
    rows, conduct, near, far = lax.optimization_barrier((rows, conduct, near, far))

    swap = [(i, i ^ 1) for i in range(ka)]
    fold = [(i, ka - 1 - i) for i in range(ka)]
    target = momentum[:, 0]
    each = max(PAIR, pair_dev // 4 // PAIR * PAIR)
    sizes = [pair_dev - 3 * each, each, each, each]
    kernels, start = [], 0
    for size in sizes:
        kernels.append(pair_kernels(start, size, target, rows, blocks, conduct, local_trials))
        start += size
    turns = (swap, fold)
    kernels = [x + lax.ppermute(x, "ka", turns[i % 2]) for i, x in enumerate(kernels)]
    kernels = [x + lax.ppermute(x, "ka", turns[1 - i % 2]) for i, x in enumerate(kernels)]

    summed = contributions(0, near, far, blocks, local_trials, kernels[:2])
    summed = contributions(sum(sizes[:2]), near, far, blocks, local_trials, kernels[2:], (summed,))
    parts = lax.all_to_all(summed, "pb", split_axis=0, concat_axis=0, tiled=True)
    response = jnp.sum(parts, axis=0).reshape(local_trials, VB, CD)[:, :, :CB]
    return response.reshape(1, -1)


def solution(mesh):
    return jax.shard_map(
        local,
        mesh=mesh,
        in_specs=(
            P("pb", "ka", None),
            P("pb", None, "ka"),
            P("pb", None, None),
            P("pb", None),
            P("pb", None),
            P(),
            P("pb", "ka"),
        ),
        out_specs=P("pb", "ka"),
        check_vma=False,
    )
```

time: 320 us -> 300 us (0.938)
  waiting for transfers between devices: 195 us -> 161 us
  Pallas kernels: 43.3 us -> 62.1 us
  local copies, waits for them, and re-layouts: 16.2 us -> 7.37 us
  starting transfers between devices: 7.83 us -> 11.1 us
    all_gather x2 -> x1, waiting for transfers between devices: 41.5 us -> 12 us  [local(): lax.all_gather(pack(here, own_trials, jnp.asarray(spread), screened, ka),...]
    pallas_call x3 -> x8, Pallas kernels: 43.3 us -> 62.1 us  [the longest x4 29.3 us: pair_kernels(): pl.pallas_call(lambda *refs: pair_body(skip, *refs), out_shape=jax.ShapeD...]
    ppermute x4 -> x8, waiting for transfers between devices: 31.5 us -> 23.4 us  [the longest x4 17.1 us: local(): lax.ppermute(x, 'ka', turns[1 - i % 2])]
    unnamed x26 -> x22, local copies, waits for them, and re-layouts: 6.39 us -> 0.18 us
    ppermute x3, waiting for transfers between devices: 109 us -> 113 us  [local(): rows.append(lax.ppermute(rows[-1], 'ka', ahead))]
    ppermute x4 -> x8, starting transfers between devices: 4.23 us -> 7.57 us  [the longest x4 4.36 us: local(): lax.ppermute(x, 'ka', turns[i % 2])]
  transfers between devices with their start and end apart: 10 -> 13, of which waited for: 9 -> 7; matrix products, arithmetic and copies ran while one was open for 5% -> 4% of each run, Pallas kernels for 11% -> 14%
where the time goes in v4:
time: 300 us; the launch traced here: 299 us
  waiting for transfers between devices  161 us (54%)
  Pallas kernels  62.1 us (21%)
  blocking collectives  36.1 us (12%)
  between operations  13.5 us (4%)
  starting transfers between devices  11.1 us (4%)
  other arithmetic  8.19 us (3%)
  local copies, waits for them, and re-layouts  7.37 us (2%)
    ppermute x3, waiting for transfers between devices, local(): rows.append(lax.ppermute(rows[-1], 'ka', ahead))  113 us
    all_to_all x1, blocking collectives, local(): lax.all_to_all(summed, 'pb', split_axis=0, concat_axis=0, tiled=True)  36.1 us
    pallas_call x4, Pallas kernels, pair_kernels(): pl.pallas_call(lambda *refs: pair_body(skip, *refs), out_shape=jax.ShapeD...  29.3 us
    pallas_call x1, Pallas kernels, prepare(): pl.pallas_call(prepare_body, out_shape=tuple((jax.ShapeDtypeStruct(shape,...  20.1 us
    ppermute x4, waiting for transfers between devices, local(): lax.ppermute(x, 'ka', turns[1 - i % 2])  17.1 us
    ppermute x1, waiting for transfers between devices, local(): conduct_next = lax.ppermute(conduct.astype(F32), 'ka', back)  12.4 us
    all_gather x1, waiting for transfers between devices, local(): lax.all_gather(pack(here, own_trials, jnp.asarray(spread), screened, ka),...  12 us
    pallas_call x2, Pallas kernels, contributions(): pl.pallas_call(lambda *refs: response_body(start, counts, *refs), out_sha...  10.5 us
  transfers between devices with their start and end apart: 13, of which 7 were waited for; matrix products, arithmetic and copies ran while one was open for 4% of the time, Pallas kernels for 14%

profile of v4, /device:TPU:1, one launch (start us, length us, event | category | flops | bytes accessed | tf_op | source)
XLA Modules:
  0.0 299.2 jit_solution(745548213536175763)
XLA Ops:
  6.5 0.0 copy-start
  6.5 0.0 all-gather.3.cloned.1.call-start
  6.5 0.8 reduce
  7.3 0.7 reshape.26.trial_ref
  8.0 2.2 shard_map.83
  10.2 0.0 all-gather.3.cloned.1.call-update
  10.2 3.7 %reshape.24 = bf16[26,14,14,256]{3,2,1,0:T(8,128)(2,1)S(1)} reshape(bf16[26,196,256]{2,1,0:T(8,128)(2,1)} %param.11) | data formatting | bytes 5218304 | tf_op jit(solution)/shard_map/reshape | solution.py:244
  13.9 0.5 pad.4
  14.3 0.0 copy-start.2
  14.3 0.0 copy-start.3
  14.4 0.0 copy-start.10
  14.4 3.4 %bitcast_convert_fusion = f32[26,224,256]{2,1,0:T(8,128)} fusion(bf16[26,14,16,256]{3,2,1,0:T(8,128)(2,1)S(1)} %pad.4), kind=kLoop, calls=%fused_computation.8 | loop fusion | flops 1490944 | bytes 8945664 | tf_op jit(solution)/shard_map/convert_element_type | solution.py:246
  17.8 0.1 copy-done.2
  17.9 3.6 %collective-permute-start.3 = (f32[26,224,256]{2,1,0:T(8,128)}, f32[26,224,256]{2,1,0:T(8,128)}, u32[]{:S(2)}, u32[]{:S(2)}) collective-permute-start(f32[26,224,256]{2,1,0:T(8,128)} %bitcast_convert_fusion), channel_id=1, source_target_pairs={{1,0},{2,1},{3,2},{0,3},{5,4},{6,5},{7,6},{4,7},{9,8},{10,9},{11,1... | collective-permute-start | bytes 17891336 | tf_op jit(solution)/shard_map/ppermute | solution.py:246
  21.5 0.0 copy-done.3
  21.5 0.0 collective-permute-start
  21.5 39.1 %collective-permute-done.refs_1_.refs_5_.refs_9_ = f32[26,16,1024]{2,1,0:T(8,128)S(1)} collective-permute-done((f32[26,16,1024]{2,1,0:T(8,128)S(1)}, f32[26,16,1024]{2,1,0:T(8,128)S(1)}, u32[]{:S(2)}, u32[]{:S(2)}) %collective-permute-start) | collective-permute-done | bytes 1703968 | tf_op jit(solution)/shard_map/ppermute | solution.py:249
  60.6 0.0 collective-permute-start.1
  60.6 38.4 %collective-permute-done.1.refs_2_.refs_6_.refs_10_ = f32[26,16,1024]{2,1,0:T(8,128)S(1)} collective-permute-done((f32[26,16,1024]{2,1,0:T(8,128)S(1)}, f32[26,16,1024]{2,1,0:T(8,128)S(1)}, u32[]{:S(2)}, u32[]{:S(2)}) %collective-permute-start.1) | collective-permute-done | bytes 1703968 | tf_op jit(solution)/shard_map/ppermute | solution.py:249
  99.0 0.0 collective-permute-start.2
  99.0 0.0 copy-done.10
  99.0 0.0 copy-done
  99.0 0.7 gather_fusion.1
  99.7 0.7 gather_fusion
  100.4 0.6 and_select_fusion
  101.0 35.6 %collective-permute-done.2.refs_3_.refs_7_.refs_11_ = f32[26,16,1024]{2,1,0:T(8,128)} collective-permute-done((f32[26,16,1024]{2,1,0:T(8,128)S(1)}, f32[26,16,1024]{2,1,0:T(8,128)}, u32[]{:S(2)}, u32[]{:S(2)}) %collective-permute-start.2) | collective-permute-done | bytes 1703968 | tf_op jit(solution)/shard_map/ppermute | solution.py:249
  136.6 12.4 %collective-permute-done.3.refs_13_ = f32[26,224,256]{2,1,0:T(8,128)} collective-permute-done((f32[26,224,256]{2,1,0:T(8,128)}, f32[26,224,256]{2,1,0:T(8,128)}, u32[]{:S(2)}, u32[]{:S(2)}) %collective-permute-start.3) | collective-permute-done | bytes 5963808 | tf_op jit(solution)/shard_map/ppermute | solution.py:246
  149.0 0.0 copy-done.4
  149.0 0.0 copy-done.5
  149.0 20.1 %shard_map.82 = (bf16[26,128,768]{2,1,0:T(8,128)(2,1)}, bf16[26,224,512]{2,1,0:T(8,128)(2,1)}) custom-call(s32[1]{0:T(128)} %bitcast.ka_ref, f32[26,16,1024]{2,1,0:T(8,128)} %refs_8_.1, f32[26,16,1024]{2,1,0:T(8,128)} %copy-done.4, f32[26,16,1024]{2,1,0:T(8,128)} %copy-done.5, f32[26,16,1024]{2,1,0:T(8,128)} %collective-permute-done.2.refs_3_.refs_7_.refs_11_, ...), custom_call_target="tpu_custom_call" | custom-call | bytes 17039360 | tf_op jit(solution)/shard_map/pallas_call | solution.py:108
  169.1 12.0 %all-gather.3.cloned.1.call-done = f32[84480,128]{1,0:T(8,128)} async-done(((f32[1320,128]{1,0:T(8,128)}), f32[84480,128]{1,0:T(8,128)}) %all-gather.3.cloned.1.call-update) | async-done | bytes 43253776 | tf_op jit(solution)/shard_map/all_gather | solution.py:240
  181.1 8.3 %shard_map.86 = f32[8,112,128]{2,1,0:T(8,128)} custom-call(s32[26]{0:T(128)} %bitcast.27, bf16[26,128,768]{2,1,0:T(8,128)(2,1)} %get-tuple-element.16.refs_1_, f32[64,1320,128]{2,1,0:T(8,128)} %bitcast.15, f32[64,1320,128]{2,1,0:T(8,128)} %bitcast.16, bf16[26,224,512]{2,1,0:T(8,128)(2,1)} %get-tuple-element.17.refs_4_), custom_call_target="tpu_custom_call" | custom-call | flops 800000000 | bytes 8800000 | tf_op jit(solution)/shard_map/pallas_call | solution.py:174
  189.4 1.2 collective-permute-start.8
  190.6 7.0 %shard_map.84 = f32[6,112,128]{2,1,0:T(8,128)} custom-call(s32[26]{0:T(128)} %bitcast.28, bf16[26,128,768]{2,1,0:T(8,128)(2,1)} %get-tuple-element.16.refs_1_, f32[64,1320,128]{2,1,0:T(8,128)} %bitcast.17, f32[64,1320,128]{2,1,0:T(8,128)} %bitcast.18, bf16[26,224,512]{2,1,0:T(8,128)(2,1)} %get-tuple-element.17.refs_4_), custom_call_target="tpu_custom_call" | custom-call | flops 600000000 | bytes 6600000 | tf_op jit(solution)/shard_map/pallas_call | solution.py:174
  197.6 0.3 collective-permute-start.4
  197.9 7.0 %shard_map.85 = f32[6,112,128]{2,1,0:T(8,128)} custom-call(s32[26]{0:T(128)} %bitcast.29, bf16[26,128,768]{2,1,0:T(8,128)(2,1)} %get-tuple-element.16.refs_1_, f32[64,1320,128]{2,1,0:T(8,128)} %bitcast.19, f32[64,1320,128]{2,1,0:T(8,128)} %bitcast.20, bf16[26,224,512]{2,1,0:T(8,128)(2,1)} %get-tuple-element.17.refs_4_), custom_call_target="tpu_custom_call" | custom-call | flops 600000000 | bytes 6600000 | tf_op jit(solution)/shard_map/pallas_call | solution.py:174
  204.9 2.5 collective-permute-start.6
  207.4 7.0 %shard_map.87 = f32[6,112,128]{2,1,0:T(8,128)} custom-call(s32[26]{0:T(128)} %bitcast.30, bf16[26,128,768]{2,1,0:T(8,128)(2,1)} %get-tuple-element.16.refs_1_, f32[64,1320,128]{2,1,0:T(8,128)} %bitcast.21, f32[64,1320,128]{2,1,0:T(8,128)} %bitcast.22, bf16[26,224,512]{2,1,0:T(8,128)(2,1)} %get-tuple-element.17.refs_4_), custom_call_target="tpu_custom_call" | custom-call | flops 600000000 | bytes 6600000 | tf_op jit(solution)/shard_map/pallas_call | solution.py:174
  214.4 0.3 collective-permute-start.10
  214.7 0.0 collective-permute-done.8
  214.7 0.0 copy-done.6
  214.8 2.4 collective-permute-start.9
  217.2 0.0 collective-permute-done.4
  217.2 0.0 copy-done.9
  217.3 0.4 collective-permute-start.5
  217.7 0.0 collective-permute-done.6
  217.7 0.3 collective-permute-start.7
  218.0 6.3 %collective-permute-done.10 = f32[6,112,128]{2,1,0:T(8,128)S(1)} collective-permute-done((f32[6,112,128]{2,1,0:T(8,128)}, f32[6,112,128]{2,1,0:T(8,128)S(1)}, u32[]{:S(2)}, u32[]{:S(2)}) %collective-permute-start.10) | collective-permute-done | bytes 344096 | tf_op jit(solution)/shard_map/ppermute | solution.py:265
  224.4 0.1 collective-permute-start.11
  224.5 17.1 %collective-permute-done.5 = f32[6,112,128]{2,1,0:T(8,128)S(1)} collective-permute-done((f32[6,112,128]{2,1,0:T(8,128)S(1)}, f32[6,112,128]{2,1,0:T(8,128)S(1)}, u32[]{:S(2)}, u32[]{:S(2)}) %collective-permute-start.5) | collective-permute-done | bytes 344096 | tf_op jit(solution)/shard_map/ppermute | solution.py:266
  241.5 0.8 add.30.refs_3_
  242.3 0.0 collective-permute-done.7
  242.3 0.8 add.32.refs_4_
  243.1 0.0 collective-permute-done.11
  243.1 0.8 add.36.refs_4_
  243.9 0.0 collective-permute-done.9
  243.9 0.8 add.34.refs_3_
  244.7 5.3 %shard_map.88.refs_5_ = f32[64,32,128]{2,1,0:T(8,128)} custom-call(s32[26]{0:T(128)} %get-tuple-element.14.refs_0_, s32[26]{0:T(128)} %get-tuple-element.15.refs_1_, f32[64,1320,128]{2,1,0:T(8,128)} %bitcast.23, f32[8,112,128]{2,1,0:T(8,128)} %add.34.refs_3_, f32[6,112,128]{2,1,0:T(8,128)} %add.36.refs_4_), custom_call_target="tpu_custom_call" | custom-call | flops 140000000 | bytes 4000000 | tf_op jit(solution)/shard_map/pallas_call | solution.py:219
  250.0 5.2 %shard_map.89 = f32[64,32,128]{2,1,0:T(8,128)} custom-call(s32[26]{0:T(128)} %get-tuple-element.14.refs_0_, s32[26]{0:T(128)} %get-tuple-element.15.refs_1_, f32[64,1320,128]{2,1,0:T(8,128)} %bitcast.24, f32[6,112,128]{2,1,0:T(8,128)} %add.30.refs_3_, f32[6,112,128]{2,1,0:T(8,128)} %add.32.refs_4_, f32[64,32,128]{2,1,0:T(8,128)} %shard_map.88.refs_5_), custom_call_target="tpu_custom_call" | custom-call | flops 120000000 | bytes 4000000 | tf_op jit(solution)/shard_map/pallas_call | solution.py:219
  255.2 36.1 %all_to_all.5 = f32[64,32,128]{2,1,0:T(8,128)S(1)} all-to-all(f32[64,32,128]{2,1,0:T(8,128)} %shard_map.89), channel_id=1, replica_groups=mesh['pb'=64,'ka'=4] {'pb'}, dimensions={0} | all-to-all | bytes 2097152 | tf_op jit(solution)/shard_map/all_to_all | solution.py:270
  291.3 0.1 reduce_sum.9
  291.4 0.1 copy.10
  291.5 0.1 copy.11
  291.6 0.8 reshape.28
  (16 shorter events, 0.2 us)
Async XLA Ops:
  6.5 92.5 %copy-start = (s32[64]{0:T(128)S(1)}, s32[64]{0:T(128)}, u32[]{:S(2)}) copy-start(s32[64]{0:T(128)} %param.15) | copy-start | bytes 772
  6.5 174.5 %all-gather.3.cloned.1.call-start = ((), (), s32[]{:S(2)}) async-start(), calls=%async_computation.1 | async-start | bytes 43929600 | tf_op jit(solution)/shard_map/all_gather | solution.py:240
  14.3 3.6 %copy-start.2 = (bf16[26,14,16,256]{3,2,1,0:T(8,128)(2,1)}, bf16[26,14,16,256]{3,2,1,0:T(8,128)(2,1)S(1)}, u32[]{:S(2)}) copy-start(bf16[26,14,16,256]{3,2,1,0:T(8,128)(2,1)S(1)} %pad.4) | copy-start | bytes 8945668
  14.3 7.2 %copy-start.3 = (f32[26,16,1024]{2,1,0:T(8,128)S(1)}, f32[26,16,1024]{2,1,0:T(8,128)}, u32[]{:S(2)}) copy-start(f32[26,16,1024]{2,1,0:T(8,128)} %refs_8_.1) | copy-start | bytes 5111812
  14.4 84.6 %copy-start.10 = (s32[26,2]{0,1:T(2,128)S(1)}, s32[26,2]{0,1:T(2,128)}, u32[]{:S(2)}) copy-start(s32[26,2]{0,1:T(2,128)} %param.14) | copy-start | bytes 628
  17.9 131.0 %collective-permute-start.3 = (f32[26,224,256]{2,1,0:T(8,128)}, f32[26,224,256]{2,1,0:T(8,128)}, u32[]{:S(2)}, u32[]{:S(2)}) collective-permute-start(f32[26,224,256]{2,1,0:T(8,128)} %bitcast_convert_fusion), channel_id=1, source_target_pairs={{1,0},{2,1},{3,2},{0,3},{5,4},{6,5},{7,6},{4,7},{9,8},{10,9},{11,1... | collective-permute-start | bytes 17891336 | tf_op jit(solution)/shard_map/ppermute | solution.py:246
  21.5 39.1 %collective-permute-start = (f32[26,16,1024]{2,1,0:T(8,128)S(1)}, f32[26,16,1024]{2,1,0:T(8,128)S(1)}, u32[]{:S(2)}, u32[]{:S(2)}) collective-permute-start(f32[26,16,1024]{2,1,0:T(8,128)S(1)} %copy-done.3), channel_id=1, source_target_pairs={{0,1},{1,2},{2,3},{3,0},{4,5},{5,6},{6,7},{7,4},{8,9},{9,10},{10,1... | collective-permute-start | bytes 5111816 | tf_op jit(solution)/shard_map/ppermute | solution.py:249
  60.6 88.4 %copy-start.4 = (f32[26,16,1024]{2,1,0:T(8,128)}, f32[26,16,1024]{2,1,0:T(8,128)S(1)}, u32[]{:S(2)}) copy-start(f32[26,16,1024]{2,1,0:T(8,128)S(1)} %collective-permute-done.refs_1_.refs_5_.refs_9_) | copy-start | bytes 5111812
  60.6 38.4 %collective-permute-start.1 = (f32[26,16,1024]{2,1,0:T(8,128)S(1)}, f32[26,16,1024]{2,1,0:T(8,128)S(1)}, u32[]{:S(2)}, u32[]{:S(2)}) collective-permute-start(f32[26,16,1024]{2,1,0:T(8,128)S(1)} %collective-permute-done.refs_1_.refs_5_.refs_9_), channel_id=1, source_target_pairs={{0,1},{1,2},{2,3},{3,0},{4,5},{5,6},{6,7},{7,4},{8,9},{9,10},{10,1... | collective-permute-start | bytes 5111816 | tf_op jit(solution)/shard_map/ppermute | solution.py:249
  99.0 50.0 %copy-start.5 = (f32[26,16,1024]{2,1,0:T(8,128)}, f32[26,16,1024]{2,1,0:T(8,128)S(1)}, u32[]{:S(2)}) copy-start(f32[26,16,1024]{2,1,0:T(8,128)S(1)} %collective-permute-done.1.refs_2_.refs_6_.refs_10_) | copy-start | bytes 5111812
  99.0 37.6 %collective-permute-start.2 = (f32[26,16,1024]{2,1,0:T(8,128)S(1)}, f32[26,16,1024]{2,1,0:T(8,128)}, u32[]{:S(2)}, u32[]{:S(2)}) collective-permute-start(f32[26,16,1024]{2,1,0:T(8,128)S(1)} %collective-permute-done.1.refs_2_.refs_6_.refs_10_), channel_id=1, source_target_pairs={{0,1},{1,2},{2,3},{3,0},{4,5},{5,6},{6,7},{7,4},{8,9},{9,10},{10,1... | collective-permute-start | bytes 5111816 | tf_op jit(solution)/shard_map/ppermute | solution.py:249
  189.4 25.3 %collective-permute-start.8 = (f32[8,112,128]{2,1,0:T(8,128)}, f32[8,112,128]{2,1,0:T(8,128)S(1)}, u32[]{:S(2)}, u32[]{:S(2)}) collective-permute-start(f32[8,112,128]{2,1,0:T(8,128)} %shard_map.86), channel_id=1, source_target_pairs={{0,1},{1,0},{2,3},{3,2},{4,5},{5,4},{6,7},{7,6},{8,9},{9,8},{10,11... | collective-permute-start | bytes 1376264 | tf_op jit(solution)/shard_map/ppermute | solution.py:265
  197.6 19.6 %collective-permute-start.4 = (f32[6,112,128]{2,1,0:T(8,128)}, f32[6,112,128]{2,1,0:T(8,128)S(1)}, u32[]{:S(2)}, u32[]{:S(2)}) collective-permute-start(f32[6,112,128]{2,1,0:T(8,128)} %shard_map.84), channel_id=1, source_target_pairs={{0,1},{1,0},{2,3},{3,2},{4,5},{5,4},{6,7},{7,6},{8,9},{9,8},{10,11... | collective-permute-start | bytes 1032200 | tf_op jit(solution)/shard_map/ppermute | solution.py:265
  204.8 9.9 %copy-start.6 = (f32[8,112,128]{2,1,0:T(8,128)S(1)}, f32[8,112,128]{2,1,0:T(8,128)}, u32[]{:S(2)}) copy-start(f32[8,112,128]{2,1,0:T(8,128)} %shard_map.86) | copy-start | bytes 1376260
  204.9 12.4 %copy-start.9 = (f32[6,112,128]{2,1,0:T(8,128)S(1)}, f32[6,112,128]{2,1,0:T(8,128)}, u32[]{:S(2)}) copy-start(f32[6,112,128]{2,1,0:T(8,128)} %shard_map.84) | copy-start | bytes 1032196
  204.9 12.9 %copy-start.8 = (f32[6,112,128]{2,1,0:T(8,128)S(1)}, f32[6,112,128]{2,1,0:T(8,128)}, u32[]{:S(2)}) copy-start(f32[6,112,128]{2,1,0:T(8,128)} %shard_map.85) | copy-start | bytes 1032196
  204.9 12.8 %collective-permute-start.6 = (f32[6,112,128]{2,1,0:T(8,128)}, f32[6,112,128]{2,1,0:T(8,128)S(1)}, u32[]{:S(2)}, u32[]{:S(2)}) collective-permute-start(f32[6,112,128]{2,1,0:T(8,128)} %shard_map.85), channel_id=1, source_target_pairs={{0,3},{1,2},{2,1},{3,0},{4,7},{5,6},{6,5},{7,4},{8,11},{9,10},{10,... | collective-permute-start | bytes 1032200 | tf_op jit(solution)/shard_map/ppermute | solution.py:265
  214.4 9.9 %copy-start.7 = (f32[6,112,128]{2,1,0:T(8,128)S(1)}, f32[6,112,128]{2,1,0:T(8,128)}, u32[]{:S(2)}) copy-start(f32[6,112,128]{2,1,0:T(8,128)} %shard_map.87) | copy-start | bytes 1032196
  214.4 9.9 %collective-permute-start.10 = (f32[6,112,128]{2,1,0:T(8,128)}, f32[6,112,128]{2,1,0:T(8,128)S(1)}, u32[]{:S(2)}, u32[]{:S(2)}) collective-permute-start(f32[6,112,128]{2,1,0:T(8,128)} %shard_map.87), channel_id=1, source_target_pairs={{0,3},{1,2},{2,1},{3,0},{4,7},{5,6},{6,5},{7,4},{8,11},{9,10},{10,... | collective-permute-start | bytes 1032200 | tf_op jit(solution)/shard_map/ppermute | solution.py:265
  214.8 29.1 %collective-permute-start.9 = (f32[8,112,128]{2,1,0:T(8,128)S(1)}, f32[8,112,128]{2,1,0:T(8,128)S(1)}, u32[]{:S(2)}, u32[]{:S(2)}) collective-permute-start(f32[8,112,128]{2,1,0:T(8,128)S(1)} %add.33), channel_id=1, source_target_pairs={{0,3},{1,2},{2,1},{3,0},{4,7},{5,6},{6,5},{7,4},{8,11},{9,10},{10,... | collective-permute-start | bytes 1376264 | tf_op jit(solution)/shard_map/ppermute | solution.py:266
  217.3 24.3 %collective-permute-start.5 = (f32[6,112,128]{2,1,0:T(8,128)S(1)}, f32[6,112,128]{2,1,0:T(8,128)S(1)}, u32[]{:S(2)}, u32[]{:S(2)}) collective-permute-start(f32[6,112,128]{2,1,0:T(8,128)S(1)} %add.29), channel_id=1, source_target_pairs={{0,3},{1,2},{2,1},{3,0},{4,7},{5,6},{6,5},{7,4},{8,11},{9,10},{10,... | collective-permute-start | bytes 1032200 | tf_op jit(solution)/shard_map/ppermute | solution.py:266
  217.7 24.6 %collective-permute-start.7 = (f32[6,112,128]{2,1,0:T(8,128)S(1)}, f32[6,112,128]{2,1,0:T(8,128)S(1)}, u32[]{:S(2)}, u32[]{:S(2)}) collective-permute-start(f32[6,112,128]{2,1,0:T(8,128)S(1)} %add.31), channel_id=1, source_target_pairs={{0,1},{1,0},{2,3},{3,2},{4,5},{5,4},{6,7},{7,6},{8,9},{9,8},{10,11... | collective-permute-start | bytes 1032200 | tf_op jit(solution)/shard_map/ppermute | solution.py:266
  224.4 18.7 %collective-permute-start.11 = (f32[6,112,128]{2,1,0:T(8,128)S(1)}, f32[6,112,128]{2,1,0:T(8,128)S(1)}, u32[]{:S(2)}, u32[]{:S(2)}) collective-permute-start(f32[6,112,128]{2,1,0:T(8,128)S(1)} %add.35), channel_id=1, source_target_pairs={{0,1},{1,0},{2,3},{3,2},{4,5},{5,4},{6,7},{7,6},{8,9},{9,8},{10,11... | collective-permute-start | bytes 1032200 | tf_op jit(solution)/shard_map/ppermute | solution.py:266
  250.0 42.4 %copy-start.1 = (s32[64]{0:T(128)S(1)}, s32[64]{0:T(128)}, u32[]{:S(2)}) copy-start(s32[64]{0:T(128)} %param.15) | copy-start | bytes 772
Sparse Core Ops, SparseCore 0:
  10.3 170.7 all-gather.2

commit v5 on v4

--- a/solution.py
+++ b/solution.py
@@ -187,7 +187,7 @@
     )(momentum, rows, *([blocks] * PAIR), conduct)
 
 
-def response_body(start, counts, near_ref, far_ref, trial_ref, *refs):
+def response_body(start, counts, near_ref, far_ref, near_place_ref, far_place_ref, trial_ref, *refs):
     kernels, (out_ref, turn_ref) = refs[: len(counts)], refs[-2:]
     if len(refs) > len(counts) + 2:
         out_ref[...] = refs[len(counts)][...]
@@ -204,13 +204,14 @@
             kernel = turn_ref[...]
             direct = mul3(trial_ref[far], kernel, TURNED)
             mirror = mul3(trial_ref[near], kernel, PLAIN)
+            near, far = near_place_ref[start + p], far_place_ref[start + p]
             out_ref[near] = out_ref[near] + direct
             out_ref[far] = out_ref[far] + mirror
 
         start += count
 
 
-def contributions(start, near, far, blocks, trials, kernels, before=()):
+def contributions(start, places, blocks, trials, kernels, before=()):
     counts = [kernel.shape[0] for kernel in kernels]
     shape = (blocks.shape[0], trials, VC)
     whole = [pl.BlockSpec(x.shape, lambda g: (0, 0, 0)) for x in kernels]
@@ -220,14 +221,14 @@
         lambda *refs: response_body(start, counts, *refs),
         out_shape=jax.ShapeDtypeStruct(shape, F32),
         grid=(1,),
-        in_specs=[scalar, scalar, result, *whole] + [result] * len(before),
+        in_specs=[scalar] * len(places) + [result, *whole] + [result] * len(before),
         out_specs=result,
         scratch_shapes=[pltpu.VMEM((VC, VC), F32)],
         cost_estimate=pl.CostEstimate(flops=sum(counts) * 10**7, bytes_accessed=4 * 10**6, transcendentals=0),
-    )(near, far, blocks, *kernels, *before)
-
-
-def local(valence, conduction, screened, momentum, kpairs, kpoint_slot, trial_blocks):
+    )(*places, blocks, *kernels, *before)
+
+
+def compute(valence, conduction, screened, momentum, kpairs, kpoint_slot, trial_blocks):
     ka = lax.axis_size("ka")
     pair_dev = valence.shape[0]
     own = conduction.shape[2]
@@ -250,31 +251,45 @@
     near = jnp.take(kpoint_slot, kpairs[:, 0])
     far = jnp.take(kpoint_slot, kpairs[:, 1])
     rows, conduct = prepare(here, rows, conduct, conduct_next)
-    rows, conduct, near, far = lax.optimization_barrier((rows, conduct, near, far))
+    owners = lax.axis_size("pb")
+    core = lax.rem(lax.axis_index("pb").astype(jnp.int32), 2)
+    places = [near, far] + [lax.rem(x + core, 2) * (owners // 2) + x // 2 for x in (near, far)]
+    rows, conduct, places = lax.optimization_barrier((rows, conduct, places))
 
     swap = [(i, i ^ 1) for i in range(ka)]
     fold = [(i, ka - 1 - i) for i in range(ka)]
     target = momentum[:, 0]
     each = max(PAIR, pair_dev // 4 // PAIR * PAIR)
     sizes = [pair_dev - 3 * each, each, each, each]
+    turns = (swap, fold)
+
+    def again(i, kernel):
+        return kernel + lax.ppermute(kernel, "ka", turns[1 - i % 2])
+
     kernels, start = [], 0
-    for size in sizes:
-        kernels.append(pair_kernels(start, size, target, rows, blocks, conduct, local_trials))
+    for i, size in enumerate(sizes):
+        if i == len(sizes) - 1:
+            target, kernels[0] = lax.optimization_barrier((target, kernels[0]))
+            kernels[0] = again(0, kernels[0])
+        kernel = pair_kernels(start, size, target, rows, blocks, conduct, local_trials)
+        kernels.append(kernel + lax.ppermute(kernel, "ka", turns[i % 2]))
         start += size
-    turns = (swap, fold)
-    kernels = [x + lax.ppermute(x, "ka", turns[i % 2]) for i, x in enumerate(kernels)]
-    kernels = [x + lax.ppermute(x, "ka", turns[1 - i % 2]) for i, x in enumerate(kernels)]
-
-    summed = contributions(0, near, far, blocks, local_trials, kernels[:2])
-    summed = contributions(sum(sizes[:2]), near, far, blocks, local_trials, kernels[2:], (summed,))
-    parts = lax.all_to_all(summed, "pb", split_axis=0, concat_axis=0, tiled=True)
+    for i in range(1, len(sizes)):
+        kernels[i] = again(i, kernels[i])
+
+    summed = contributions(0, places, blocks, local_trials, kernels[:2])
+    summed = contributions(sum(sizes[:2]), places, blocks, local_trials, kernels[2:], (summed,))
+    half = owners // 2
+    other = lax.ppermute(summed[half:], "pb", [(i, i ^ 1) for i in range(owners)])
+    groups = [list(range(c, owners, 2)) for c in range(2)]
+    parts = lax.all_to_all(summed[:half] + other, "pb", split_axis=0, concat_axis=0, axis_index_groups=groups, tiled=True)
     response = jnp.sum(parts, axis=0).reshape(local_trials, VB, CD)[:, :, :CB]
     return response.reshape(1, -1)
 
 
 def solution(mesh):
     return jax.shard_map(
-        local,
+        compute,
         mesh=mesh,
         in_specs=(
             P("pb", "ka", None),

time: 300 us -> 291 us (0.970); the launches traced: 299 us -> 287 us
  blocking collectives: 36.1 us -> 19.2 us
    all_to_all x1, blocking collectives: 36.1 us -> 19.2 us  [compute(): lax.all_to_all(summed[:half] + other, 'pb', split_axis=0, concat_axis=0,...]
    add x8 -> x11, other arithmetic: 3.3 us -> 6.53 us  [the longest x4 3.14 us: again(): return kernel + lax.ppermute(kernel, 'ka', turns[1 - i % 2])]
    ppermute x12 -> x13, starting transfers between devices: 11.1 us -> 12.8 us  [the longest x4 4.08 us: compute(): kernels.append(kernel + lax.ppermute(kernel, 'ka', turns[i % 2]))]
    ppermute x12 -> x13, waiting for transfers between devices: 149 us -> 148 us  [the longest x3 113 us: compute(): rows.append(lax.ppermute(rows[-1], 'ka', ahead))]
  transfers between devices with their start and end apart: 13 -> 14, of which waited for: 7 -> 8; matrix products, arithmetic and copies ran while one was open for 4% -> 5% of each run, Pallas kernels for 14% -> 16%
where the time goes in v5:
time: 291 us; the launch traced here: 287 us
  waiting for transfers between devices  160 us (55%)
  Pallas kernels  62.3 us (21%)
  blocking collectives  19.2 us (7%)
  between operations  13.6 us (5%)
  starting transfers between devices  12.8 us (4%)
  other arithmetic  10.8 us (4%)
  local copies, waits for them, and re-layouts  8.43 us (3%)
    ppermute x3, waiting for transfers between devices, compute(): rows.append(lax.ppermute(rows[-1], 'ka', ahead))  113 us
    pallas_call x4, Pallas kernels, pair_kernels(): pl.pallas_call(lambda *refs: pair_body(skip, *refs), out_shape=jax.ShapeD...  29.4 us
    pallas_call x1, Pallas kernels, prepare(): pl.pallas_call(prepare_body, out_shape=tuple((jax.ShapeDtypeStruct(shape,...  20.2 us
    all_to_all x1, blocking collectives, compute(): lax.all_to_all(summed[:half] + other, 'pb', split_axis=0, concat_axis=0,...  19.2 us
    ppermute x4, waiting for transfers between devices, again(): return kernel + lax.ppermute(kernel, 'ka', turns[1 - i % 2])  15.3 us
    ppermute x1, waiting for transfers between devices, compute(): conduct_next = lax.ppermute(conduct.astype(F32), 'ka', back)  12.4 us
    all_gather x1, waiting for transfers between devices, compute(): lax.all_gather(pack(here, own_trials, jnp.asarray(spread), screened, ka),...  11.9 us
    pallas_call x2, Pallas kernels, contributions(): pl.pallas_call(lambda *refs: response_body(start, counts, *refs), out_sha...  10.5 us
  transfers between devices with their start and end apart: 14, of which 8 were waited for; matrix products, arithmetic and copies ran while one was open for 5% of the time, Pallas kernels for 16%

profile of v5, /device:TPU:1, one launch (start us, length us, event | category | flops | bytes accessed | tf_op | source)
XLA Modules:
  0.0 286.8 jit_solution(7427964605616115767)
XLA Ops:
  6.5 0.0 copy-start
  6.5 0.8 reduce
  7.3 0.7 reshape.26.trial_ref
  8.0 2.2 shard_map.83
  10.2 0.0 all-gather.3.cloned.1.call-update
  10.2 3.7 %reshape.24 = bf16[26,14,14,256]{3,2,1,0:T(8,128)(2,1)S(1)} reshape(bf16[26,196,256]{2,1,0:T(8,128)(2,1)} %param.11) | data formatting | bytes 5218304 | tf_op jit(solution)/shard_map/reshape | solution.py:245
  13.9 0.5 pad.4
  14.3 0.0 copy-start.3
  14.3 0.0 copy-start.9
  14.4 3.4 %bitcast_convert_fusion = f32[26,224,256]{2,1,0:T(8,128)} fusion(bf16[26,14,16,256]{3,2,1,0:T(8,128)(2,1)S(1)} %pad.4), kind=kLoop, calls=%fused_computation.27 | loop fusion | flops 1490944 | bytes 8945664 | tf_op jit(solution)/shard_map/convert_element_type | solution.py:247
  17.8 0.1 copy-done.2
  17.9 3.6 %collective-permute-start.3 = (f32[26,224,256]{2,1,0:T(8,128)}, f32[26,224,256]{2,1,0:T(8,128)}, u32[]{:S(2)}, u32[]{:S(2)}) collective-permute-start(f32[26,224,256]{2,1,0:T(8,128)} %bitcast_convert_fusion), channel_id=1, source_target_pairs={{1,0},{2,1},{3,2},{0,3},{5,4},{6,5},{7,6},{4,7},{9,8},{10,9},{11,1... | collective-permute-start | bytes 17891336 | tf_op jit(solution)/shard_map/ppermute | solution.py:247
  21.5 0.0 collective-permute-start
  21.5 39.1 %collective-permute-done.refs_1_.refs_5_.refs_9_ = f32[26,16,1024]{2,1,0:T(8,128)S(1)} collective-permute-done((f32[26,16,1024]{2,1,0:T(8,128)S(1)}, f32[26,16,1024]{2,1,0:T(8,128)S(1)}, u32[]{:S(2)}, u32[]{:S(2)}) %collective-permute-start) | collective-permute-done | bytes 1703968 | tf_op jit(solution)/shard_map/ppermute | solution.py:250
  60.6 0.0 collective-permute-start.1
  60.6 38.4 %collective-permute-done.1.refs_2_.refs_6_.refs_10_ = f32[26,16,1024]{2,1,0:T(8,128)S(1)} collective-permute-done((f32[26,16,1024]{2,1,0:T(8,128)S(1)}, f32[26,16,1024]{2,1,0:T(8,128)S(1)}, u32[]{:S(2)}, u32[]{:S(2)}) %collective-permute-start.1) | collective-permute-done | bytes 1703968 | tf_op jit(solution)/shard_map/ppermute | solution.py:250
  99.0 0.0 collective-permute-start.2
  99.0 0.0 copy-done.9
  99.0 0.0 copy-done
  99.0 0.7 gather_fusion.1
  99.7 0.5 fusion.5
  100.3 0.7 gather_fusion
  101.0 0.6 fusion.2
  101.6 35.0 %collective-permute-done.2.refs_3_.refs_7_.refs_11_ = f32[26,16,1024]{2,1,0:T(8,128)} collective-permute-done((f32[26,16,1024]{2,1,0:T(8,128)S(1)}, f32[26,16,1024]{2,1,0:T(8,128)}, u32[]{:S(2)}, u32[]{:S(2)}) %collective-permute-start.2) | collective-permute-done | bytes 1703968 | tf_op jit(solution)/shard_map/ppermute | solution.py:250
  136.6 12.4 %collective-permute-done.3.refs_13_ = f32[26,224,256]{2,1,0:T(8,128)} collective-permute-done((f32[26,224,256]{2,1,0:T(8,128)}, f32[26,224,256]{2,1,0:T(8,128)}, u32[]{:S(2)}, u32[]{:S(2)}) %collective-permute-start.3) | collective-permute-done | bytes 5963808 | tf_op jit(solution)/shard_map/ppermute | solution.py:247
  149.0 20.2 %shard_map.82 = (bf16[26,128,768]{2,1,0:T(8,128)(2,1)}, bf16[26,224,512]{2,1,0:T(8,128)(2,1)}) custom-call(s32[1]{0:T(128)} %bitcast.ka_ref, f32[26,16,1024]{2,1,0:T(8,128)} %refs_8_.1, f32[26,16,1024]{2,1,0:T(8,128)} %copy-done.4, f32[26,16,1024]{2,1,0:T(8,128)} %copy-done.5, f32[26,16,1024]{2,1,0:T(8,128)} %collective-permute-done.2.refs_3_.refs_7_.refs_11_, ...), custom_call_target="tpu_custom_call" | custom-call | bytes 17039360 | tf_op jit(solution)/shard_map/pallas_call | solution.py:108
  169.1 11.9 %all-gather.3.cloned.1.call-done = f32[84480,128]{1,0:T(8,128)} async-done(((f32[1320,128]{1,0:T(8,128)}), f32[84480,128]{1,0:T(8,128)}) %all-gather.3.cloned.1.call-update) | async-done | bytes 43253776 | tf_op jit(solution)/shard_map/all_gather | solution.py:241
  181.1 8.3 %shard_map.85 = f32[8,112,128]{2,1,0:T(8,128)} custom-call(s32[26]{0:T(128)} %bitcast.29, bf16[26,128,768]{2,1,0:T(8,128)(2,1)} %get-tuple-element.22.refs_1_, f32[64,1320,128]{2,1,0:T(8,128)} %bitcast.17, f32[64,1320,128]{2,1,0:T(8,128)} %bitcast.18, bf16[26,224,512]{2,1,0:T(8,128)(2,1)} %get-tuple-element.23.refs_4_), custom_call_target="tpu_custom_call" | custom-call | flops 800000000 | bytes 8800000 | tf_op jit(solution)/shard_map/pallas_call | solution.py:174
  189.4 1.2 collective-permute-start.6
  190.6 7.0 %shard_map.87 = f32[6,112,128]{2,1,0:T(8,128)} custom-call(s32[26]{0:T(128)} %bitcast.30, bf16[26,128,768]{2,1,0:T(8,128)(2,1)} %get-tuple-element.22.refs_1_, f32[64,1320,128]{2,1,0:T(8,128)} %bitcast.19, f32[64,1320,128]{2,1,0:T(8,128)} %bitcast.20, bf16[26,224,512]{2,1,0:T(8,128)(2,1)} %get-tuple-element.23.refs_4_), custom_call_target="tpu_custom_call" | custom-call | flops 600000000 | bytes 6600000 | tf_op jit(solution)/shard_map/pallas_call | solution.py:174
  197.6 1.8 collective-permute-start.10
  199.4 7.0 %shard_map.84 = f32[6,112,128]{2,1,0:T(8,128)} custom-call(s32[26]{0:T(128)} %bitcast.31, bf16[26,128,768]{2,1,0:T(8,128)(2,1)} %get-tuple-element.22.refs_1_, f32[64,1320,128]{2,1,0:T(8,128)} %bitcast.21, f32[64,1320,128]{2,1,0:T(8,128)} %bitcast.22, bf16[26,224,512]{2,1,0:T(8,128)(2,1)} %get-tuple-element.23.refs_4_), custom_call_target="tpu_custom_call" | custom-call | flops 600000000 | bytes 6600000 | tf_op jit(solution)/shard_map/pallas_call | solution.py:174
  206.4 0.3 collective-permute-start.4
  206.7 0.0 collective-permute-done.6
  206.7 0.0 copy-done.6
  206.8 7.1 %shard_map.86 = f32[6,112,128]{2,1,0:T(8,128)} custom-call(s32[26]{0:T(128)} %bitcast.32, bf16[26,128,768]{2,1,0:T(8,128)(2,1)} %get-tuple-element.22.refs_1_, f32[64,1320,128]{2,1,0:T(8,128)} %bitcast.23, f32[64,1320,128]{2,1,0:T(8,128)} %bitcast.24, bf16[26,224,512]{2,1,0:T(8,128)(2,1)} %get-tuple-element.23.refs_4_), custom_call_target="tpu_custom_call" | custom-call | flops 600000000 | bytes 6600000 | tf_op jit(solution)/shard_map/pallas_call | solution.py:174
  213.9 0.7 collective-permute-start.7
  214.7 1.9 collective-permute-start.9
  216.6 0.0 collective-permute-done.10
  216.6 0.1 collective-permute-start.11
  216.7 0.0 collective-permute-done.4
  216.8 1.0 collective-permute-start.5
  217.8 6.0 %collective-permute-done.7 = f32[6,112,128]{2,1,0:T(8,128)S(1)} collective-permute-done((f32[6,112,128]{2,1,0:T(8,128)}, f32[6,112,128]{2,1,0:T(8,128)S(1)}, u32[]{:S(2)}, u32[]{:S(2)}) %collective-permute-start.7) | collective-permute-done | bytes 344096 | tf_op jit(solution)/shard_map/ppermute | solution.py:275
  223.9 1.0 add.58
  224.9 0.1 collective-permute-start.8
  225.0 0.0 collective-permute-done.11
  225.0 0.8 add.62.refs_6_
  225.8 15.3 %collective-permute-done.5 = f32[6,112,128]{2,1,0:T(8,128)S(1)} collective-permute-done((f32[6,112,128]{2,1,0:T(8,128)S(1)}, f32[6,112,128]{2,1,0:T(8,128)S(1)}, u32[]{:S(2)}, u32[]{:S(2)}) %collective-permute-start.5) | collective-permute-done | bytes 344096 | tf_op jit(solution)/shard_map/ppermute | solution.py:267
  241.1 0.7 add.56.refs_5_
  241.8 0.0 collective-permute-done.9
  241.8 0.8 add.60.refs_5_
  242.6 5.3 %shard_map.88.refs_7_ = f32[64,32,128]{2,1,0:T(8,128)} custom-call(s32[26]{0:T(128)} %get-tuple-element.18.refs_0_, s32[26]{0:T(128)} %get-tuple-element.19.refs_1_, s32[26]{0:T(128)} %get-tuple-element.20.refs_2_, s32[26]{0:T(128)} %get-tuple-element.21.refs_3_, f32[64,1320,128]{2,1,0:T(8,128)} %bitcast.25, f32[8,112,128]{2,1,0:T(8,128)} %add.60.refs_5_, ...), custom_call_target="tpu_custom_call" | custom-call | flops 140000000 | bytes 4000000 | tf_op jit(solution)/shard_map/pallas_call | solution.py:220
  248.0 0.0 collective-permute-done.8
  248.0 0.8 add.59.refs_6_
  248.7 5.2 %shard_map.89 = f32[64,32,128]{2,1,0:T(8,128)} custom-call(s32[26]{0:T(128)} %get-tuple-element.18.refs_0_, s32[26]{0:T(128)} %get-tuple-element.19.refs_1_, s32[26]{0:T(128)} %get-tuple-element.20.refs_2_, s32[26]{0:T(128)} %get-tuple-element.21.refs_3_, f32[64,1320,128]{2,1,0:T(8,128)} %bitcast.26, f32[6,112,128]{2,1,0:T(8,128)} %add.56.refs_5_, ...), custom_call_target="tpu_custom_call" | custom-call | flops 120000000 | bytes 4000000 | tf_op jit(solution)/shard_map/pallas_call | solution.py:220
  253.9 1.1 slice.25
  255.0 2.0 collective-permute-start.12
  257.0 1.5 collective-permute-done.12
  258.6 1.1 slice_add_fusion
  259.7 19.2 %all_to_all.5 = f32[32,32,128]{2,1,0:T(8,128)S(1)} all-to-all(f32[32,32,128]{2,1,0:T(8,128)S(1)} %slice_add_fusion), channel_id=1, replica_groups={{0,8,16,24,32,40,48,56,64,72,80,88,96,104,112,120,128,136,144,152,160,1..., dimensions={0} | all-to-all | bytes 1048576 | tf_op jit(solution)/shard_map/all_to_all | solution.py:285
  279.0 0.1 copy.10
  279.1 0.1 copy.11
  279.2 0.8 reshape.28
  280.0 0.0 copy-done.1
  (20 shorter events, 0.2 us)
Async XLA Ops:
  6.5 92.5 %copy-start = (s32[64]{0:T(128)S(1)}, s32[64]{0:T(128)}, u32[]{:S(2)}) copy-start(s32[64]{0:T(128)} %param.15) | copy-start | bytes 772
  6.5 174.5 %all-gather.3.cloned.1.call-start = ((), (), s32[]{:S(2)}) async-start(), calls=%async_computation.1 | async-start | bytes 43929600 | tf_op jit(solution)/shard_map/all_gather | solution.py:241
  14.3 3.6 %copy-start.2 = (bf16[26,14,16,256]{3,2,1,0:T(8,128)(2,1)}, bf16[26,14,16,256]{3,2,1,0:T(8,128)(2,1)S(1)}, u32[]{:S(2)}) copy-start(bf16[26,14,16,256]{3,2,1,0:T(8,128)(2,1)S(1)} %pad.4) | copy-start | bytes 8945668
  14.3 7.1 %copy-start.3 = (f32[26,16,1024]{2,1,0:T(8,128)S(1)}, f32[26,16,1024]{2,1,0:T(8,128)}, u32[]{:S(2)}) copy-start(f32[26,16,1024]{2,1,0:T(8,128)} %refs_8_.1) | copy-start | bytes 5111812
  14.3 84.6 %copy-start.9 = (s32[26,2]{0,1:T(2,128)S(1)}, s32[26,2]{0,1:T(2,128)}, u32[]{:S(2)}) copy-start(s32[26,2]{0,1:T(2,128)} %param.14) | copy-start | bytes 628
  17.9 131.0 %collective-permute-start.3 = (f32[26,224,256]{2,1,0:T(8,128)}, f32[26,224,256]{2,1,0:T(8,128)}, u32[]{:S(2)}, u32[]{:S(2)}) collective-permute-start(f32[26,224,256]{2,1,0:T(8,128)} %bitcast_convert_fusion), channel_id=1, source_target_pairs={{1,0},{2,1},{3,2},{0,3},{5,4},{6,5},{7,6},{4,7},{9,8},{10,9},{11,1... | collective-permute-start | bytes 17891336 | tf_op jit(solution)/shard_map/ppermute | solution.py:247
  21.5 39.1 %collective-permute-start = (f32[26,16,1024]{2,1,0:T(8,128)S(1)}, f32[26,16,1024]{2,1,0:T(8,128)S(1)}, u32[]{:S(2)}, u32[]{:S(2)}) collective-permute-start(f32[26,16,1024]{2,1,0:T(8,128)S(1)} %copy-done.3), channel_id=1, source_target_pairs={{0,1},{1,2},{2,3},{3,0},{4,5},{5,6},{6,7},{7,4},{8,9},{9,10},{10,1... | collective-permute-start | bytes 5111816 | tf_op jit(solution)/shard_map/ppermute | solution.py:250
  60.6 88.4 %copy-start.4 = (f32[26,16,1024]{2,1,0:T(8,128)}, f32[26,16,1024]{2,1,0:T(8,128)S(1)}, u32[]{:S(2)}) copy-start(f32[26,16,1024]{2,1,0:T(8,128)S(1)} %collective-permute-done.refs_1_.refs_5_.refs_9_) | copy-start | bytes 5111812
  60.6 38.4 %collective-permute-start.1 = (f32[26,16,1024]{2,1,0:T(8,128)S(1)}, f32[26,16,1024]{2,1,0:T(8,128)S(1)}, u32[]{:S(2)}, u32[]{:S(2)}) collective-permute-start(f32[26,16,1024]{2,1,0:T(8,128)S(1)} %collective-permute-done.refs_1_.refs_5_.refs_9_), channel_id=1, source_target_pairs={{0,1},{1,2},{2,3},{3,0},{4,5},{5,6},{6,7},{7,4},{8,9},{9,10},{10,1... | collective-permute-start | bytes 5111816 | tf_op jit(solution)/shard_map/ppermute | solution.py:250
  99.0 50.0 %copy-start.5 = (f32[26,16,1024]{2,1,0:T(8,128)}, f32[26,16,1024]{2,1,0:T(8,128)S(1)}, u32[]{:S(2)}) copy-start(f32[26,16,1024]{2,1,0:T(8,128)S(1)} %collective-permute-done.1.refs_2_.refs_6_.refs_10_) | copy-start | bytes 5111812
  99.0 37.6 %collective-permute-start.2 = (f32[26,16,1024]{2,1,0:T(8,128)S(1)}, f32[26,16,1024]{2,1,0:T(8,128)}, u32[]{:S(2)}, u32[]{:S(2)}) collective-permute-start(f32[26,16,1024]{2,1,0:T(8,128)S(1)} %collective-permute-done.1.refs_2_.refs_6_.refs_10_), channel_id=1, source_target_pairs={{0,1},{1,2},{2,3},{3,0},{4,5},{5,6},{6,7},{7,4},{8,9},{9,10},{10,1... | collective-permute-start | bytes 5111816 | tf_op jit(solution)/shard_map/ppermute | solution.py:250
  189.4 17.3 %collective-permute-start.6 = (f32[8,112,128]{2,1,0:T(8,128)}, f32[8,112,128]{2,1,0:T(8,128)S(1)}, u32[]{:S(2)}, u32[]{:S(2)}) collective-permute-start(f32[8,112,128]{2,1,0:T(8,128)} %shard_map.85), channel_id=1, source_target_pairs={{0,1},{1,0},{2,3},{3,2},{4,5},{5,4},{6,7},{7,6},{8,9},{9,8},{10,11... | collective-permute-start | bytes 1376264 | tf_op jit(solution)/shard_map/ppermute | solution.py:275
  197.6 9.1 %copy-start.6 = (f32[8,112,128]{2,1,0:T(8,128)S(1)}, f32[8,112,128]{2,1,0:T(8,128)}, u32[]{:S(2)}) copy-start(f32[8,112,128]{2,1,0:T(8,128)} %shard_map.85) | copy-start | bytes 1376260
  197.6 19.0 %collective-permute-start.10 = (f32[6,112,128]{2,1,0:T(8,128)}, f32[6,112,128]{2,1,0:T(8,128)S(1)}, u32[]{:S(2)}, u32[]{:S(2)}) collective-permute-start(f32[6,112,128]{2,1,0:T(8,128)} %shard_map.87), channel_id=1, source_target_pairs={{0,3},{1,2},{2,1},{3,0},{4,7},{5,6},{6,5},{7,4},{8,11},{9,10},{10,... | collective-permute-start | bytes 1032200 | tf_op jit(solution)/shard_map/ppermute | solution.py:275
  206.4 10.3 %collective-permute-start.4 = (f32[6,112,128]{2,1,0:T(8,128)}, f32[6,112,128]{2,1,0:T(8,128)S(1)}, u32[]{:S(2)}, u32[]{:S(2)}) collective-permute-start(f32[6,112,128]{2,1,0:T(8,128)} %shard_map.84), channel_id=1, source_target_pairs={{0,1},{1,0},{2,3},{3,2},{4,5},{5,4},{6,7},{7,6},{8,9},{9,8},{10,11... | collective-permute-start | bytes 1032200 | tf_op jit(solution)/shard_map/ppermute | solution.py:275
  206.8 9.8 %copy-start.8 = (f32[6,112,128]{2,1,0:T(8,128)S(1)}, f32[6,112,128]{2,1,0:T(8,128)}, u32[]{:S(2)}) copy-start(f32[6,112,128]{2,1,0:T(8,128)} %shard_map.87) | copy-start | bytes 1032196
  206.8 10.0 %copy-start.7 = (f32[6,112,128]{2,1,0:T(8,128)S(1)}, f32[6,112,128]{2,1,0:T(8,128)}, u32[]{:S(2)}) copy-start(f32[6,112,128]{2,1,0:T(8,128)} %shard_map.84) | copy-start | bytes 1032196
  213.9 9.9 %collective-permute-start.7 = (f32[6,112,128]{2,1,0:T(8,128)}, f32[6,112,128]{2,1,0:T(8,128)S(1)}, u32[]{:S(2)}, u32[]{:S(2)}) collective-permute-start(f32[6,112,128]{2,1,0:T(8,128)} %shard_map.86), channel_id=1, source_target_pairs={{0,3},{1,2},{2,1},{3,0},{4,7},{5,6},{6,5},{7,4},{8,11},{9,10},{10,... | collective-permute-start | bytes 1032200 | tf_op jit(solution)/shard_map/ppermute | solution.py:275
  214.7 27.2 %collective-permute-start.9 = (f32[8,112,128]{2,1,0:T(8,128)S(1)}, f32[8,112,128]{2,1,0:T(8,128)S(1)}, u32[]{:S(2)}, u32[]{:S(2)}) collective-permute-start(f32[8,112,128]{2,1,0:T(8,128)S(1)} %add.57), channel_id=1, source_target_pairs={{0,3},{1,2},{2,1},{3,0},{4,7},{5,6},{6,5},{7,4},{8,11},{9,10},{10,... | collective-permute-start | bytes 1376264 | tf_op jit(solution)/shard_map/ppermute | solution.py:267
  216.6 8.3 %collective-permute-start.11 = (f32[6,112,128]{2,1,0:T(8,128)S(1)}, f32[6,112,128]{2,1,0:T(8,128)S(1)}, u32[]{:S(2)}, u32[]{:S(2)}) collective-permute-start(f32[6,112,128]{2,1,0:T(8,128)S(1)} %add.61), channel_id=1, source_target_pairs={{0,1},{1,0},{2,3},{3,2},{4,5},{5,4},{6,7},{7,6},{8,9},{9,8},{10,11... | collective-permute-start | bytes 1032200 | tf_op jit(solution)/shard_map/ppermute | solution.py:267
  216.8 24.3 %collective-permute-start.5 = (f32[6,112,128]{2,1,0:T(8,128)S(1)}, f32[6,112,128]{2,1,0:T(8,128)S(1)}, u32[]{:S(2)}, u32[]{:S(2)}) collective-permute-start(f32[6,112,128]{2,1,0:T(8,128)S(1)} %add.55), channel_id=1, source_target_pairs={{0,3},{1,2},{2,1},{3,0},{4,7},{5,6},{6,5},{7,4},{8,11},{9,10},{10,... | collective-permute-start | bytes 1032200 | tf_op jit(solution)/shard_map/ppermute | solution.py:267
  224.9 23.1 %collective-permute-start.8 = (f32[6,112,128]{2,1,0:T(8,128)S(1)}, f32[6,112,128]{2,1,0:T(8,128)S(1)}, u32[]{:S(2)}, u32[]{:S(2)}) collective-permute-start(f32[6,112,128]{2,1,0:T(8,128)S(1)} %add.58), channel_id=1, source_target_pairs={{0,1},{1,0},{2,3},{3,2},{4,5},{5,4},{6,7},{7,6},{8,9},{9,8},{10,11... | collective-permute-start | bytes 1032200 | tf_op jit(solution)/shard_map/ppermute | solution.py:267
  248.7 31.2 %copy-start.1 = (s32[64]{0:T(128)S(1)}, s32[64]{0:T(128)}, u32[]{:S(2)}) copy-start(s32[64]{0:T(128)} %param.15) | copy-start | bytes 772
  255.0 3.6 %collective-permute-start.12 = (f32[32,32,128]{2,1,0:T(8,128)S(1)}, f32[32,32,128]{2,1,0:T(8,128)S(1)}, u32[]{:S(2)}, u32[]{:S(2)}) collective-permute-start(f32[32,32,128]{2,1,0:T(8,128)S(1)} %slice.25), channel_id=1, source_target_pairs={{0,4},{4,0},{8,12},{12,8},{16,20},{20,16},{24,28},{28,24},{32,36},... | collective-permute-start | bytes 1572872 | tf_op jit(solution)/shard_map/ppermute | solution.py:283
Sparse Core Ops, SparseCore 0:
  10.3 170.7 all-gather.2

commit v6 on v5

--- a/solution.py
+++ b/solution.py
@@ -118,7 +118,7 @@
     )(ka, *(valence * 3), conduction, conduction_next)
 
 
-def one_pair(rows, blocks, conduct, out_ref, number, low_ref, high_ref, skip):
+def one_pair(rows, blocks, conduct, out_ref, low_ref, high_ref, skip):
     half = blocks.shape[1]
     width = 2 * half
     count = rows.shape[0] // 2
@@ -156,13 +156,13 @@
         for i in range(VB):
             c = part * VB + i
             if c < CB:
-                out_ref[number, c * VB : (c + 1) * VB, :] = tiles[i]
+                out_ref[0, c * VB : (c + 1) * VB, :] = tiles[i]
 
 
 def pair_body(skip, momentum_ref, rows_ref, *refs):
-    blocks, (conduct_ref, out_ref), scratch = refs[:PAIR], refs[PAIR : PAIR + 2], refs[PAIR + 2 :]
+    blocks, conduct_ref, outs, scratch = refs[:PAIR], refs[PAIR], refs[PAIR + 1 : 2 * PAIR + 1], refs[2 * PAIR + 1 :]
     for i in range(PAIR):
-        one_pair(rows_ref[i], blocks[i][0], conduct_ref[i], out_ref, i, scratch[2 * i], scratch[2 * i + 1], skip)
+        one_pair(rows_ref[i], blocks[i][0], conduct_ref[i], outs[i], scratch[2 * i], scratch[2 * i + 1], skip)
 
 
 def pair_kernels(start, count, momentum, rows, blocks, conduct, skip):
@@ -173,14 +173,14 @@
 
     return pl.pallas_call(
         lambda *refs: pair_body(skip, *refs),
-        out_shape=jax.ShapeDtypeStruct((count, VB * CB, VC), F32),
+        out_shape=[jax.ShapeDtypeStruct((count // PAIR, VB * CB, VC), F32)] * PAIR,
         grid_spec=pltpu.PrefetchScalarGridSpec(
             num_scalar_prefetch=1,
             grid=(count // PAIR,),
             in_specs=[pl.BlockSpec((PAIR,) + rows.shape[1:], lambda p, q: (first + p, 0, 0))]
             + [block(i) for i in range(PAIR)]
             + [pl.BlockSpec((PAIR,) + conduct.shape[1:], lambda p, q: (first + p, 0, 0))],
-            out_specs=pl.BlockSpec((PAIR, VB * CB, VC), lambda p, q: (p, 0, 0)),
+            out_specs=[pl.BlockSpec((1, VB * CB, VC), lambda p, q: (p, 0, 0))] * PAIR,
             scratch_shapes=[pltpu.VMEM((VB * VB, VC), F32)] * (2 * PAIR),
         ),
         cost_estimate=pl.CostEstimate(flops=count * 10**8, bytes_accessed=count * 11 * 10**5, transcendentals=0),
@@ -194,21 +194,20 @@
     else:
         out_ref[...] = jnp.zeros_like(out_ref)
     turn_ref[...] = jnp.zeros_like(turn_ref)
-    for count, kernel_ref in zip(counts, kernels):
+    for number, (count, kernel_ref) in enumerate(zip(counts, kernels)):
 
         @pl.loop(0, count)
-        def _(p, start=start, kernel_ref=kernel_ref):
-            near, far = near_ref[start + p], far_ref[start + p]
+        def _(p, number=number, kernel_ref=kernel_ref):
+            pair = start + PAIR * p + number
+            near, far = near_ref[pair], far_ref[pair]
             for v in range(VB):
                 turn_ref[v * CD : v * CD + CB, :] = kernel_ref[p, pl.ds(v, CB, stride=VB), :]
             kernel = turn_ref[...]
             direct = mul3(trial_ref[far], kernel, TURNED)
             mirror = mul3(trial_ref[near], kernel, PLAIN)
-            near, far = near_place_ref[start + p], far_place_ref[start + p]
+            near, far = near_place_ref[pair], far_place_ref[pair]
             out_ref[near] = out_ref[near] + direct
             out_ref[far] = out_ref[far] + mirror
-
-        start += count
 
 
 def contributions(start, places, blocks, trials, kernels, before=()):
@@ -259,26 +258,20 @@
     swap = [(i, i ^ 1) for i in range(ka)]
     fold = [(i, ka - 1 - i) for i in range(ka)]
     target = momentum[:, 0]
-    each = max(PAIR, pair_dev // 4 // PAIR * PAIR)
-    sizes = [pair_dev - 3 * each, each, each, each]
     turns = (swap, fold)
-
-    def again(i, kernel):
-        return kernel + lax.ppermute(kernel, "ka", turns[1 - i % 2])
-
-    kernels, start = [], 0
-    for i, size in enumerate(sizes):
-        if i == len(sizes) - 1:
-            target, kernels[0] = lax.optimization_barrier((target, kernels[0]))
-            kernels[0] = again(0, kernels[0])
-        kernel = pair_kernels(start, size, target, rows, blocks, conduct, local_trials)
-        kernels.append(kernel + lax.ppermute(kernel, "ka", turns[i % 2]))
-        start += size
-    for i in range(1, len(sizes)):
-        kernels[i] = again(i, kernels[i])
-
-    summed = contributions(0, places, blocks, local_trials, kernels[:2])
-    summed = contributions(sum(sizes[:2]), places, blocks, local_trials, kernels[2:], (summed,))
+    cut = -(-pair_dev // (2 * PAIR)) * PAIR
+
+    def exchanged(number, first):
+        return [x + lax.ppermute(x, "ka", turns[(i + number) % 2]) for i, x in enumerate(first)]
+
+    first = pair_kernels(0, cut, target, rows, blocks, conduct, local_trials)
+    first = exchanged(0, first)
+    second = pair_kernels(cut, pair_dev - cut, target, rows, blocks, conduct, local_trials)
+    first = exchanged(1, first)
+    second = exchanged(0, second)
+    second = exchanged(1, second)
+    summed = contributions(0, places, blocks, local_trials, first)
+    summed = contributions(cut, places, blocks, local_trials, second, (summed,))
     half = owners // 2
     other = lax.ppermute(summed[half:], "pb", [(i, i ^ 1) for i in range(owners)])
     groups = [list(range(c, owners, 2)) for c in range(2)]

time: 291 us -> 285 us (0.979)
  Pallas kernels: 62.3 us -> 56.8 us
    pallas_call x4 -> x2, Pallas kernels: 29.4 us -> 23.9 us  [pair_kernels(): pl.pallas_call(lambda *refs: pair_body(skip, *refs), out_shape=[jax.Shape...]
  transfers between devices with their start and end apart: 14 -> 14, of which waited for: 8 -> 8; matrix products, arithmetic and copies ran while one was open for 5% -> 5% of each run, Pallas kernels for 16% -> 11%
where the time goes in v6:
time: 285 us; the launch traced here: 281 us
  waiting for transfers between devices  159 us (56%)
  Pallas kernels  56.8 us (20%)
  blocking collectives  19.2 us (7%)
  between operations  13.5 us (5%)
  starting transfers between devices  12.9 us (5%)
  other arithmetic  10.8 us (4%)
  local copies, waits for them, and re-layouts  8.42 us (3%)
    ppermute x3, waiting for transfers between devices, compute(): rows.append(lax.ppermute(rows[-1], 'ka', ahead))  113 us
    pallas_call x2, Pallas kernels, pair_kernels(): pl.pallas_call(lambda *refs: pair_body(skip, *refs), out_shape=[jax.Shape...  23.9 us
    ppermute x8, waiting for transfers between devices, exchanged(): lax.ppermute(x, 'ka', turns[(i + number) % 2])  20.8 us
    pallas_call x1, Pallas kernels, prepare(): pl.pallas_call(prepare_body, out_shape=tuple((jax.ShapeDtypeStruct(shape,...  20.2 us
    all_to_all x1, blocking collectives, compute(): lax.all_to_all(summed[:half] + other, 'pb', split_axis=0, concat_axis=0,...  19.2 us
    ppermute x1, waiting for transfers between devices, compute(): conduct_next = lax.ppermute(conduct.astype(F32), 'ka', back)  12.4 us
    all_gather x1, waiting for transfers between devices, compute(): lax.all_gather(pack(here, own_trials, jnp.asarray(spread), screened, ka),...  11.9 us
    pallas_call x2, Pallas kernels, contributions(): pl.pallas_call(lambda *refs: response_body(start, counts, *refs), out_sha...  10.5 us
  transfers between devices with their start and end apart: 14, of which 8 were waited for; matrix products, arithmetic and copies ran while one was open for 5% of the time, Pallas kernels for 11%

profile of v6, /device:TPU:1, one launch (start us, length us, event | category | flops | bytes accessed | tf_op | source)
XLA Modules:
  0.0 280.8 jit_solution(8693791654672610562)
XLA Ops:
  6.5 0.0 copy-start
  6.5 0.8 reduce
  7.3 0.7 reshape.26.trial_ref
  8.0 2.2 shard_map.83
  10.2 0.0 all-gather.3.cloned.1.call-update
  10.2 3.7 %reshape.24 = bf16[26,14,14,256]{3,2,1,0:T(8,128)(2,1)S(1)} reshape(bf16[26,196,256]{2,1,0:T(8,128)(2,1)} %param.11) | data formatting | bytes 5218304 | tf_op jit(solution)/shard_map/reshape | solution.py:244
  13.9 0.5 pad.4
  14.3 0.0 copy-start.3
  14.4 0.0 copy-start.9
  14.4 3.4 %bitcast_convert_fusion = f32[26,224,256]{2,1,0:T(8,128)} fusion(bf16[26,14,16,256]{3,2,1,0:T(8,128)(2,1)S(1)} %pad.4), kind=kLoop, calls=%fused_computation.27 | loop fusion | flops 1490944 | bytes 8945664 | tf_op jit(solution)/shard_map/convert_element_type | solution.py:246
  17.8 0.1 copy-done.2
  17.9 3.6 %collective-permute-start.3 = (f32[26,224,256]{2,1,0:T(8,128)}, f32[26,224,256]{2,1,0:T(8,128)}, u32[]{:S(2)}, u32[]{:S(2)}) collective-permute-start(f32[26,224,256]{2,1,0:T(8,128)} %bitcast_convert_fusion), channel_id=1, source_target_pairs={{1,0},{2,1},{3,2},{0,3},{5,4},{6,5},{7,6},{4,7},{9,8},{10,9},{11,1... | collective-permute-start | bytes 17891336 | tf_op jit(solution)/shard_map/ppermute | solution.py:246
  21.5 0.0 copy-done.3
  21.5 0.0 collective-permute-start
  21.5 39.1 %collective-permute-done.refs_1_.refs_5_.refs_9_ = f32[26,16,1024]{2,1,0:T(8,128)S(1)} collective-permute-done((f32[26,16,1024]{2,1,0:T(8,128)S(1)}, f32[26,16,1024]{2,1,0:T(8,128)S(1)}, u32[]{:S(2)}, u32[]{:S(2)}) %collective-permute-start) | collective-permute-done | bytes 1703968 | tf_op jit(solution)/shard_map/ppermute | solution.py:249
  60.6 0.0 collective-permute-start.1
  60.6 38.4 %collective-permute-done.1.refs_2_.refs_6_.refs_10_ = f32[26,16,1024]{2,1,0:T(8,128)S(1)} collective-permute-done((f32[26,16,1024]{2,1,0:T(8,128)S(1)}, f32[26,16,1024]{2,1,0:T(8,128)S(1)}, u32[]{:S(2)}, u32[]{:S(2)}) %collective-permute-start.1) | collective-permute-done | bytes 1703968 | tf_op jit(solution)/shard_map/ppermute | solution.py:249
  99.0 0.0 collective-permute-start.2
  99.0 0.7 gather_fusion.1
  99.7 0.5 fusion.5
  100.3 0.7 gather_fusion
  101.0 0.6 fusion.2
  101.6 35.0 %collective-permute-done.2.refs_3_.refs_7_.refs_11_ = f32[26,16,1024]{2,1,0:T(8,128)} collective-permute-done((f32[26,16,1024]{2,1,0:T(8,128)S(1)}, f32[26,16,1024]{2,1,0:T(8,128)}, u32[]{:S(2)}, u32[]{:S(2)}) %collective-permute-start.2) | collective-permute-done | bytes 1703968 | tf_op jit(solution)/shard_map/ppermute | solution.py:249
  136.6 12.4 %collective-permute-done.3.refs_13_ = f32[26,224,256]{2,1,0:T(8,128)} collective-permute-done((f32[26,224,256]{2,1,0:T(8,128)}, f32[26,224,256]{2,1,0:T(8,128)}, u32[]{:S(2)}, u32[]{:S(2)}) %collective-permute-start.3) | collective-permute-done | bytes 5963808 | tf_op jit(solution)/shard_map/ppermute | solution.py:246
  149.0 0.0 copy-done.4
  149.0 20.2 %shard_map.82 = (bf16[26,128,768]{2,1,0:T(8,128)(2,1)}, bf16[26,224,512]{2,1,0:T(8,128)(2,1)}) custom-call(s32[1]{0:T(128)} %bitcast.ka_ref, f32[26,16,1024]{2,1,0:T(8,128)} %refs_8_.1, f32[26,16,1024]{2,1,0:T(8,128)} %copy-done.4, f32[26,16,1024]{2,1,0:T(8,128)} %copy-done.5, f32[26,16,1024]{2,1,0:T(8,128)} %collective-permute-done.2.refs_3_.refs_7_.refs_11_, ...), custom_call_target="tpu_custom_call" | custom-call | bytes 17039360 | tf_op jit(solution)/shard_map/pallas_call | solution.py:108
  169.2 11.9 %all-gather.3.cloned.1.call-done = f32[84480,128]{1,0:T(8,128)} async-done(((f32[1320,128]{1,0:T(8,128)}), f32[84480,128]{1,0:T(8,128)}) %all-gather.3.cloned.1.call-update) | async-done | bytes 43253776 | tf_op jit(solution)/shard_map/all_gather | solution.py:240
  181.1 12.7 %shard_map.85 = (f32[7,112,128]{2,1,0:T(8,128)}, f32[7,112,128]{2,1,0:T(8,128)}) custom-call(s32[26]{0:T(128)} %bitcast.25, bf16[26,128,768]{2,1,0:T(8,128)(2,1)} %get-tuple-element.24.refs_1_, f32[64,1320,128]{2,1,0:T(8,128)} %bitcast.17, f32[64,1320,128]{2,1,0:T(8,128)} %bitcast.18, bf16[26,224,512]{2,1,0:T(8,128)(2,1)} %get-tuple-element.25.refs_4_), custom_call_target="tpu_custom_call" | custom-call | flops 1400000000 | bytes 15400000 | tf_op jit(solution)/shard_map/pallas_call | solution.py:174
  193.8 1.2 collective-permute-start.8
  195.0 1.8 collective-permute-start.10
  196.8 11.2 %shard_map.84 = (f32[6,112,128]{2,1,0:T(8,128)}, f32[6,112,128]{2,1,0:T(8,128)}) custom-call(s32[26]{0:T(128)} %bitcast.26, bf16[26,128,768]{2,1,0:T(8,128)(2,1)} %get-tuple-element.24.refs_1_, f32[64,1320,128]{2,1,0:T(8,128)} %bitcast.19, f32[64,1320,128]{2,1,0:T(8,128)} %bitcast.20, bf16[26,224,512]{2,1,0:T(8,128)(2,1)} %get-tuple-element.25.refs_4_), custom_call_target="tpu_custom_call" | custom-call | flops 1200000000 | bytes 13200000 | tf_op jit(solution)/shard_map/pallas_call | solution.py:174
  208.0 0.4 collective-permute-start.4
  208.3 0.7 collective-permute-start.6
  209.1 0.0 collective-permute-done.8
  209.1 0.0 copy-done.7
  209.1 0.1 add.59
  209.2 2.0 collective-permute-start.9
  211.2 0.0 collective-permute-done.10
  211.2 0.1 add.61
  211.3 0.1 collective-permute-start.11
  211.4 5.7 %collective-permute-done.4 = f32[6,112,128]{2,1,0:T(8,128)S(1)} collective-permute-done((f32[6,112,128]{2,1,0:T(8,128)}, f32[6,112,128]{2,1,0:T(8,128)S(1)}, u32[]{:S(2)}, u32[]{:S(2)}) %collective-permute-start.4) | collective-permute-done | bytes 344096 | tf_op jit(solution)/shard_map/ppermute | solution.py:265
  217.0 1.0 add.55
  218.1 1.0 collective-permute-start.5
  219.0 0.0 collective-permute-done.6
  219.0 0.0 copy-done.8
  219.1 0.1 collective-permute-start.7
  219.2 15.1 %collective-permute-done.5 = f32[6,112,128]{2,1,0:T(8,128)S(1)} collective-permute-done((f32[6,112,128]{2,1,0:T(8,128)S(1)}, f32[6,112,128]{2,1,0:T(8,128)S(1)}, u32[]{:S(2)}, u32[]{:S(2)}) %collective-permute-start.5) | collective-permute-done | bytes 344096 | tf_op jit(solution)/shard_map/ppermute | solution.py:265
  234.3 0.8 add.56.refs_5_
  235.0 0.0 collective-permute-done.7
  235.0 0.8 add.58.refs_6_
  235.8 0.0 collective-permute-done.9
  235.8 0.8 add.60.refs_5_
  236.6 0.0 collective-permute-done.11
  236.6 0.8 add.62.refs_6_
  237.4 5.3 %shard_map.86.refs_7_ = f32[64,32,128]{2,1,0:T(8,128)} custom-call(s32[26]{0:T(128)} %get-tuple-element.20.refs_0_, s32[26]{0:T(128)} %get-tuple-element.21.refs_1_, s32[26]{0:T(128)} %get-tuple-element.22.refs_2_, s32[26]{0:T(128)} %get-tuple-element.23.refs_3_, f32[64,1320,128]{2,1,0:T(8,128)} %bitcast.21, f32[7,112,128]{2,1,0:T(8,128)} %add.60.refs_5_, ...), custom_call_target="tpu_custom_call" | custom-call | flops 140000000 | bytes 4000000 | tf_op jit(solution)/shard_map/pallas_call | solution.py:219
  242.7 5.2 %shard_map.87 = f32[64,32,128]{2,1,0:T(8,128)} custom-call(s32[26]{0:T(128)} %get-tuple-element.20.refs_0_, s32[26]{0:T(128)} %get-tuple-element.21.refs_1_, s32[26]{0:T(128)} %get-tuple-element.22.refs_2_, s32[26]{0:T(128)} %get-tuple-element.23.refs_3_, f32[64,1320,128]{2,1,0:T(8,128)} %bitcast.22, f32[6,112,128]{2,1,0:T(8,128)} %add.56.refs_5_, ...), custom_call_target="tpu_custom_call" | custom-call | flops 120000000 | bytes 4000000 | tf_op jit(solution)/shard_map/pallas_call | solution.py:219
  247.9 1.1 slice.25
  249.0 2.0 collective-permute-start.12
  251.0 1.5 collective-permute-done.12
  252.6 1.1 slice_add_fusion
  253.7 19.2 %all_to_all.5 = f32[32,32,128]{2,1,0:T(8,128)S(1)} all-to-all(f32[32,32,128]{2,1,0:T(8,128)S(1)} %slice_add_fusion), channel_id=1, replica_groups={{0,8,16,24,32,40,48,56,64,72,80,88,96,104,112,120,128,136,144,152,160,1..., dimensions={0} | all-to-all | bytes 1048576 | tf_op jit(solution)/shard_map/all_to_all | solution.py:278
  273.0 0.1 copy.10
  273.1 0.1 copy.11
  273.2 0.8 reshape.28
  (18 shorter events, 0.1 us)
Async XLA Ops:
  6.5 92.5 %copy-start = (s32[64]{0:T(128)S(1)}, s32[64]{0:T(128)}, u32[]{:S(2)}) copy-start(s32[64]{0:T(128)} %param.15) | copy-start | bytes 772
  6.5 174.6 %all-gather.3.cloned.1.call-start = ((), (), s32[]{:S(2)}) async-start(), calls=%async_computation.1 | async-start | bytes 43929600 | tf_op jit(solution)/shard_map/all_gather | solution.py:240
  14.3 3.6 %copy-start.2 = (bf16[26,14,16,256]{3,2,1,0:T(8,128)(2,1)}, bf16[26,14,16,256]{3,2,1,0:T(8,128)(2,1)S(1)}, u32[]{:S(2)}) copy-start(bf16[26,14,16,256]{3,2,1,0:T(8,128)(2,1)S(1)} %pad.4) | copy-start | bytes 8945668
  14.3 7.1 %copy-start.3 = (f32[26,16,1024]{2,1,0:T(8,128)S(1)}, f32[26,16,1024]{2,1,0:T(8,128)}, u32[]{:S(2)}) copy-start(f32[26,16,1024]{2,1,0:T(8,128)} %refs_8_.1) | copy-start | bytes 5111812
  14.4 84.6 %copy-start.9 = (s32[26,2]{0,1:T(2,128)S(1)}, s32[26,2]{0,1:T(2,128)}, u32[]{:S(2)}) copy-start(s32[26,2]{0,1:T(2,128)} %param.14) | copy-start | bytes 628
  17.9 131.0 %collective-permute-start.3 = (f32[26,224,256]{2,1,0:T(8,128)}, f32[26,224,256]{2,1,0:T(8,128)}, u32[]{:S(2)}, u32[]{:S(2)}) collective-permute-start(f32[26,224,256]{2,1,0:T(8,128)} %bitcast_convert_fusion), channel_id=1, source_target_pairs={{1,0},{2,1},{3,2},{0,3},{5,4},{6,5},{7,6},{4,7},{9,8},{10,9},{11,1... | collective-permute-start | bytes 17891336 | tf_op jit(solution)/shard_map/ppermute | solution.py:246
  21.5 39.1 %collective-permute-start = (f32[26,16,1024]{2,1,0:T(8,128)S(1)}, f32[26,16,1024]{2,1,0:T(8,128)S(1)}, u32[]{:S(2)}, u32[]{:S(2)}) collective-permute-start(f32[26,16,1024]{2,1,0:T(8,128)S(1)} %copy-done.3), channel_id=1, source_target_pairs={{0,1},{1,2},{2,3},{3,0},{4,5},{5,6},{6,7},{7,4},{8,9},{9,10},{10,1... | collective-permute-start | bytes 5111816 | tf_op jit(solution)/shard_map/ppermute | solution.py:249
  60.6 88.4 %copy-start.4 = (f32[26,16,1024]{2,1,0:T(8,128)}, f32[26,16,1024]{2,1,0:T(8,128)S(1)}, u32[]{:S(2)}) copy-start(f32[26,16,1024]{2,1,0:T(8,128)S(1)} %collective-permute-done.refs_1_.refs_5_.refs_9_) | copy-start | bytes 5111812
  60.6 38.4 %collective-permute-start.1 = (f32[26,16,1024]{2,1,0:T(8,128)S(1)}, f32[26,16,1024]{2,1,0:T(8,128)S(1)}, u32[]{:S(2)}, u32[]{:S(2)}) collective-permute-start(f32[26,16,1024]{2,1,0:T(8,128)S(1)} %collective-permute-done.refs_1_.refs_5_.refs_9_), channel_id=1, source_target_pairs={{0,1},{1,2},{2,3},{3,0},{4,5},{5,6},{6,7},{7,4},{8,9},{9,10},{10,1... | collective-permute-start | bytes 5111816 | tf_op jit(solution)/shard_map/ppermute | solution.py:249
  99.0 50.0 %copy-start.5 = (f32[26,16,1024]{2,1,0:T(8,128)}, f32[26,16,1024]{2,1,0:T(8,128)S(1)}, u32[]{:S(2)}) copy-start(f32[26,16,1024]{2,1,0:T(8,128)S(1)} %collective-permute-done.1.refs_2_.refs_6_.refs_10_) | copy-start | bytes 5111812
  99.0 37.6 %collective-permute-start.2 = (f32[26,16,1024]{2,1,0:T(8,128)S(1)}, f32[26,16,1024]{2,1,0:T(8,128)}, u32[]{:S(2)}, u32[]{:S(2)}) collective-permute-start(f32[26,16,1024]{2,1,0:T(8,128)S(1)} %collective-permute-done.1.refs_2_.refs_6_.refs_10_), channel_id=1, source_target_pairs={{0,1},{1,2},{2,3},{3,0},{4,5},{5,6},{6,7},{7,4},{8,9},{9,10},{10,1... | collective-permute-start | bytes 5111816 | tf_op jit(solution)/shard_map/ppermute | solution.py:249
  193.8 15.3 %collective-permute-start.8 = (f32[7,112,128]{2,1,0:T(8,128)}, f32[7,112,128]{2,1,0:T(8,128)S(1)}, u32[]{:S(2)}, u32[]{:S(2)}) collective-permute-start(f32[7,112,128]{2,1,0:T(8,128)} %get-tuple-element.28), channel_id=1, source_target_pairs={{0,1},{1,0},{2,3},{3,2},{4,5},{5,4},{6,7},{7,6},{8,9},{9,8},{10,11... | collective-permute-start | bytes 1204232 | tf_op jit(solution)/shard_map/ppermute | solution.py:265
  195.0 14.1 %copy-start.7 = (f32[7,112,128]{2,1,0:T(8,128)S(1)}, f32[7,112,128]{2,1,0:T(8,128)}, u32[]{:S(2)}) copy-start(f32[7,112,128]{2,1,0:T(8,128)} %get-tuple-element.28) | copy-start | bytes 1204228
  195.0 16.2 %copy-start.6 = (f32[7,112,128]{2,1,0:T(8,128)S(1)}, f32[7,112,128]{2,1,0:T(8,128)}, u32[]{:S(2)}) copy-start(f32[7,112,128]{2,1,0:T(8,128)} %get-tuple-element.29) | copy-start | bytes 1204228
  195.0 16.2 %collective-permute-start.10 = (f32[7,112,128]{2,1,0:T(8,128)}, f32[7,112,128]{2,1,0:T(8,128)S(1)}, u32[]{:S(2)}, u32[]{:S(2)}) collective-permute-start(f32[7,112,128]{2,1,0:T(8,128)} %get-tuple-element.29), channel_id=1, source_target_pairs={{0,3},{1,2},{2,1},{3,0},{4,7},{5,6},{6,5},{7,4},{8,11},{9,10},{10,... | collective-permute-start | bytes 1204232 | tf_op jit(solution)/shard_map/ppermute | solution.py:265
  208.0 11.0 %copy-start.8 = (f32[6,112,128]{2,1,0:T(8,128)S(1)}, f32[6,112,128]{2,1,0:T(8,128)}, u32[]{:S(2)}) copy-start(f32[6,112,128]{2,1,0:T(8,128)} %get-tuple-element.27) | copy-start | bytes 1032196
  208.0 9.1 %collective-permute-start.4 = (f32[6,112,128]{2,1,0:T(8,128)}, f32[6,112,128]{2,1,0:T(8,128)S(1)}, u32[]{:S(2)}, u32[]{:S(2)}) collective-permute-start(f32[6,112,128]{2,1,0:T(8,128)} %get-tuple-element.26), channel_id=1, source_target_pairs={{0,1},{1,0},{2,3},{3,2},{4,5},{5,4},{6,7},{7,6},{8,9},{9,8},{10,11... | collective-permute-start | bytes 1032200 | tf_op jit(solution)/shard_map/ppermute | solution.py:265
  208.3 10.7 %collective-permute-start.6 = (f32[6,112,128]{2,1,0:T(8,128)}, f32[6,112,128]{2,1,0:T(8,128)S(1)}, u32[]{:S(2)}, u32[]{:S(2)}) collective-permute-start(f32[6,112,128]{2,1,0:T(8,128)} %get-tuple-element.27), channel_id=1, source_target_pairs={{0,3},{1,2},{2,1},{3,0},{4,7},{5,6},{6,5},{7,4},{8,11},{9,10},{10,... | collective-permute-start | bytes 1032200 | tf_op jit(solution)/shard_map/ppermute | solution.py:265
  209.2 26.6 %collective-permute-start.9 = (f32[7,112,128]{2,1,0:T(8,128)S(1)}, f32[7,112,128]{2,1,0:T(8,128)S(1)}, u32[]{:S(2)}, u32[]{:S(2)}) collective-permute-start(f32[7,112,128]{2,1,0:T(8,128)S(1)} %add.59), channel_id=1, source_target_pairs={{0,3},{1,2},{2,1},{3,0},{4,7},{5,6},{6,5},{7,4},{8,11},{9,10},{10,... | collective-permute-start | bytes 1204232 | tf_op jit(solution)/shard_map/ppermute | solution.py:265
  211.3 25.3 %collective-permute-start.11 = (f32[7,112,128]{2,1,0:T(8,128)S(1)}, f32[7,112,128]{2,1,0:T(8,128)S(1)}, u32[]{:S(2)}, u32[]{:S(2)}) collective-permute-start(f32[7,112,128]{2,1,0:T(8,128)S(1)} %add.61), channel_id=1, source_target_pairs={{0,1},{1,0},{2,3},{3,2},{4,5},{5,4},{6,7},{7,6},{8,9},{9,8},{10,11... | collective-permute-start | bytes 1204232 | tf_op jit(solution)/shard_map/ppermute | solution.py:265
  218.1 16.2 %collective-permute-start.5 = (f32[6,112,128]{2,1,0:T(8,128)S(1)}, f32[6,112,128]{2,1,0:T(8,128)S(1)}, u32[]{:S(2)}, u32[]{:S(2)}) collective-permute-start(f32[6,112,128]{2,1,0:T(8,128)S(1)} %add.55), channel_id=1, source_target_pairs={{0,3},{1,2},{2,1},{3,0},{4,7},{5,6},{6,5},{7,4},{8,11},{9,10},{10,... | collective-permute-start | bytes 1032200 | tf_op jit(solution)/shard_map/ppermute | solution.py:265
  219.1 16.0 %collective-permute-start.7 = (f32[6,112,128]{2,1,0:T(8,128)S(1)}, f32[6,112,128]{2,1,0:T(8,128)S(1)}, u32[]{:S(2)}, u32[]{:S(2)}) collective-permute-start(f32[6,112,128]{2,1,0:T(8,128)S(1)} %add.57), channel_id=1, source_target_pairs={{0,1},{1,0},{2,3},{3,2},{4,5},{5,4},{6,7},{7,6},{8,9},{9,8},{10,11... | collective-permute-start | bytes 1032200 | tf_op jit(solution)/shard_map/ppermute | solution.py:265
  242.7 31.3 %copy-start.1 = (s32[64]{0:T(128)S(1)}, s32[64]{0:T(128)}, u32[]{:S(2)}) copy-start(s32[64]{0:T(128)} %param.15) | copy-start | bytes 772
  249.0 3.6 %collective-permute-start.12 = (f32[32,32,128]{2,1,0:T(8,128)S(1)}, f32[32,32,128]{2,1,0:T(8,128)S(1)}, u32[]{:S(2)}, u32[]{:S(2)}) collective-permute-start(f32[32,32,128]{2,1,0:T(8,128)S(1)} %slice.25), channel_id=1, source_target_pairs={{0,4},{4,0},{8,12},{12,8},{16,20},{20,16},{24,28},{28,24},{32,36},... | collective-permute-start | bytes 1572872 | tf_op jit(solution)/shard_map/ppermute | solution.py:276
Sparse Core Ops, SparseCore 0:
  10.3 170.7 all-gather.2

commit v7 on v6

--- a/solution.py
+++ b/solution.py
@@ -187,21 +187,23 @@
     )(momentum, rows, *([blocks] * PAIR), conduct)
 
 
-def response_body(start, counts, near_ref, far_ref, near_place_ref, far_place_ref, trial_ref, *refs):
-    kernels, (out_ref, turn_ref) = refs[: len(counts)], refs[-2:]
-    if len(refs) > len(counts) + 2:
-        out_ref[...] = refs[len(counts)][...]
+def response_body(bases, near_ref, far_ref, near_place_ref, far_place_ref, trial_ref, *refs):
+    kernels, (out_ref, turn_ref) = refs[: 2 * len(bases)], refs[-2:]
+    if len(refs) > 2 * len(bases) + 2:
+        out_ref[...] = refs[2 * len(bases)][...]
     else:
         out_ref[...] = jnp.zeros_like(out_ref)
     turn_ref[...] = jnp.zeros_like(turn_ref)
-    for number, (count, kernel_ref) in enumerate(zip(counts, kernels)):
-
-        @pl.loop(0, count)
-        def _(p, number=number, kernel_ref=kernel_ref):
-            pair = start + PAIR * p + number
+    for number, base in enumerate(bases):
+        own_ref, came_ref = kernels[2 * number : 2 * number + 2]
+
+        @pl.loop(0, own_ref.shape[0])
+        def _(p, base=base, own_ref=own_ref, came_ref=came_ref):
+            pair = base + PAIR * p
             near, far = near_ref[pair], far_ref[pair]
             for v in range(VB):
-                turn_ref[v * CD : v * CD + CB, :] = kernel_ref[p, pl.ds(v, CB, stride=VB), :]
+                rows = pl.ds(v, CB, stride=VB)
+                turn_ref[v * CD : v * CD + CB, :] = own_ref[p, rows, :] + came_ref[p, rows, :]
             kernel = turn_ref[...]
             direct = mul3(trial_ref[far], kernel, TURNED)
             mirror = mul3(trial_ref[near], kernel, PLAIN)
@@ -210,20 +212,20 @@
             out_ref[far] = out_ref[far] + mirror
 
 
-def contributions(start, places, blocks, trials, kernels, before=()):
-    counts = [kernel.shape[0] for kernel in kernels]
+def contributions(bases, places, blocks, trials, kernels, before=()):
+    pairs = sum(kernel.shape[0] for kernel in kernels) // 2
     shape = (blocks.shape[0], trials, VC)
     whole = [pl.BlockSpec(x.shape, lambda g: (0, 0, 0)) for x in kernels]
     result = pl.BlockSpec(shape, lambda g: (0, 0, 0))
     scalar = pl.BlockSpec(memory_space=pltpu.SMEM)
     return pl.pallas_call(
-        lambda *refs: response_body(start, counts, *refs),
+        lambda *refs: response_body(bases, *refs),
         out_shape=jax.ShapeDtypeStruct(shape, F32),
         grid=(1,),
         in_specs=[scalar] * len(places) + [result, *whole] + [result] * len(before),
         out_specs=result,
         scratch_shapes=[pltpu.VMEM((VC, VC), F32)],
-        cost_estimate=pl.CostEstimate(flops=sum(counts) * 10**7, bytes_accessed=4 * 10**6, transcendentals=0),
+        cost_estimate=pl.CostEstimate(flops=pairs * 10**7, bytes_accessed=4 * 10**6, transcendentals=0),
     )(*places, blocks, *kernels, *before)
 
 
@@ -259,19 +261,22 @@
     fold = [(i, ka - 1 - i) for i in range(ka)]
     target = momentum[:, 0]
     turns = (swap, fold)
-    cut = -(-pair_dev // (2 * PAIR)) * PAIR
-
-    def exchanged(number, first):
-        return [x + lax.ppermute(x, "ka", turns[(i + number) % 2]) for i, x in enumerate(first)]
-
-    first = pair_kernels(0, cut, target, rows, blocks, conduct, local_trials)
-    first = exchanged(0, first)
-    second = pair_kernels(cut, pair_dev - cut, target, rows, blocks, conduct, local_trials)
-    first = exchanged(1, first)
-    second = exchanged(0, second)
-    second = exchanged(1, second)
-    summed = contributions(0, places, blocks, local_trials, first)
-    summed = contributions(cut, places, blocks, local_trials, second, (summed,))
+    each = -(-3 * pair_dev // (8 * PAIR)) * PAIR
+    starts = [0, each, 2 * each]
+    sizes = [each, each, pair_dev - 2 * each]
+
+    def twice(kernels):
+        came = [lax.ppermute(x, "ka", turns[1 - i % 2]) for i, x in enumerate(kernels)]
+        return [x for both in zip(kernels, came) for x in both]
+
+    calls = []
+    for call in range(3):
+        kernels = pair_kernels(starts[call], sizes[call], target, rows, blocks, conduct, local_trials)
+        calls.append([x + lax.ppermute(x, "ka", turns[i % 2]) for i, x in enumerate(kernels)])
+    calls = [twice(kernels) for kernels in calls]
+    bases = [[start + i for i in range(PAIR)] for start in starts]
+    summed = contributions(bases[0] + bases[1], places, blocks, local_trials, calls[0] + calls[1])
+    summed = contributions(bases[2], places, blocks, local_trials, calls[2], (summed,))
     half = owners // 2
     other = lax.ppermute(summed[half:], "pb", [(i, i ^ 1) for i in range(owners)])
     groups = [list(range(c, owners, 2)) for c in range(2)]

time: 285 us -> 284 us (level)
  waiting for transfers between devices: 159 us -> 148 us
  starting transfers between devices: 12.9 us -> 20.7 us
  other arithmetic: 10.8 us -> 6.68 us
  Pallas kernels: 56.8 us -> 60.2 us
    ppermute x8 -> x12, waiting for transfers between devices: 20.8 us -> 9.78 us  [the longest x6 5.62 us: compute(): lax.ppermute(x, 'ka', turns[i % 2])]
    ppermute x8 -> x12, starting transfers between devices: 7.3 us -> 12.7 us  [the longest x6 6.9 us: twice(): lax.ppermute(x, 'ka', turns[1 - i % 2])]
    add x8 -> x6, other arithmetic: 4.3 us -> 0.19 us  [compute(): x + lax.ppermute(x, 'ka', turns[i % 2])]
    pallas_call x2 -> x3, Pallas kernels: 23.9 us -> 26.6 us  [pair_kernels(): pl.pallas_call(lambda *refs: pair_body(skip, *refs), out_shape=[jax.Shape...]
  transfers between devices with their start and end apart: 14 -> 18, of which waited for: 8 -> 8; matrix products, arithmetic and copies ran while one was open for 5% -> 4% of each run, Pallas kernels for 11% -> 16%
where the time goes in v7:
time: 284 us; the launch traced here: 280 us
  waiting for transfers between devices  148 us (52%)
  Pallas kernels  60.2 us (21%)
  starting transfers between devices  20.7 us (7%)
  blocking collectives  19.2 us (7%)
  between operations  13.7 us (5%)
  local copies, waits for them, and re-layouts  11.2 us (4%)
  other arithmetic  6.68 us (2%)
    ppermute x3, waiting for transfers between devices, compute(): rows.append(lax.ppermute(rows[-1], 'ka', ahead))  113 us
    pallas_call x3, Pallas kernels, pair_kernels(): pl.pallas_call(lambda *refs: pair_body(skip, *refs), out_shape=[jax.Shape...  26.6 us
    pallas_call x1, Pallas kernels, prepare(): pl.pallas_call(prepare_body, out_shape=tuple((jax.ShapeDtypeStruct(shape,...  20.2 us
    all_to_all x1, blocking collectives, compute(): lax.all_to_all(summed[:half] + other, 'pb', split_axis=0, concat_axis=0,...  19.2 us
    ppermute x1, waiting for transfers between devices, compute(): conduct_next = lax.ppermute(conduct.astype(F32), 'ka', back)  12.4 us
    all_gather x1, waiting for transfers between devices, compute(): lax.all_gather(pack(here, own_trials, jnp.asarray(spread), screened, ka),...  11.8 us
    pallas_call x2, Pallas kernels, contributions(): pl.pallas_call(lambda *refs: response_body(bases, *refs), out_shape=jax.S...  11.2 us
    ppermute x6, starting transfers between devices, twice(): lax.ppermute(x, 'ka', turns[1 - i % 2])  6.9 us
  transfers between devices with their start and end apart: 18, of which 8 were waited for; matrix products, arithmetic and copies ran while one was open for 4% of the time, Pallas kernels for 16%

profile of v7, /device:TPU:1, one launch (start us, length us, event | category | flops | bytes accessed | tf_op | source)
XLA Modules:
  0.0 279.8 jit_solution(5464914861920431284)
XLA Ops:
  6.5 0.8 reduce
  7.3 0.7 reshape.26.trial_ref
  8.0 2.2 shard_map.83
  10.2 0.0 all-gather.3.cloned.1.call-update
  10.2 3.7 %reshape.24 = bf16[26,14,14,256]{3,2,1,0:T(8,128)(2,1)S(1)} reshape(bf16[26,196,256]{2,1,0:T(8,128)(2,1)} %param.11) | data formatting | bytes 5218304 | tf_op jit(solution)/shard_map/reshape | solution.py:246
  13.9 0.5 pad.4
  14.3 0.0 copy-start.3
  14.3 0.0 copy-start.24
  14.4 3.4 %bitcast_convert_fusion = f32[26,224,256]{2,1,0:T(8,128)} fusion(bf16[26,14,16,256]{3,2,1,0:T(8,128)(2,1)S(1)} %pad.4), kind=kLoop, calls=%fused_computation.27 | loop fusion | flops 1490944 | bytes 8945664 | tf_op jit(solution)/shard_map/convert_element_type | solution.py:248
  17.8 0.2 copy-done.2
  18.0 3.6 %collective-permute-start.3 = (f32[26,224,256]{2,1,0:T(8,128)}, f32[26,224,256]{2,1,0:T(8,128)}, u32[]{:S(2)}, u32[]{:S(2)}) collective-permute-start(f32[26,224,256]{2,1,0:T(8,128)} %bitcast_convert_fusion), channel_id=1, source_target_pairs={{1,0},{2,1},{3,2},{0,3},{5,4},{6,5},{7,6},{4,7},{9,8},{10,9},{11,1... | collective-permute-start | bytes 17891336 | tf_op jit(solution)/shard_map/ppermute | solution.py:248
  21.5 0.0 collective-permute-start
  21.5 39.1 %collective-permute-done.refs_1_.refs_5_.refs_9_ = f32[26,16,1024]{2,1,0:T(8,128)S(1)} collective-permute-done((f32[26,16,1024]{2,1,0:T(8,128)S(1)}, f32[26,16,1024]{2,1,0:T(8,128)S(1)}, u32[]{:S(2)}, u32[]{:S(2)}) %collective-permute-start) | collective-permute-done | bytes 1703968 | tf_op jit(solution)/shard_map/ppermute | solution.py:251
  60.6 0.0 collective-permute-start.1
  60.7 38.4 %collective-permute-done.1.refs_2_.refs_6_.refs_10_ = f32[26,16,1024]{2,1,0:T(8,128)S(1)} collective-permute-done((f32[26,16,1024]{2,1,0:T(8,128)S(1)}, f32[26,16,1024]{2,1,0:T(8,128)S(1)}, u32[]{:S(2)}, u32[]{:S(2)}) %collective-permute-start.1) | collective-permute-done | bytes 1703968 | tf_op jit(solution)/shard_map/ppermute | solution.py:251
  99.0 0.0 collective-permute-start.2
  99.1 0.7 gather_fusion.1
  99.8 0.6 fusion.5
  100.3 0.7 gather_fusion
  101.0 0.6 fusion.2
  101.6 35.0 %collective-permute-done.2.refs_3_.refs_7_.refs_11_ = f32[26,16,1024]{2,1,0:T(8,128)} collective-permute-done((f32[26,16,1024]{2,1,0:T(8,128)S(1)}, f32[26,16,1024]{2,1,0:T(8,128)}, u32[]{:S(2)}, u32[]{:S(2)}) %collective-permute-start.2) | collective-permute-done | bytes 1703968 | tf_op jit(solution)/shard_map/ppermute | solution.py:251
  136.6 12.4 %collective-permute-done.3.refs_13_ = f32[26,224,256]{2,1,0:T(8,128)} collective-permute-done((f32[26,224,256]{2,1,0:T(8,128)}, f32[26,224,256]{2,1,0:T(8,128)}, u32[]{:S(2)}, u32[]{:S(2)}) %collective-permute-start.3) | collective-permute-done | bytes 5963808 | tf_op jit(solution)/shard_map/ppermute | solution.py:248
  149.0 20.2 %shard_map.82 = (bf16[26,128,768]{2,1,0:T(8,128)(2,1)}, bf16[26,224,512]{2,1,0:T(8,128)(2,1)}) custom-call(s32[1]{0:T(128)} %bitcast.ka_ref, f32[26,16,1024]{2,1,0:T(8,128)} %refs_8_.1, f32[26,16,1024]{2,1,0:T(8,128)} %copy-done.4, f32[26,16,1024]{2,1,0:T(8,128)} %copy-done.5, f32[26,16,1024]{2,1,0:T(8,128)} %collective-permute-done.2.refs_3_.refs_7_.refs_11_, ...), custom_call_target="tpu_custom_call" | custom-call | bytes 17039360 | tf_op jit(solution)/shard_map/pallas_call | solution.py:108
  169.3 11.8 %all-gather.3.cloned.1.call-done = f32[84480,128]{1,0:T(8,128)} async-done(((f32[1320,128]{1,0:T(8,128)}), f32[84480,128]{1,0:T(8,128)}) %all-gather.3.cloned.1.call-update) | async-done | bytes 43253776 | tf_op jit(solution)/shard_map/all_gather | solution.py:242
  181.1 9.8 %shard_map.85 = (f32[5,112,128]{2,1,0:T(8,128)}, f32[5,112,128]{2,1,0:T(8,128)}) custom-call(s32[26]{0:T(128)} %bitcast.27, bf16[26,128,768]{2,1,0:T(8,128)(2,1)} %get-tuple-element.26.refs_1_, f32[64,1320,128]{2,1,0:T(8,128)} %bitcast.17, f32[64,1320,128]{2,1,0:T(8,128)} %bitcast.18, bf16[26,224,512]{2,1,0:T(8,128)(2,1)} %get-tuple-element.27.refs_4_), custom_call_target="tpu_custom_call" | custom-call | flops 1000000000 | bytes 11000000 | tf_op jit(solution)/shard_map/pallas_call | solution.py:174
  190.9 1.2 collective-permute-start.8
  192.1 1.8 collective-permute-start.10
  193.9 9.8 %shard_map.86 = (f32[5,112,128]{2,1,0:T(8,128)}, f32[5,112,128]{2,1,0:T(8,128)}) custom-call(s32[26]{0:T(128)} %bitcast.28, bf16[26,128,768]{2,1,0:T(8,128)(2,1)} %get-tuple-element.26.refs_1_, f32[64,1320,128]{2,1,0:T(8,128)} %bitcast.19, f32[64,1320,128]{2,1,0:T(8,128)} %bitcast.20, bf16[26,224,512]{2,1,0:T(8,128)(2,1)} %get-tuple-element.27.refs_4_), custom_call_target="tpu_custom_call" | custom-call | flops 1000000000 | bytes 11000000 | tf_op jit(solution)/shard_map/pallas_call | solution.py:174
  203.7 0.3 collective-permute-start.12
  204.0 0.7 collective-permute-start.14
  204.7 7.0 %shard_map.84 = (f32[3,112,128]{2,1,0:T(8,128)}, f32[3,112,128]{2,1,0:T(8,128)}) custom-call(s32[26]{0:T(128)} %bitcast.29, bf16[26,128,768]{2,1,0:T(8,128)(2,1)} %get-tuple-element.26.refs_1_, f32[64,1320,128]{2,1,0:T(8,128)} %bitcast.21, f32[64,1320,128]{2,1,0:T(8,128)} %bitcast.22, bf16[26,224,512]{2,1,0:T(8,128)(2,1)} %get-tuple-element.27.refs_4_), custom_call_target="tpu_custom_call" | custom-call | flops 600000000 | bytes 6600000 | tf_op jit(solution)/shard_map/pallas_call | solution.py:174
  211.7 0.9 collective-permute-start.4
  212.6 0.0 collective-permute-done.8
  212.6 1.9 collective-permute-start.9
  214.5 0.0 collective-permute-done.10
  214.5 0.9 collective-permute-start.6
  215.5 0.0 collective-permute-done.12
  215.5 0.3 collective-permute-start.11
  215.8 0.0 collective-permute-done.14
  215.8 1.9 collective-permute-start.13
  217.8 0.0 collective-permute-done.4
  217.8 0.9 collective-permute-start.15
  218.8 5.6 %collective-permute-done.6 = f32[3,112,128]{2,1,0:T(8,128)S(1)} collective-permute-done((f32[3,112,128]{2,1,0:T(8,128)}, f32[3,112,128]{2,1,0:T(8,128)S(1)}, u32[]{:S(2)}, u32[]{:S(2)}) %collective-permute-start.6) | collective-permute-done | bytes 172064 | tf_op jit(solution)/shard_map/ppermute | solution.py:275
  224.4 1.8 collective-permute-start.5
  226.2 0.0 collective-permute-done.9.refs_6_
  226.2 0.1 collective-permute-start.7
  226.3 0.0 collective-permute-done.11.refs_8_
  226.3 4.2 %collective-permute-done.13.refs_10_ = f32[5,112,128]{2,1,0:T(8,128)S(1)} collective-permute-done((f32[5,112,128]{2,1,0:T(8,128)S(1)}, f32[5,112,128]{2,1,0:T(8,128)S(1)}, u32[]{:S(2)}, u32[]{:S(2)}) %collective-permute-start.13) | collective-permute-done | bytes 286752 | tf_op jit(solution)/shard_map/ppermute | solution.py:269
  230.5 0.0 collective-permute-done.15.refs_12_
  230.6 0.7 copy-done.14
  231.2 0.7 copy-done.15
  231.9 7.1 %shard_map.87.refs_9_ = f32[64,32,128]{2,1,0:T(8,128)} custom-call(s32[26]{0:T(128)} %get-tuple-element.22.refs_0_, s32[26]{0:T(128)} %get-tuple-element.23.refs_1_, s32[26]{0:T(128)} %get-tuple-element.24.refs_2_, s32[26]{0:T(128)} %get-tuple-element.25.refs_3_, f32[64,1320,128]{2,1,0:T(8,128)} %bitcast.23, f32[5,112,128]{2,1,0:T(8,128)} %copy-done.6, ...), custom_call_target="tpu_custom_call" | custom-call | flops 200000000 | bytes 4000000 | tf_op jit(solution)/shard_map/pallas_call | solution.py:221
  239.1 0.0 collective-permute-done.5.refs_6_
  239.1 0.6 copy-done.20
  239.7 0.7 copy-done.21
  240.4 4.1 %shard_map.88 = f32[64,32,128]{2,1,0:T(8,128)} custom-call(s32[26]{0:T(128)} %get-tuple-element.22.refs_0_, s32[26]{0:T(128)} %get-tuple-element.23.refs_1_, s32[26]{0:T(128)} %get-tuple-element.24.refs_2_, s32[26]{0:T(128)} %get-tuple-element.25.refs_3_, f32[64,1320,128]{2,1,0:T(8,128)} %bitcast.24, f32[3,112,128]{2,1,0:T(8,128)} %copy-done.10, ...), custom_call_target="tpu_custom_call" | custom-call | flops 60000000 | bytes 4000000 | tf_op jit(solution)/shard_map/pallas_call | solution.py:221
  244.5 1.1 slice.25
  245.5 4.4 %collective-permute-start.16 = (f32[32,32,128]{2,1,0:T(8,128)S(1)}, f32[32,32,128]{2,1,0:T(8,128)S(1)}, u32[]{:S(2)}, u32[]{:S(2)}) collective-permute-start(f32[32,32,128]{2,1,0:T(8,128)S(1)} %slice.25), channel_id=1, source_target_pairs={{0,4},{4,0},{8,12},{12,8},{16,20},{20,16},{24,28},{28,24},{32,36},... | collective-permute-start | bytes 1572872 | tf_op jit(solution)/shard_map/ppermute | solution.py:281
  250.0 1.5 collective-permute-done.16
  251.5 1.1 slice_add_fusion
  252.6 19.2 %all_to_all.5 = f32[32,32,128]{2,1,0:T(8,128)S(1)} all-to-all(f32[32,32,128]{2,1,0:T(8,128)S(1)} %slice_add_fusion), channel_id=1, replica_groups={{0,8,16,24,32,40,48,56,64,72,80,88,96,104,112,120,128,136,144,152,160,1..., dimensions={0} | all-to-all | bytes 1048576 | tf_op jit(solution)/shard_map/all_to_all | solution.py:283
  271.9 0.1 copy.10
  272.0 0.1 copy.11
  272.2 0.8 reshape.28
  (55 shorter events, 0.3 us)
Async XLA Ops:
  6.5 92.5 %copy-start = (s32[64]{0:T(128)S(1)}, s32[64]{0:T(128)}, u32[]{:S(2)}) copy-start(s32[64]{0:T(128)} %param.15) | copy-start | bytes 772
  6.5 174.5 %all-gather.3.cloned.1.call-start = ((), (), s32[]{:S(2)}) async-start(), calls=%async_computation.1 | async-start | bytes 43929600 | tf_op jit(solution)/shard_map/all_gather | solution.py:242
  14.3 3.6 %copy-start.2 = (bf16[26,14,16,256]{3,2,1,0:T(8,128)(2,1)}, bf16[26,14,16,256]{3,2,1,0:T(8,128)(2,1)S(1)}, u32[]{:S(2)}) copy-start(bf16[26,14,16,256]{3,2,1,0:T(8,128)(2,1)S(1)} %pad.4) | copy-start | bytes 8945668
  14.3 7.2 %copy-start.3 = (f32[26,16,1024]{2,1,0:T(8,128)S(1)}, f32[26,16,1024]{2,1,0:T(8,128)}, u32[]{:S(2)}) copy-start(f32[26,16,1024]{2,1,0:T(8,128)} %refs_8_.1) | copy-start | bytes 5111812
  14.3 84.7 %copy-start.24 = (s32[26,2]{0,1:T(2,128)S(1)}, s32[26,2]{0,1:T(2,128)}, u32[]{:S(2)}) copy-start(s32[26,2]{0,1:T(2,128)} %param.14) | copy-start | bytes 628
  18.0 131.0 %collective-permute-start.3 = (f32[26,224,256]{2,1,0:T(8,128)}, f32[26,224,256]{2,1,0:T(8,128)}, u32[]{:S(2)}, u32[]{:S(2)}) collective-permute-start(f32[26,224,256]{2,1,0:T(8,128)} %bitcast_convert_fusion), channel_id=1, source_target_pairs={{1,0},{2,1},{3,2},{0,3},{5,4},{6,5},{7,6},{4,7},{9,8},{10,9},{11,1... | collective-permute-start | bytes 17891336 | tf_op jit(solution)/shard_map/ppermute | solution.py:248
  21.5 39.1 %collective-permute-start = (f32[26,16,1024]{2,1,0:T(8,128)S(1)}, f32[26,16,1024]{2,1,0:T(8,128)S(1)}, u32[]{:S(2)}, u32[]{:S(2)}) collective-permute-start(f32[26,16,1024]{2,1,0:T(8,128)S(1)} %copy-done.3), channel_id=1, source_target_pairs={{0,1},{1,2},{2,3},{3,0},{4,5},{5,6},{6,7},{7,4},{8,9},{9,10},{10,1... | collective-permute-start | bytes 5111816 | tf_op jit(solution)/shard_map/ppermute | solution.py:251
  60.6 88.4 %copy-start.4 = (f32[26,16,1024]{2,1,0:T(8,128)}, f32[26,16,1024]{2,1,0:T(8,128)S(1)}, u32[]{:S(2)}) copy-start(f32[26,16,1024]{2,1,0:T(8,128)S(1)} %collective-permute-done.refs_1_.refs_5_.refs_9_) | copy-start | bytes 5111812
  60.6 38.4 %collective-permute-start.1 = (f32[26,16,1024]{2,1,0:T(8,128)S(1)}, f32[26,16,1024]{2,1,0:T(8,128)S(1)}, u32[]{:S(2)}, u32[]{:S(2)}) collective-permute-start(f32[26,16,1024]{2,1,0:T(8,128)S(1)} %collective-permute-done.refs_1_.refs_5_.refs_9_), channel_id=1, source_target_pairs={{0,1},{1,2},{2,3},{3,0},{4,5},{5,6},{6,7},{7,4},{8,9},{9,10},{10,1... | collective-permute-start | bytes 5111816 | tf_op jit(solution)/shard_map/ppermute | solution.py:251
  99.0 50.0 %copy-start.5 = (f32[26,16,1024]{2,1,0:T(8,128)}, f32[26,16,1024]{2,1,0:T(8,128)S(1)}, u32[]{:S(2)}) copy-start(f32[26,16,1024]{2,1,0:T(8,128)S(1)} %collective-permute-done.1.refs_2_.refs_6_.refs_10_) | copy-start | bytes 5111812
  99.0 37.6 %collective-permute-start.2 = (f32[26,16,1024]{2,1,0:T(8,128)S(1)}, f32[26,16,1024]{2,1,0:T(8,128)}, u32[]{:S(2)}, u32[]{:S(2)}) collective-permute-start(f32[26,16,1024]{2,1,0:T(8,128)S(1)} %collective-permute-done.1.refs_2_.refs_6_.refs_10_), channel_id=1, source_target_pairs={{0,1},{1,2},{2,3},{3,0},{4,5},{5,6},{6,7},{7,4},{8,9},{9,10},{10,1... | collective-permute-start | bytes 5111816 | tf_op jit(solution)/shard_map/ppermute | solution.py:251
  190.9 21.7 %collective-permute-start.8 = (f32[5,112,128]{2,1,0:T(8,128)}, f32[5,112,128]{2,1,0:T(8,128)S(1)}, u32[]{:S(2)}, u32[]{:S(2)}) collective-permute-start(f32[5,112,128]{2,1,0:T(8,128)} %get-tuple-element.30), channel_id=1, source_target_pairs={{0,1},{1,0},{2,3},{3,2},{4,5},{5,4},{6,7},{7,6},{8,9},{9,8},{10,11... | collective-permute-start | bytes 860168 | tf_op jit(solution)/shard_map/ppermute | solution.py:275
  192.1 22.5 %collective-permute-start.10 = (f32[5,112,128]{2,1,0:T(8,128)}, f32[5,112,128]{2,1,0:T(8,128)S(1)}, u32[]{:S(2)}, u32[]{:S(2)}) collective-permute-start(f32[5,112,128]{2,1,0:T(8,128)} %get-tuple-element.31), channel_id=1, source_target_pairs={{0,3},{1,2},{2,1},{3,0},{4,7},{5,6},{6,5},{7,4},{8,11},{9,10},{10,... | collective-permute-start | bytes 860168 | tf_op jit(solution)/shard_map/ppermute | solution.py:275
  203.7 11.8 %collective-permute-start.12 = (f32[5,112,128]{2,1,0:T(8,128)}, f32[5,112,128]{2,1,0:T(8,128)S(1)}, u32[]{:S(2)}, u32[]{:S(2)}) collective-permute-start(f32[5,112,128]{2,1,0:T(8,128)} %get-tuple-element.32), channel_id=1, source_target_pairs={{0,1},{1,0},{2,3},{3,2},{4,5},{5,4},{6,7},{7,6},{8,9},{9,8},{10,11... | collective-permute-start | bytes 860168 | tf_op jit(solution)/shard_map/ppermute | solution.py:275
  204.0 8.6 %copy-start.19 = (f32[5,112,128]{2,1,0:T(8,128)S(1)}, f32[5,112,128]{2,1,0:T(8,128)}, u32[]{:S(2)}) copy-start(f32[5,112,128]{2,1,0:T(8,128)} %get-tuple-element.30) | copy-start | bytes 860164
  204.0 11.4 %copy-start.17 = (f32[5,112,128]{2,1,0:T(8,128)S(1)}, f32[5,112,128]{2,1,0:T(8,128)}, u32[]{:S(2)}) copy-start(f32[5,112,128]{2,1,0:T(8,128)} %get-tuple-element.31) | copy-start | bytes 860164
  204.0 11.8 %copy-start.18 = (f32[5,112,128]{2,1,0:T(8,128)S(1)}, f32[5,112,128]{2,1,0:T(8,128)}, u32[]{:S(2)}) copy-start(f32[5,112,128]{2,1,0:T(8,128)} %get-tuple-element.32) | copy-start | bytes 860164
  204.0 13.7 %copy-start.16 = (f32[5,112,128]{2,1,0:T(8,128)S(1)}, f32[5,112,128]{2,1,0:T(8,128)}, u32[]{:S(2)}) copy-start(f32[5,112,128]{2,1,0:T(8,128)} %get-tuple-element.33) | copy-start | bytes 860164
  204.0 11.8 %collective-permute-start.14 = (f32[5,112,128]{2,1,0:T(8,128)}, f32[5,112,128]{2,1,0:T(8,128)S(1)}, u32[]{:S(2)}, u32[]{:S(2)}) collective-permute-start(f32[5,112,128]{2,1,0:T(8,128)} %get-tuple-element.33), channel_id=1, source_target_pairs={{0,3},{1,2},{2,1},{3,0},{4,7},{5,6},{6,5},{7,4},{8,11},{9,10},{10,... | collective-permute-start | bytes 860168 | tf_op jit(solution)/shard_map/ppermute | solution.py:275
  211.7 7.0 %copy-start.23 = (f32[3,112,128]{2,1,0:T(8,128)S(1)}, f32[3,112,128]{2,1,0:T(8,128)}, u32[]{:S(2)}) copy-start(f32[3,112,128]{2,1,0:T(8,128)} %get-tuple-element.28) | copy-start | bytes 516100
  211.7 14.5 %copy-start.22 = (f32[3,112,128]{2,1,0:T(8,128)S(1)}, f32[3,112,128]{2,1,0:T(8,128)}, u32[]{:S(2)}) copy-start(f32[3,112,128]{2,1,0:T(8,128)} %get-tuple-element.29) | copy-start | bytes 516100
  211.7 6.1 %collective-permute-start.4 = (f32[3,112,128]{2,1,0:T(8,128)}, f32[3,112,128]{2,1,0:T(8,128)S(1)}, u32[]{:S(2)}, u32[]{:S(2)}) collective-permute-start(f32[3,112,128]{2,1,0:T(8,128)} %get-tuple-element.28), channel_id=1, source_target_pairs={{0,1},{1,0},{2,3},{3,2},{4,5},{5,4},{6,7},{7,6},{8,9},{9,8},{10,11... | collective-permute-start | bytes 516104 | tf_op jit(solution)/shard_map/ppermute | solution.py:275
  212.6 17.9 %copy-start.6 = (f32[5,112,128]{2,1,0:T(8,128)}, f32[5,112,128]{2,1,0:T(8,128)S(1)}, u32[]{:S(2)}) copy-start(f32[5,112,128]{2,1,0:T(8,128)S(1)} %add.51.refs_5_) | copy-start | bytes 860164
  212.6 13.6 %collective-permute-start.9 = (f32[5,112,128]{2,1,0:T(8,128)S(1)}, f32[5,112,128]{2,1,0:T(8,128)S(1)}, u32[]{:S(2)}, u32[]{:S(2)}) collective-permute-start(f32[5,112,128]{2,1,0:T(8,128)S(1)} %add.51.refs_5_), channel_id=1, source_target_pairs={{0,3},{1,2},{2,1},{3,0},{4,7},{5,6},{6,5},{7,4},{8,11},{9,10},{10,... | collective-permute-start | bytes 860168 | tf_op jit(solution)/shard_map/ppermute | solution.py:269
  214.5 9.8 %collective-permute-start.6 = (f32[3,112,128]{2,1,0:T(8,128)}, f32[3,112,128]{2,1,0:T(8,128)S(1)}, u32[]{:S(2)}, u32[]{:S(2)}) collective-permute-start(f32[3,112,128]{2,1,0:T(8,128)} %get-tuple-element.29), channel_id=1, source_target_pairs={{0,3},{1,2},{2,1},{3,0},{4,7},{5,6},{6,5},{7,4},{8,11},{9,10},{10,... | collective-permute-start | bytes 516104 | tf_op jit(solution)/shard_map/ppermute | solution.py:275
  215.5 15.1 %copy-start.7 = (f32[5,112,128]{2,1,0:T(8,128)}, f32[5,112,128]{2,1,0:T(8,128)S(1)}, u32[]{:S(2)}) copy-start(f32[5,112,128]{2,1,0:T(8,128)S(1)} %add.52.refs_7_) | copy-start | bytes 860164
  215.5 10.9 %collective-permute-start.11 = (f32[5,112,128]{2,1,0:T(8,128)S(1)}, f32[5,112,128]{2,1,0:T(8,128)S(1)}, u32[]{:S(2)}, u32[]{:S(2)}) collective-permute-start(f32[5,112,128]{2,1,0:T(8,128)S(1)} %add.52.refs_7_), channel_id=1, source_target_pairs={{0,1},{1,0},{2,3},{3,2},{4,5},{5,4},{6,7},{7,6},{8,9},{9,8},{10,11... | collective-permute-start | bytes 860168 | tf_op jit(solution)/shard_map/ppermute | solution.py:269
  215.8 14.7 %copy-start.8 = (f32[5,112,128]{2,1,0:T(8,128)}, f32[5,112,128]{2,1,0:T(8,128)S(1)}, u32[]{:S(2)}) copy-start(f32[5,112,128]{2,1,0:T(8,128)S(1)} %add.53.refs_9_) | copy-start | bytes 860164
  215.8 14.7 %collective-permute-start.13 = (f32[5,112,128]{2,1,0:T(8,128)S(1)}, f32[5,112,128]{2,1,0:T(8,128)S(1)}, u32[]{:S(2)}, u32[]{:S(2)}) collective-permute-start(f32[5,112,128]{2,1,0:T(8,128)S(1)} %add.53.refs_9_), channel_id=1, source_target_pairs={{0,3},{1,2},{2,1},{3,0},{4,7},{5,6},{6,5},{7,4},{8,11},{9,10},{10,... | collective-permute-start | bytes 860168 | tf_op jit(solution)/shard_map/ppermute | solution.py:269
  217.8 12.8 %copy-start.9 = (f32[5,112,128]{2,1,0:T(8,128)}, f32[5,112,128]{2,1,0:T(8,128)S(1)}, u32[]{:S(2)}) copy-start(f32[5,112,128]{2,1,0:T(8,128)S(1)} %add.54.refs_11_) | copy-start | bytes 860164
  217.8 12.7 %collective-permute-start.15 = (f32[5,112,128]{2,1,0:T(8,128)S(1)}, f32[5,112,128]{2,1,0:T(8,128)S(1)}, u32[]{:S(2)}, u32[]{:S(2)}) collective-permute-start(f32[5,112,128]{2,1,0:T(8,128)S(1)} %add.54.refs_11_), channel_id=1, source_target_pairs={{0,1},{1,0},{2,3},{3,2},{4,5},{5,4},{6,7},{7,6},{8,9},{9,8},{10,11... | collective-permute-start | bytes 860168 | tf_op jit(solution)/shard_map/ppermute | solution.py:269
  218.7 20.3 %copy-start.10 = (f32[3,112,128]{2,1,0:T(8,128)}, f32[3,112,128]{2,1,0:T(8,128)S(1)}, u32[]{:S(2)}) copy-start(f32[3,112,128]{2,1,0:T(8,128)S(1)} %add.49.refs_5_) | copy-start | bytes 516100
  224.4 14.7 %collective-permute-start.5 = (f32[3,112,128]{2,1,0:T(8,128)S(1)}, f32[3,112,128]{2,1,0:T(8,128)S(1)}, u32[]{:S(2)}, u32[]{:S(2)}) collective-permute-start(f32[3,112,128]{2,1,0:T(8,128)S(1)} %add.49.refs_5_), channel_id=1, source_target_pairs={{0,3},{1,2},{2,1},{3,0},{4,7},{5,6},{6,5},{7,4},{8,11},{9,10},{10,... | collective-permute-start | bytes 516104 | tf_op jit(solution)/shard_map/ppermute | solution.py:269
  226.2 12.9 %copy-start.11 = (f32[3,112,128]{2,1,0:T(8,128)}, f32[3,112,128]{2,1,0:T(8,128)S(1)}, u32[]{:S(2)}) copy-start(f32[3,112,128]{2,1,0:T(8,128)S(1)} %add.50.refs_7_) | copy-start | bytes 516100
  226.2 4.3 %copy-start.12 = (f32[5,112,128]{2,1,0:T(8,128)}, f32[5,112,128]{2,1,0:T(8,128)S(1)}, u32[]{:S(2)}) copy-start(f32[5,112,128]{2,1,0:T(8,128)S(1)} %collective-permute-done.9.refs_6_) | copy-start | bytes 860164
  226.2 12.9 %collective-permute-start.7 = (f32[3,112,128]{2,1,0:T(8,128)S(1)}, f32[3,112,128]{2,1,0:T(8,128)S(1)}, u32[]{:S(2)}, u32[]{:S(2)}) collective-permute-start(f32[3,112,128]{2,1,0:T(8,128)S(1)} %add.50.refs_7_), channel_id=1, source_target_pairs={{0,1},{1,0},{2,3},{3,2},{4,5},{5,4},{6,7},{7,6},{8,9},{9,8},{10,11... | collective-permute-start | bytes 516104 | tf_op jit(solution)/shard_map/ppermute | solution.py:269
  226.3 4.2 %copy-start.13 = (f32[5,112,128]{2,1,0:T(8,128)}, f32[5,112,128]{2,1,0:T(8,128)S(1)}, u32[]{:S(2)}) copy-start(f32[5,112,128]{2,1,0:T(8,128)S(1)} %collective-permute-done.11.refs_8_) | copy-start | bytes 860164
  230.5 0.7 copy-start.14
  231.2 0.7 copy-start.15
  239.1 0.7 copy-start.20
  239.7 0.7 copy-start.21
  240.4 32.5 %copy-start.1 = (s32[64]{0:T(128)S(1)}, s32[64]{0:T(128)}, u32[]{:S(2)}) copy-start(s32[64]{0:T(128)} %param.15) | copy-start | bytes 772
  245.5 6.0 %collective-permute-start.16 = (f32[32,32,128]{2,1,0:T(8,128)S(1)}, f32[32,32,128]{2,1,0:T(8,128)S(1)}, u32[]{:S(2)}, u32[]{:S(2)}) collective-permute-start(f32[32,32,128]{2,1,0:T(8,128)S(1)} %slice.25), channel_id=1, source_target_pairs={{0,4},{4,0},{8,12},{12,8},{16,20},{20,16},{24,28},{28,24},{32,36},... | collective-permute-start | bytes 1572872 | tf_op jit(solution)/shard_map/ppermute | solution.py:281
Sparse Core Ops, SparseCore 0:
  10.3 170.7 all-gather.2
